TPU v7x, 32 devices: a whole 2x2x4 slice. The times are simulated.
32 devices in a mesh: seq: 8 (over z, y), batch: 4 (over x, core).
Axes of the slice: x: 2, y: 2, z: 4, core: 2. Of those that a mesh axis runs over, the one named last changes fastest.
Arguments:
- residual_in: bfloat16 [4, 2048, 1536], P('batch', 'seq'), may hold values from -6 to 6
- seg_ids: int32 [4, 2048], P('batch', 'seq'), may hold values from 0 to 10, as said below
- doc_starts: int32 [4, 12], P('batch'), may hold values from 0 to 2048, as said below
- norm_gain: bfloat16 [1536], P(('seq', 'batch')), may hold values from 0.5 to 1.5
- in_weight: bfloat16 [1536, 6448], P(('seq', 'batch')), may hold values from -0.15625 to 0.15625
- conv_weight: bfloat16 [3328, 4], P(('seq', 'batch')), may hold values from -3 to 3
- conv_bias: bfloat16 [3328], P(('seq', 'batch')), may hold values from -3 to 3
- dt_bias: float32 [48], replicated, may hold values from -7 to -1
- a_log: float32 [48], replicated, may hold values from 0 to 1.5
- skip_weight: float32 [48], replicated, may hold values from 0.5 to 1.5
- gate_gain: bfloat16 [3072], P(('seq', 'batch')), may hold values from 0.5 to 1.5
- out_weight: bfloat16 [3072, 1536], P(('seq', 'batch')), may hold values from -0.109375 to 0.109375
- cotangent: bfloat16 [4, 2048, 1536], P('batch', 'seq'), may hold values from -6 to 6
Outputs:
- mixed_out: bfloat16 [4, 2048, 1536], P('batch', 'seq')
- input_grad: float32 [4, 2048, 1536], P('batch', 'seq')
- norm_gain_grad: float32 [1536], P(('seq', 'batch'))
- in_weight_grad: float32 [1536, 6448], P(('seq', 'batch'))
- conv_weight_grad: float32 [3328, 4], P(('seq', 'batch'))
- conv_bias_grad: float32 [3328], P(('seq', 'batch'))
- dt_bias_grad: float32 [48], replicated
- a_log_grad: float32 [48], replicated
- skip_weight_grad: float32 [48], replicated
- gate_gain_grad: float32 [3072], P(('seq', 'batch'))
- out_weight_grad: float32 [3072, 1536], P(('seq', 'batch'))
Inputs may be any that keep to these rules, and one draw needn't show every extreme that they name: `doc_starts`: each row starts with 0; entries below 2048 rise by 200 to 2000 from one to the next; all later entries equal 2048. seg_ids at a position is the number of entries of its sequence's doc_starts at or below that position, minus one.
All inputs are finite; a program needn't handle non-finite values.
Results may differ from a plain program's by a relative error of at most 0.011.
Values may be sent and summed in bfloat16 or wider, within the bound.
No kernel may reach another device: no remote copies, remote signals or barrier semaphores. Data moves between devices by JAX's collectives and lax.ppermute only.
A program may use at most 256 MiB of HBM per device.

v0:
```python
import jax
import jax.numpy as jnp
from jax import lax
from jax.sharding import PartitionSpec as P

E = 3072
H = 48
P_SIZE = 64
N = 128
C = 3328
F_IN = 6448


highest = lax.Precision.HIGHEST
epsilon = 1e-05


def from_behind(block, axis, distance):
    devices = range(lax.axis_size(axis))
    route = [(i - distance, i) for i in devices if i - distance in devices]
    return lax.ppermute(block, axis, route)


def entering_2(part, axis, combine, identity):
    place = lax.axis_index(axis)
    gathered = jax.tree.map(lambda a: lax.all_gather(a, axis), part)
    state = jax.tree.map(lambda a, e: jnp.zeros_like(a) + jnp.asarray(e, a.dtype), part, identity)

    def one(lap, state):
        return combine(
            state, jax.tree.map(lambda a: lax.dynamic_index_in_dim(a, lap, 0, False), gathered)
        )

    return lax.fori_loop(0, place, one, state)


def carried_in(array, axis, combine, identity):
    devices, place = (lax.axis_size(axis), lax.axis_index(axis))
    everything = jax.tree.map(
        lambda part, kind: lax.all_gather(part.astype(kind), axis),
        array,
        jax.tree.map(lambda a: jnp.bfloat16 if a.dtype == jnp.float32 else a.dtype, array),
    )
    start = jax.tree.map(
        lambda part, zero: jnp.broadcast_to(jnp.asarray(zero, part.dtype), part.shape),
        array,
        identity,
    )

    def lap(k, before):
        at = devices - 1 - k
        reached = at > place
        new = combine(
            before, jax.tree.map(lambda part, own: part[at].astype(own.dtype), everything, array)
        )
        return jax.tree.map(lambda a, b: jnp.where(reached, a, b), new, before)

    return lax.fori_loop(0, devices, lap, start)


def rms_scale(values, gain_vec):
    return (
        values * lax.rsqrt(jnp.mean(values * values, axis=-1, keepdims=True) + epsilon) * gain_vec
    )


def doc_index(starts, places):
    return jnp.sum((starts[..., None, :] <= places[..., None]).astype(jnp.int32), axis=-1) - 1


def conv_block(inputs, edge_rows, kernel, offset, seg_rows, doc_edge, doc_head):
    lead_taps = kernel.shape[1] - 1
    block_len = inputs.shape[1]
    lanes = inputs.shape[0]
    extended = jnp.concatenate([edge_rows, inputs], axis=1)
    running = offset + kernel[:, lead_taps] * inputs
    for shift_by in range(1, lead_taps + 1):
        source = extended[:, lead_taps - shift_by : lead_taps - shift_by + block_len]
        near_ids = jnp.concatenate(
            [jnp.full((lanes, shift_by), -1, jnp.int32), seg_rows[:, : block_len - shift_by]],
            axis=1,
        )
        near_same = seg_rows == near_ids
        far_same = doc_edge[:, lead_taps - shift_by : lead_taps] == doc_head[:, :shift_by]
        far_full = jnp.concatenate(
            [far_same, jnp.zeros((lanes, block_len - shift_by), dtype=bool)], axis=1
        )
        weight_mask = jnp.where(near_same | far_full, 1.0, 0.0).astype(inputs.dtype)
        running = running + kernel[:, lead_taps - shift_by] * source * weight_mask[..., None]
    return running


def prep_block(
    projected, edge_rows, kernel, offset, bias_dt, alog_vec, seg_rows, doc_edge, doc_head
):
    lanes = projected.shape[0]
    block_len = projected.shape[1]
    gate_part = projected[..., :E]
    conv_in = projected[..., E : E + C]
    dt_raw = projected[..., E + C :]
    activated = jax.nn.silu(
        conv_block(conv_in, edge_rows, kernel, offset, seg_rows, doc_edge, doc_head)
    )
    heads_x = activated[..., :E].reshape(lanes, block_len, H, P_SIZE)
    b_rows = activated[..., E : E + N]
    c_rows = activated[..., E + N :]
    step_dt = jax.nn.softplus(dt_raw + bias_dt)
    rates = -jnp.exp(alog_vec) * step_dt
    return (gate_part, heads_x, b_rows, c_rows, step_dt, rates)


def block_state(heads_x, b_rows, step_dt, rates, seg_rows, begins_doc):
    cumulative = jnp.cumsum(rates, axis=1)
    last_cum = cumulative[:, -1:, :]
    in_tail = seg_rows == seg_rows[:, -1:]
    weights = jnp.where(in_tail[..., None], jnp.exp(last_cum - cumulative), 0.0) * step_dt
    scaled = heads_x * weights[..., None]
    end_state = jnp.einsum("bshp,bsn->bhpn", scaled, b_rows, precision=highest)
    whole_doc = (seg_rows[:, -1] == seg_rows[:, 0]) & jnp.logical_not(begins_doc)
    block_decay = jnp.where(whole_doc[:, None], jnp.exp(last_cum[:, 0, :]), 0.0)
    return (end_state, block_decay)


def block_output(
    heads_x,
    b_rows,
    c_rows,
    step_dt,
    rates,
    gate_part,
    seg_rows,
    begins_doc,
    state_in,
    skip_vec,
    gain_vec,
):
    lanes, block_len = seg_rows.shape
    cumulative = jnp.cumsum(rates, axis=1)
    cum_heads = jnp.swapaxes(cumulative, 1, 2)
    differences = cum_heads[:, :, :, None] - cum_heads[:, :, None, :]
    places = jnp.arange(block_len, dtype=jnp.int32)
    causal = places[:, None] >= places[None, :]
    same_doc = (seg_rows[:, :, None] == seg_rows[:, None, :]) & causal[None]
    decays = jnp.exp(jnp.where(same_doc[:, None], differences, -jnp.inf))
    scores = jnp.einsum("btn,bsn->bts", c_rows, b_rows, precision=highest)
    mixing = decays * scores[:, None]
    scaled = heads_x * step_dt[..., None]
    within = jnp.einsum("bhts,bshp->bthp", mixing, scaled, precision=highest)
    continues = (seg_rows == seg_rows[:, :1]) & jnp.logical_not(begins_doc)[:, None]
    entering = jnp.where(continues[..., None], jnp.exp(cumulative), 0.0)
    carried = (
        jnp.einsum("btn,bhpn->bthp", c_rows, state_in, precision=highest) * entering[..., None]
    )
    summed = within + carried + skip_vec[:, None] * heads_x
    gated_rows = summed.reshape(lanes, block_len, E) * jax.nn.silu(gate_part)
    return rms_scale(gated_rows, gain_vec)


def chain_combine(earlier_part, later_part):
    return (
        earlier_part[0] * later_part[0],
        later_part[0][:, :, None, None] * earlier_part[1] + later_part[1],
    )


def per_device(
    residual_in,
    seg_ids,
    doc_starts,
    norm_gain,
    in_weight,
    conv_weight,
    conv_bias,
    dt_bias,
    a_log,
    skip_weight,
    gate_gain,
    out_weight,
    cotangent,
):
    full_gain, full_in, full_kernel, full_offset, full_gate, full_out = (
        lax.all_gather(norm_gain, ("seq", "batch"), axis=0, tiled=True),
        lax.all_gather(in_weight, ("seq", "batch"), axis=0, tiled=True),
        lax.all_gather(conv_weight, ("seq", "batch"), axis=0, tiled=True),
        lax.all_gather(conv_bias, ("seq", "batch"), axis=0, tiled=True),
        lax.all_gather(gate_gain, ("seq", "batch"), axis=0, tiled=True),
        lax.all_gather(out_weight, ("seq", "batch"), axis=0, tiled=True),
    )
    lanes, block_len, _ = residual_in.shape
    lead_taps = full_kernel.shape[1] - 1
    block_start = lax.axis_index("seq") * block_len
    begins_doc = jnp.any(doc_starts == block_start, axis=1)
    tap_places = jnp.arange(lead_taps, dtype=jnp.int32)
    doc_edge = doc_index(
        doc_starts, jnp.broadcast_to(block_start - lead_taps + tap_places, (lanes, lead_taps))
    )
    doc_head = doc_index(doc_starts, jnp.broadcast_to(block_start + tap_places, (lanes, lead_taps)))
    resid_float = residual_in.astype(jnp.float32)
    normed, norm_back = jax.vjp(rms_scale, resid_float, full_gain.astype(jnp.float32))
    normed_low = normed.astype(jnp.bfloat16)
    projected = jnp.einsum(
        "btd,df->btf", normed_low, full_in, preferred_element_type=jnp.float32
    ).astype(jnp.bfloat16)
    edge_rows = from_behind(projected[:, block_len - lead_taps :, E : E + C], "seq", 1)

    def prep_local(proj_f, edge_f, kernel, offset, bias_dt, alog_vec):
        return prep_block(
            proj_f, edge_f, kernel, offset, bias_dt, alog_vec, seg_ids, doc_edge, doc_head
        )

    prepared, prep_back = jax.vjp(
        prep_local,
        projected.astype(jnp.float32),
        edge_rows.astype(jnp.float32),
        full_kernel.astype(jnp.float32),
        full_offset.astype(jnp.float32),
        dt_bias,
        a_log,
    )
    gate_part, heads_x, b_rows, c_rows, step_dt, rates = prepared

    def state_local(heads_in, b_in, dt_in, rates_in):
        return block_state(heads_in, b_in, dt_in, rates_in, seg_ids, begins_doc)

    (end_state, block_decay), state_back = jax.vjp(state_local, heads_x, b_rows, step_dt, rates)
    unit_decay = jnp.ones_like(block_decay)
    empty_state = jnp.zeros_like(end_state)
    _, state_in = entering_2(
        (block_decay, end_state), "seq", chain_combine, (unit_decay, empty_state)
    )

    def output_local(
        heads_in, b_in, c_in, dt_in, rates_in, gate_in, entering_state, skip_vec, gain_vec
    ):
        return block_output(
            heads_in,
            b_in,
            c_in,
            dt_in,
            rates_in,
            gate_in,
            seg_ids,
            begins_doc,
            entering_state,
            skip_vec,
            gain_vec,
        )

    mixer_out, out_back = jax.vjp(
        output_local,
        heads_x,
        b_rows,
        c_rows,
        step_dt,
        rates,
        gate_part,
        state_in,
        skip_weight,
        full_gate.astype(jnp.float32),
    )
    mixer_low = mixer_out.astype(jnp.bfloat16)
    mixed_out = (
        resid_float
        + jnp.einsum("bte,ed->btd", mixer_low, full_out, preferred_element_type=jnp.float32)
    ).astype(jnp.bfloat16)
    back_in, back_out = (
        lax.all_gather(in_weight, ("seq", "batch"), axis=0, tiled=True),
        lax.all_gather(out_weight, ("seq", "batch"), axis=0, tiled=True),
    )
    mixer_grad = jnp.einsum("btd,ed->bte", cotangent, back_out, preferred_element_type=jnp.float32)
    out_w_grad = jnp.einsum("bte,btd->ed", mixer_low, cotangent, preferred_element_type=jnp.float32)
    heads_g1, b_g1, c_grad, dt_g1, rates_g1, gate_grad_rows, state_grad, skip_grad, gain_grad = (
        out_back(mixer_grad)
    )
    _, later_grads = carried_in(
        (block_decay, state_grad), "seq", chain_combine, (unit_decay, empty_state)
    )
    decay_grad = jnp.sum(later_grads * state_in, axis=(2, 3))
    heads_g2, b_g2, dt_g2, rates_g2 = state_back((later_grads, decay_grad))
    proj_grad, edge_grad, kernel_grad, offset_grad, bias_grad, alog_grad = prep_back(
        (
            gate_grad_rows,
            heads_g1 + heads_g2,
            b_g1 + b_g2,
            c_grad,
            dt_g1 + dt_g2,
            rates_g1 + rates_g2,
        )
    )
    returned = from_behind(edge_grad.astype(jnp.bfloat16), "seq", -1).astype(edge_grad.dtype)
    proj_grad = proj_grad + jnp.pad(
        returned, ((0, 0), (block_len - lead_taps, 0), (E, F_IN - E - C))
    )
    proj_low = proj_grad.astype(jnp.bfloat16)
    normed_grad = jnp.einsum("btf,df->btd", proj_low, back_in, preferred_element_type=jnp.float32)
    in_w_grad = jnp.einsum("btd,btf->df", normed_low, proj_low, preferred_element_type=jnp.float32)
    resid_grad, norm_grad = norm_back(normed_grad)
    input_grad = cotangent.astype(jnp.float32) + resid_grad
    norm_share, in_share, kernel_share, offset_share, gain_share, out_w_share = (
        lax.psum_scatter(norm_grad, ("seq", "batch"), scatter_dimension=0, tiled=True),
        lax.psum_scatter(in_w_grad, ("seq", "batch"), scatter_dimension=0, tiled=True),
        lax.psum_scatter(kernel_grad, ("seq", "batch"), scatter_dimension=0, tiled=True),
        lax.psum_scatter(offset_grad, ("seq", "batch"), scatter_dimension=0, tiled=True),
        lax.psum_scatter(gain_grad, ("seq", "batch"), scatter_dimension=0, tiled=True),
        lax.psum_scatter(out_w_grad, ("seq", "batch"), scatter_dimension=0, tiled=True),
    )
    bias_total, alog_total, skip_total = lax.psum(
        (bias_grad, alog_grad, skip_grad), ("seq", "batch")
    )
    return (
        mixed_out,
        input_grad,
        norm_share,
        in_share,
        kernel_share,
        offset_share,
        bias_total,
        alog_total,
        skip_total,
        gain_share,
        out_w_share,
    )


def solution(mesh):
    return jax.shard_map(
        per_device,
        mesh=mesh,
        in_specs=(
            P("batch", "seq", None),
            P("batch", "seq"),
            P("batch", None),
            P(("seq", "batch")),
            P(("seq", "batch"), None),
            P(("seq", "batch"), None),
            P(("seq", "batch")),
            P(),
            P(),
            P(),
            P(("seq", "batch")),
            P(("seq", "batch"), None),
            P("batch", "seq", None),
        ),
        out_specs=(
            P("batch", "seq", None),
            P("batch", "seq", None),
            P(("seq", "batch")),
            P(("seq", "batch"), None),
            P(("seq", "batch"), None),
            P(("seq", "batch")),
            P(),
            P(),
            P(),
            P(("seq", "batch")),
            P(("seq", "batch"), None),
        ),
        check_vma=False,
    )
```

profile of v0, /device:TPU:0, one launch (start us, length us, event | category | flops | bytes accessed | tf_op | source)
XLA Modules:
  0.0 1375.1 jit_solution(14505195594288302598)
XLA Ops:
  14.0 43.8 %all-reduce.28 = (bf16[1536]{0:T(1024)(128)(2,1)S(1)}, bf16[3328]{0:T(1024)(128)(2,1)S(1)}, bf16[3072]{0:T(1024)(128)(2,1)}) all-reduce(bf16[1536]{0:T(1024)(128)(2,1)S(1)} %dynamic-update-slice.1, bf16[3328]{0:T(1024)(128)(2,1)S(1)} %dynamic-update-slice, ...), channel_id=1, replica_groups=mesh['seq'=8,'batch'=4] {'seq','batch'}, use_global_device_ids=true, to_apply=%add.21 | all-reduce | flops 7936 | bytes 31744
  58.5 42.0 %all-gather.2 = bf16[32,104,4]{1,2,0:T(4,128)(2,1)S(1)} all-gather(bf16[1,104,4]{1,2,0:T(4,128)(2,1)} %bitcast.372), channel_id=1, replica_groups=mesh['seq'=8,'batch'=4] {'seq','batch'}, dimensions={0}, use_global_device_ids=true | all-gather | bytes 27456 | tf_op jit(solution)/shard_map/all_gather | solution.py:184
  103.8 2.5 and_reduce_fusion
  110.6 33.9 %all-gather.8.cloned.1.call-done = bf16[1536,6448]{1,0:T(8,128)(2,1)} async-done(((bf16[48,6448]{1,0:T(8,128)(2,1)}), bf16[1536,6448]{1,0:T(8,128)(2,1)}) %all-gather.8.cloned.1.call-update) | async-done | bytes 19808272 | tf_op jit(solution)/shard_map/all_gather | solution.py:183
  144.6 10.0 fusion.134
  154.7 2.8 copy-done.9
  160.4 4.0 collective-permute-start
  164.4 1.7 select_bitcast_fusion
  166.6 1.7 multiply_bitcast_fusion
  168.3 1.9 slice.123
  171.5 2.4 copy.203
  174.7 8.3 fusion.23
  183.0 3.6 slice_multiply_fusion
  186.6 3.6 copy.204
  190.1 5.7 fusion.93
  199.5 1.6 copy.197
  202.4 1.6 copy.230
  204.1 1.6 copy.206
  205.7 2.7 mul.590
  208.4 3.6 copy.211
  212.0 17.1 %all_gather.44 = f32[8,1,48]{2,1,0:T(1,128)S(1)} all-gather(f32[1,1,48]{2,1,0:T(1,128)} %get-tuple-element.337), channel_id=1, replica_groups=mesh['seq'=8,'batch'=4] {'seq'}, dimensions={0}, use_global_device_ids=true | all-gather | bytes 1728 | tf_op jit(solution)/shard_map/all_gather | solution.py:26
  230.5 3.5 copy.196
  235.2 134.4 %all-gather.12.cloned.1.call-done = f32[384,64,128]{2,1,0:T(8,128)} async-done(((f32[48,64,128]{2,1,0:T(8,128)}), f32[384,64,128]{2,1,0:T(8,128)}) %all-gather.12.cloned.1.call-update) | async-done | bytes 12582928 | tf_op jit(solution)/shard_map/all_gather | solution.py:26
  369.8 3.7 fusion.53
  373.6 15.2 %fusion.27 = f32[1,256,48,64]{1,3,2,0:T(8,128)} fusion(f32[1,256,48,64]{1,3,2,0:T(8,128)S(1)} %bitcast.343, f32[256,48,64]{0,2,1:T(8,128)S(1)} %fusion.53, f32[48]{0:T(128)S(1)} %copy-done.78, f32[256,48]{0,1:T(8,128)S(1)} %copy-done.32, f32[256,256]{1,0:T(8,128)S(1)} %copy-done.30, f32[48,256]{1,0:T(8,128)S(1)} %copy-done.50, ...), kind=kOutput, calls=%fused_computation.52 | convolution fusion | flops 2429288448 | bytes 13058240 | tf_op jit(solution)/shard_map/jvp(bhts,bshp->bthp)/dot_general | solution.py:148
  388.8 3.6 copy.208
  392.3 5.5 multiply_reduce_fusion.7
  397.8 54.4 %all-gather.10.cloned.1.call-done = bf16[3072,1536]{1,0:T(8,128)(2,1)} async-done(((bf16[96,1536]{1,0:T(8,128)(2,1)}), bf16[3072,1536]{1,0:T(8,128)(2,1)}) %all-gather.10.cloned.1.call-update) | async-done | bytes 9437200 | tf_op jit(solution)/shard_map/all_gather | solution.py:187
  452.2 12.5 fusion.28
  464.7 5.5 multiply_reduce_fusion.5
  470.3 1.7 copy-done.6
  472.0 2.1 mul.615
  474.0 3.5 copy.212
  477.6 5.4 convolution_convert_fusion.1
  483.1 19.4 %all_gather.49 = bf16[8,1,48]{2,1,0:T(2,128)(2,1)S(1)} all-gather(bf16[1,1,48]{2,1,0:T(2,128)(2,1)S(1)} %copy-done.77), channel_id=1, replica_groups=mesh['seq'=8,'batch'=4] {'seq'}, dimensions={0}, use_global_device_ids=true | all-gather | bytes 864 | tf_op jit(solution)/shard_map/all_gather | solution.py:40
  502.5 3.7 copy.209
  506.9 3.6 multiply_reduce_fusion.6
  511.3 20.1 %fusion.8 = (f32[48,256]{1,0:T(8,128)}, f32[48,256]{1,0:T(8,128)}, f32[256,256]{1,0:T(8,128)S(1)}) fusion(f32[256,256]{1,0:T(8,128)} %fusion.98, f32[48,256]{1,0:T(8,128)} %bitcast_add_fusion.6, pred[256,256]{1,0:T(8,128)(4,1)} %fusion.78, f32[48,64,256]{2,1,0:T(8,128)} %bitcast.334, f32[256,48,64]{0,2,1:T(8,128)} %bitcast.341, f32[256,48]{0,1:T(8,128)} %copy.197), kind=kOutput, calls=%fused_computation.14 | convolution fusion | flops 2444926976 | bytes 7077888 | tf_op jit(solution)/shard_map/transpose(jvp(bhts,bshp->bthp))/dot_general | solution.py:148
  531.5 1.5 copy.217
  533.0 1.6 copy.218
  534.6 2.3 convolution_bitcast_fusion.1
  536.9 6.9 fusion.62
  543.8 1.9 fusion.71
  545.8 11.7 fusion.2
  557.5 22.9 %all-gather.14.cloned.1.call-done = bf16[384,64,128]{2,1,0:T(8,128)(2,1)} async-done(((bf16[48,64,128]{2,1,0:T(8,128)(2,1)}), bf16[384,64,128]{2,1,0:T(8,128)(2,1)}) %all-gather.14.cloned.1.call-update) | async-done | bytes 6291472 | tf_op jit(solution)/shard_map/all_gather | solution.py:40
  580.4 12.6 while.29
  580.4 1.5 fusion.148
  595.0 7.4 fusion.31
  603.7 2.9 reduce-window.24
  608.2 2.5 reduce-window.26
  612.1 7.6 fusion.68
  619.7 3.7 copy.226
  623.4 7.3 multiply_reduce_fusion.4
  632.7 2.2 slice_add_fusion
  637.2 1.6 fusion.126
  639.3 1.6 collective-permute-done.1
  641.5 13.6 fusion.42
  655.2 9.1 fusion.73
  665.0 22.2 %fusion.79 = f32[1536,6448]{1,0:T(8,128)} fusion(bf16[1,256,1536]{2,1,0:T(8,128)(2,1)} %param.17, f32[1536]{0:T(1024)S(1)} %copy-done.42, f32[256]{0:T(256)S(1)} %copy-done.58, f32[1,256,3072]{2,1,0:T(8,128)} %get-tuple-element.344, f32[1,256,3328]{2,1,0:T(8,128)} %slice_add_fusion, f32[1,256,48]{2,1,0:T(8,128)S(1)} %get-tuple-element.332, ...), kind=kOutput, calls=%fused_computation.120 | convolution fusion | flops 5080739840 | bytes 47032832 | tf_op jit(solution)/shard_map/btd,btf->df/dot_general | solution.py:296
  687.3 7.5 fusion.38
  694.9 1.6 fusion.43
  696.5 83.7 %all-reduce.31.cloned.1.call-done = (f32[1536]{0:T(1024)}, f32[3328,4]{0,1:T(4,128)}, f32[3328]{0:T(1024)}, f32[48]{0:T(128)}, f32[48]{0:T(128)}, /*index=5*/f32[48]{0:T(128)}, f32[3072]{0:T(1024)}) async-done(((f32[1536]{0:T(1024)}, f32[3328,4]{0,1:T(4,128)}, f32[3328]{0:T(1024)}, f32[48]{0:T(128)}, f32[48]{0:T(128)}, /*index=5*/f32[48]{0:T(128)}, f32[3072]{0:T(1024)}), (f32[1536]{0:T(1024)}, ...) | async-done | bytes 85584
  785.3 209.5 %reduce-scatter.6.cloned.1.call-done = f32[96,1536]{1,0:T(8,128)} async-done(((f32[3072,1536]{1,0:T(8,128)}), f32[96,1536]{1,0:T(8,128)}) %reduce-scatter.6.cloned.1.call-update) | async-done | bytes 589840 | tf_op jit(solution)/shard_map/reduce_scatter | solution.py:305
  994.8 369.9 %reduce-scatter.4.cloned.1.call-done = f32[48,6448]{1,0:T(8,128)} async-done(((f32[1536,6448]{1,0:T(8,128)}), f32[48,6448]{1,0:T(8,128)}) %reduce-scatter.4.cloned.1.call-update) | async-done | bytes 1238032 | tf_op jit(solution)/shard_map/reduce_scatter | solution.py:301
  (274 shorter events, 58.8 us)
Async XLA Ops:
  7.2 137.4 %all-gather.8.cloned.1.call-start = ((), (), s32[]{:S(2)}) async-start(), calls=%async_computation.2 | async-start | bytes 20680704 | tf_op jit(solution)/shard_map/all_gather | solution.py:183
  7.9 361.6 %all-gather.12.cloned.1.call-start = ((), (), s32[]{:S(2)}) async-start(), calls=%async_computation.6 | async-start | bytes 14155776 | tf_op jit(solution)/shard_map/all_gather | solution.py:26
  57.8 96.8 %copy-start.41 = (f32[1536]{0:T(1024)}, f32[1536]{0:T(1024)S(1)}, u32[]{:S(2)}) copy-start(f32[1536]{0:T(1024)S(1)} %convert_element_type.122) | copy-start | bytes 18436
  107.0 67.6 %copy-start.36 = (f32[3328]{0:T(1024)}, f32[3328]{0:T(1024)S(1)}, u32[]{:S(2)}) copy-start(f32[3328]{0:T(1024)S(1)} %get-tuple-element.291) | copy-start | bytes 39940
  108.4 46.3 %copy-start.62 = (f32[256]{0:T(256)}, f32[256]{0:T(256)S(1)}, u32[]{:S(2)}) copy-start(f32[256]{0:T(256)S(1)} %fusion.44) | copy-start | bytes 3076
  109.0 45.6 %copy-start.75 = (f32[48]{0:T(128)}, f32[48]{0:T(128)S(1)}, u32[]{:S(2)}) copy-start(f32[48]{0:T(128)S(1)} %exponential_negate_fusion) | copy-start | bytes 580
  109.1 45.5 %copy-start.57 = (f32[256]{0:T(256)}, f32[256]{0:T(256)S(1)}, u32[]{:S(2)}) copy-start(f32[256]{0:T(256)S(1)} %fusion.112) | copy-start | bytes 3076
  110.6 46.8 %copy-start.64 = (f32[48]{0:T(128)S(1)}, f32[48]{0:T(128)}, u32[]{:S(2)}) copy-start(f32[48]{0:T(128)} %param.24) | copy-start | bytes 580
  158.9 11.4 copy-start.20
  160.4 13.5 collective-permute-start
  164.4 5.8 copy-start.61
  174.6 8.3 copy-start.27
  174.6 8.3 copy-start.13
  183.0 51.1 %copy-start = (f32[1,256,3328]{2,1,0:T(8,128)}, f32[1,256,3328]{2,1,0:T(8,128)S(1)}, u32[]{:S(2)}) copy-start(f32[1,256,3328]{2,1,0:T(8,128)S(1)} %get-tuple-element.342) | copy-start | bytes 10223620
  190.1 7.2 copy-start.47
  195.8 256.4 %all-gather.10.cloned.1.call-start = ((), (), s32[]{:S(2)}) async-start(), calls=%async_computation.3 | async-start | bytes 9732096 | tf_op jit(solution)/shard_map/all_gather | solution.py:187
  196.6 383.9 %all-gather.14.cloned.1.call-start = ((), (), s32[]{:S(2)}) async-start(), calls=%async_computation.7 | async-start | bytes 7077888 | tf_op jit(solution)/shard_map/all_gather | solution.py:40
  373.5 15.3 %copy-start.10 = (f32[256,48,64]{0,2,1:T(8,128)}, f32[256,48,64]{0,2,1:T(8,128)S(1)}, u32[]{:S(2)}) copy-start(f32[256,48,64]{0,2,1:T(8,128)S(1)} %fusion.53) | copy-start | bytes 9437188
  392.3 59.9 %copy-start.15 = (bf16[1,256,1536]{2,1,0:T(8,128)(2,1)S(1)}, bf16[1,256,1536]{2,1,0:T(8,128)(2,1)}, u32[]{:S(2)}) copy-start(bf16[1,256,1536]{2,1,0:T(8,128)(2,1)} %param.29) | copy-start | bytes 2359300
  397.8 66.9 %copy-start.59 = (f32[256]{0:T(256)}, f32[256]{0:T(256)S(1)}, u32[]{:S(2)}) copy-start(f32[256]{0:T(256)S(1)} %fusion.113) | copy-start | bytes 3076
  452.2 12.5 copy-start.1
  452.2 12.5 copy-start.3
  452.2 12.5 copy-start.5
  464.7 7.2 copy-start.12
  477.6 5.5 copy-start.77
  483.0 297.1 %all-reduce.31.cloned.1.call-start = ((), (), s32[]{:S(2)}) async-start(), calls=%async_computation.8 | async-start | bytes 183296
  534.6 11.2 copy-start.7
  534.6 11.2 copy-start.31
  534.6 11.2 copy-start.49
  534.6 11.2 copy-start.51
  580.4 13.1 copy-start.29
  580.4 13.1 copy-start.34
  594.9 7.5 copy-start.24
  594.9 7.5 copy-start.25
  594.9 7.6 copy-start.26
  595.0 7.6 copy-start.65
  595.0 7.6 copy-start.67
  595.0 7.6 copy-start.70
  595.0 7.6 copy-start.72
  595.0 17.1 %copy-start.21 = (f32[1,256,128]{2,1,0:T(8,128)S(1)}, f32[1,256,128]{2,1,0:T(8,128)}, u32[]{:S(2)}) copy-start(f32[1,256,128]{2,1,0:T(8,128)} %convolution_bitcast_fusion.1) | copy-start | bytes 393220
  602.6 17.1 %copy-start.18 = (f32[256,48]{1,0:T(8,128)}, f32[256,48]{1,0:T(8,128)S(1)}, u32[]{:S(2)}) copy-start(f32[256,48]{1,0:T(8,128)S(1)} %copy.214) | copy-start | bytes 147460
  623.4 7.3 copy-start.38
  623.4 7.3 copy-start.39
  623.4 7.3 copy-start.40
  623.4 7.3 copy-start.55
  623.4 7.3 copy-start.56
  632.6 4.6 copy-start.19
  632.6 4.6 copy-start.22
  632.6 4.6 copy-start.23
  632.6 4.6 copy-start.66
  632.6 4.6 copy-start.68
  632.6 4.5 copy-start.71
  632.6 4.5 copy-start.76
  632.6 6.2 copy-start.80
  632.7 8.9 copy-start.58
  635.2 5.7 collective-permute-start.1
  641.5 13.7 copy-start.4
  641.5 13.7 copy-start.60
  655.1 339.6 %reduce-scatter.6.cloned.1.call-start = ((), (), s32[]{:S(2)}) async-start(), calls=%async_computation.5 | async-start | bytes 19464192 | tf_op jit(solution)/shard_map/reduce_scatter | solution.py:305
  664.3 700.3 %reduce-scatter.4.cloned.1.call-start = ((), (), s32[]{:S(2)}) async-start(), calls=%async_computation.4 | async-start | bytes 41361408 | tf_op jit(solution)/shard_map/reduce_scatter | solution.py:301
  687.3 7.6 copy-start.63
  687.3 7.6 copy-start.14
  687.3 7.6 copy-start.16
  687.3 7.6 copy-start.17
  (26 other events, 68.6 us)
Sparse Core Ops, SparseCore 0:
  10.9 133.6 all-gather.7
  195.9 173.5 all-gather.11
  372.4 79.7 all-gather.9
  483.1 97.2 all-gather.13
  655.3 124.8 all-reduce.30
  787.0 207.7 reduce-scatter.5
  1001.8 362.8 reduce-scatter.3
where the time goes:
time: 1390 us; the launch traced here: 1380 us
  waiting for transfers between devices  911 us (66%)
  matrix products  164 us (12%)
  blocking collectives  122 us (9%)
  other arithmetic  82.3 us (6%)
  local copies, waits for them, and re-layouts  71.3 us (5%)
  between operations  17.9 us (1%)
    reduce_scatter x1, waiting for transfers between devices, per_device(): lax.psum_scatter(in_w_grad, ('seq', 'batch'), scatter_dimension=0, tiled=...  370 us
    reduce_scatter x1, waiting for transfers between devices, per_device(): lax.psum_scatter(out_w_grad, ('seq', 'batch'), scatter_dimension=0, tiled...  209 us
    all_gather x1, waiting for transfers between devices, entering_2(): gathered = jax.tree.map(lambda a: lax.all_gather(a, axis), part)  134 us
    unnamed x8, waiting for transfers between devices  84.8 us
    all_gather x1, waiting for transfers between devices, per_device(): lax.all_gather(out_weight, ('seq', 'batch'), axis=0, tiled=True)  54.4 us
    dot_general x3, matrix products, block_output(): within = jnp.einsum('bhts,bshp->bthp', mixing, scaled, precision=highest)  47 us
    unnamed x1, blocking collectives  43.8 us
    all_gather x1, blocking collectives, per_device(): lax.all_gather(conv_weight, ('seq', 'batch'), axis=0, tiled=True)  42 us
  transfers between devices with their start and end apart: 9, of which 8 were waited for; matrix products, arithmetic and copies ran while one was open for 13% of the time, Pallas kernels for 0%

commit v1 on v0

v1 whole, which is shorter than its diff:
```python
import functools

import jax
import jax.numpy as jnp
from jax import lax
from jax.experimental import pallas as pl
from jax.experimental.pallas import tpu as pltpu
from jax.sharding import Mesh, PartitionSpec as P


f32 = jnp.float32
bf16 = jnp.bfloat16
highest = lax.Precision.HIGHEST
epsilon = 1e-05
HALO = 16
LANES = 128
MASKED = -1e30
INTERPRET = False
PLANE = ("lo", "bx", "core")
SWAP = ((0, 1), (1, 0))
CROSS = ((0, 3), (3, 0), (1, 2), (2, 1))


def dot(a, b, ca=1, cb=0, precision=None):
    return lax.dot_general(
        a, b, (((ca,), (cb,)), ((), ())), precision=precision, preferred_element_type=f32
    )


def iota(shape, axis):
    return lax.broadcasted_iota(jnp.int32, shape, axis)


def sigmoid(z):
    return 0.5 + 0.5 * jnp.tanh(0.5 * z)


def softplus(z):
    return jnp.maximum(z, 0.0) + jnp.log1p(jnp.exp(-jnp.abs(z)))


def segment(starts_ref, n, places):
    found = jnp.full(places.shape, -1, jnp.int32)
    for j in range(starts_ref.shape[1]):
        found = found + (places >= starts_ref[n, j]).astype(jnp.int32)
    return found


def low_half():
    return iota((1, LANES), 1) < LANES // 2


def pair_lanes(cols, j):
    return jnp.where(low_half(), cols[:, 2 * j : 2 * j + 1], cols[:, 2 * j + 1 : 2 * j + 2])


def expand(cols, pairs):
    return jnp.concatenate([pair_lanes(cols, j) for j in range(pairs)], axis=1)


def head_sum(wide):
    rows = wide.shape[1]
    half = LANES // 2
    pick = (iota((rows, LANES), 0) // half == iota((rows, LANES), 1)).astype(f32)
    return dot(wide, pick, precision=highest)


def lower_triangle(q):
    return iota((q, q), 0) >= iota((q, q), 1)


def conv_group(raw_ref, cw_ref, seg, c, q, g):
    lanes = slice(g * LANES, (g + 1) * LANES)
    window = raw_ref[0, c * q : c * q + q + HALO, lanes].astype(f32)
    taps = cw_ref[:, lanes]
    out = taps[4:5] + taps[3:4] * window[HALO:]
    for k in range(1, 4):
        near = seg[HALO:] == seg[HALO - k : HALO - k + q]
        out = out + taps[3 - k : 4 - k] * jnp.where(near, window[HALO - k : HALO - k + q], 0.0)
    return out


def chunk_segments(starts_ref, base_ref, n, c, q):
    first = base_ref[0] + c * q
    cols = segment(starts_ref, n, first - HALO + iota((q + HALO, LANES), 0))
    rows = segment(starts_ref, n, first + iota((8, q), 1))
    return cols, rows


def scan_forward(
    starts_ref,
    base_ref,
    raw_ref,
    cw_ref,
    hp_ref,
    skip_ref,
    act_ref,
    y_ref,
    ent_ref,
    step_ref,
    cum_ref,
    cumr_ref,
    state_ref,
    decay_ref,
    *,
    heads,
    q,
):
    n = pl.program_id(0)
    length = y_ref.shape[1]
    pairs = heads // 2
    wide = pairs * LANES
    tri = lower_triangle(q)
    tri_f = tri.astype(f32)
    state = None
    block = None
    for c in range(length // q):
        rows = slice(c * q, (c + 1) * q)
        seg, seg_r = chunk_segments(starts_ref, base_ref, n, c, q)
        own = seg[HALO:]
        prev = seg[HALO - 1 : HALO]
        act = []
        for g in range(pairs + 2):
            z = conv_group(raw_ref, cw_ref, seg, c, q, g)
            a = z * sigmoid(z)
            act_ref[0, rows, g * LANES : (g + 1) * LANES] = a.astype(bf16)
            act.append(a)
        b_low, c_low = act[pairs].astype(bf16), act[pairs + 1].astype(bf16)
        dt_raw = raw_ref[0, HALO + c * q : HALO + (c + 1) * q, wide + 2 * LANES :].astype(f32)
        used = iota((1, LANES), 1) < heads
        step = jnp.where(used, softplus(dt_raw + hp_ref[0:1]), 0.0)
        cum = dot(tri_f, hp_ref[1:2] * step, precision=highest)
        cum_r = cum.T
        step_ref[0, rows] = step
        cum_ref[0, rows] = cum
        cumr_ref[0, :, rows] = cum_r[:8]
        same = tri & (own[:, :1] == seg_r[:1])
        scores = dot(c_low, b_low, 1, 1)
        last = cum[q - 1 : q]
        ent = jnp.where(own == prev, jnp.exp(cum), 0.0)
        tail = jnp.where(own == own[q - 1 : q], jnp.exp(last - cum), 0.0) * step
        decay = jnp.where(own[q - 1 : q] == prev, jnp.exp(last), 0.0)
        if c:
            state_low = state.astype(bf16)
        new_state = []
        for j in range(pairs):
            lanes = slice(j * LANES, (j + 1) * LANES)
            scaled = act[j] * pair_lanes(step, j)
            out = skip_ref[0:1, lanes] * act[j]
            for half in range(2):
                h = 2 * j + half
                mixing = jnp.exp(jnp.where(same, cum[:, h : h + 1] - cum_r[h : h + 1], MASKED)) * scores
                part = jnp.where(low_half() == (half == 0), scaled, 0.0)
                out = out + dot(mixing.astype(bf16), part.astype(bf16))
            if c:
                out = out + pair_lanes(ent, j) * dot(c_low, state_low[:, lanes])
            y_ref[0, rows, lanes] = out.astype(bf16)
            weighted = (act[j] * pair_lanes(tail, j)).astype(bf16)
            new_state.append(dot(b_low, weighted, 0, 0))
        gained = jnp.concatenate(new_state, axis=1)
        if c:
            ent = ent * block
            block = block * decay
            state = expand(decay, pairs) * state + gained
        else:
            block = decay
            state = gained
        ent_ref[0, rows] = ent
    state_ref[0] = state
    decay_ref[0] = jnp.broadcast_to(expand(block, pairs), (8, wide))


def norm_rows(place_ref, halo_ref, gain_ref, *refs, low, slots):
    out_ref = refs[-1]
    n = pl.program_id(0)
    count = refs[0].shape[0]

    def scaled(rows):
        rows = rows.astype(f32)
        mean = jnp.mean(rows * rows, axis=-1, keepdims=True)
        return (rows * lax.rsqrt(mean + epsilon) * gain_ref[0:1]).astype(bf16)

    out_ref[0, :HALO] = scaled(halo_ref[0])
    for slot in range(slots):
        for k in range(low):

            @pl.when(n == slot)
            def _():
                first = HALO + (k ^ place_ref[0]) * count
                at = pl.ds(pl.multiple_of(first, HALO), count)
                out_ref[0, at] = scaled(refs[low * slot + k][...])


def pick_half(n, refs, split):
    if len(refs) == 1:
        return refs[0][0]
    return jnp.where(n < split, refs[0][0], refs[1][0])


def gate_rows(p, q):
    return pl.ds(pl.multiple_of(HALO + p * q, HALO), q)


def gate_forward(
    place_ref, y_ref, ent_ref, act_ref, enter_ref, gate_ref, gain_ref, *refs, heads, q, split
):
    u_refs, (out_ref, stat_ref, low_ref) = refs[:-3], refs[-3:]
    n, p = pl.program_id(0), pl.program_id(1)
    u_all = pick_half(n, u_refs, split)
    pairs = heads // 2
    wide = pairs * LANES
    ent = ent_ref[0]
    c_low = act_ref[0, :, wide + LANES : wide + 2 * LANES]
    squares = jnp.zeros((q, LANES), f32)
    products = jnp.zeros((q, LANES), f32)
    for j in range(pairs):
        lanes = slice(j * LANES, (j + 1) * LANES)
        y = y_ref[0, :, lanes] + pair_lanes(ent, j) * dot(c_low, enter_ref[0, :, lanes])
        out_ref[0, :, lanes] = y.astype(bf16)
        z = gate_ref[0, gate_rows(p, q), lanes].astype(f32)
        gated = y * (z * sigmoid(z))
        squares = squares + gated * gated
        gated = gated * gain_ref[0:1, lanes]
        low_ref[0, :, lanes] = gated.astype(bf16)
        products = products + gated * u_all[:, lanes].astype(f32)
    squares = jnp.sum(squares, axis=1, keepdims=True)
    products = jnp.sum(products, axis=1, keepdims=True)
    lane = iota((q, LANES), 1)
    packed = jnp.where(lane == 0, squares, jnp.where(lane == 1, products, 0.0))
    stat_ref[0] = packed.T[:8]


def gate_backward(
    place_ref,
    y_ref,
    ent_ref,
    act_ref,
    gate_ref,
    gain_ref,
    stat_ref,
    *refs,
    heads,
    q,
    columns,
    split,
):
    u_refs, (dy_ref, dgate_ref, low_ref, enter_grad_ref, sums_ref) = refs[:-5], refs[-5:]
    n, p = pl.program_id(0), pl.program_id(1)
    u_all = pick_half(n, u_refs, split)
    pairs = heads // 2
    wide = pairs * LANES

    @pl.when(p == 0)
    def _():
        dgate_ref[0, :HALO] = jnp.zeros((HALO, wide), bf16)
        sums_ref[0] = jnp.zeros((8, wide), f32)
        enter_grad_ref[0] = jnp.zeros(enter_grad_ref.shape[1:], f32)

    sums = jnp.concatenate([stat_ref[0], jnp.zeros((LANES - 8, q), f32)], axis=0).T
    scale = lax.rsqrt(sums[:, 0:1] / columns + epsilon)
    pull = scale * scale * scale * sums[:, 1:2] / columns
    ent = ent_ref[0]
    c_low = act_ref[0, :, wide + LANES : wide + 2 * LANES]
    for j in range(pairs):
        lanes = slice(j * LANES, (j + 1) * LANES)
        y = y_ref[0, :, lanes].astype(f32)
        z = gate_ref[0, gate_rows(p, q), lanes].astype(f32)
        u = u_all[:, lanes].astype(f32)
        gain = gain_ref[0:1, lanes]
        sg = sigmoid(z)
        silu = z * sg
        gated = y * silu
        unit = gated * scale
        dgated = scale * gain * u - pull * gated
        dy = dgated * silu
        dy_ref[0, :, lanes] = dy.astype(bf16)
        dgate_ref[0, gate_rows(p, q), lanes] = (
            dgated * y * (sg * (1.0 + z * (1.0 - sg)))
        ).astype(bf16)
        low_ref[0, :, lanes] = (unit * gain).astype(bf16)
        sums_ref[0, 0:1, lanes] += jnp.sum(u * unit, axis=0, keepdims=True)
        sums_ref[0, 1:2, lanes] += jnp.sum(
            dy * act_ref[0, :, lanes].astype(f32), axis=0, keepdims=True
        )
        enter_grad_ref[0, :, lanes] += dot(c_low, (dy * pair_lanes(ent, j)).astype(bf16), 0, 0)


def normed_backward(place_ref, draw_ref, dgate_ref, back_ref, conv_ref, gate_ref, out_ref, *, q):
    p = pl.program_id(1)
    rows = gate_rows(p, q)
    out = dot(draw_ref[0, rows], conv_ref[...], 1, 1) + dot(dgate_ref[0, rows], gate_ref[...], 1, 1)
    out_ref[0] = out.astype(bf16)

    @pl.when(p == pl.num_programs(1) - 1)
    def _():
        out_ref[0, q - HALO :] = (out[q - HALO :] + back_ref[0].astype(f32)).astype(bf16)


def scan_backward_inner(
    starts_ref,
    base_ref,
    act_ref,
    dy_ref,
    step_ref,
    cum_ref,
    cumr_ref,
    dscaled_ref,
    dbc_ref,
    dcum_ref,
    *,
    heads,
    q,
):
    n = pl.program_id(0)
    pairs = heads // 2
    wide = pairs * LANES
    tri = lower_triangle(q)
    for c in range(dy_ref.shape[1] // q):
        rows = slice(c * q, (c + 1) * q)
        first = base_ref[0] + c * q
        seg = segment(starts_ref, n, first + iota((q, LANES), 0))
        seg_r = segment(starts_ref, n, first + iota((8, q), 1))
        same = tri & (seg[:, :1] == seg_r[:1])
        b_low = act_ref[0, rows, wide : wide + LANES]
        c_low = act_ref[0, rows, wide + LANES : wide + 2 * LANES]
        scores = dot(c_low, b_low, 1, 1)
        step = step_ref[0, rows]
        cum = cum_ref[0, rows]
        cum_r = cumr_ref[0, :, rows]
        dscores = jnp.zeros((q, q), f32)
        lane = iota((q, LANES), 1)
        gain_t = jnp.zeros((q, LANES), f32)
        lost = []
        for j in range(pairs):
            lanes = slice(j * LANES, (j + 1) * LANES)
            scaled = (act_ref[0, rows, lanes].astype(f32) * pair_lanes(step, j)).astype(bf16)
            dy = dy_ref[0, rows, lanes].astype(f32)
            out = jnp.zeros((q, LANES), f32)
            for half in range(2):
                h = 2 * j + half
                decays = jnp.exp(jnp.where(same, cum[:, h : h + 1] - cum_r[h : h + 1], MASKED))
                mixing = decays * scores
                part = jnp.where(low_half() == (half == 0), dy, 0.0).astype(bf16)
                dmix = dot(part, scaled, 1, 1) * decays
                dscores = dscores + dmix
                flow = dmix * scores
                gain_t = jnp.where(lane == h, jnp.sum(flow, axis=1, keepdims=True), gain_t)
                lost.append(jnp.sum(flow, axis=0, keepdims=True))
                out = out + dot(mixing.astype(bf16), part, 0, 0)
            dscaled_ref[0, rows, lanes] = out.astype(bf16)
        lost = jnp.concatenate(lost + [jnp.zeros((LANES - heads, q), f32)], axis=0)
        dcum_ref[0, rows] = gain_t - lost.T
        dlow = dscores.astype(bf16)
        dbc_ref[0, rows, :LANES] = dot(dlow, c_low, 0, 0).astype(bf16)
        dbc_ref[0, rows, LANES:] = dot(dlow, b_low).astype(bf16)


def scan_backward_outer(
    starts_ref,
    base_ref,
    raw_ref,
    act_ref,
    dy_ref,
    step_ref,
    cum_ref,
    dscaled_ref,
    dbc_ref,
    dcum_ref,
    enter_ref,
    leave_ref,
    cw_ref,
    hp_ref,
    skip_ref,
    draw_ref,
    dconv_ref,
    dhead_ref,
    dz_ref,
    *,
    heads,
    q,
):
    n = pl.program_id(0)
    length = dy_ref.shape[1]
    chunks = length // q
    pairs = heads // 2
    wide = pairs * LANES
    tri_f = lower_triangle(q).astype(f32)
    used = iota((1, LANES), 1) < heads
    groups = pairs + 2

    prepared = []
    state = enter_ref[0].astype(f32)
    for c in range(chunks):
        rows = slice(c * q, (c + 1) * q)
        seg, _ = chunk_segments(starts_ref, base_ref, n, c, q)
        own, prev = seg[HALO:], seg[HALO - 1 : HALO]
        cum = cum_ref[0, rows]
        last = cum[q - 1 : q]
        ent = jnp.where(own == prev, jnp.exp(cum), 0.0)
        fade = jnp.where(own == own[q - 1 : q], jnp.exp(last - cum), 0.0)
        decay = jnp.where(own[q - 1 : q] == prev, jnp.exp(last), 0.0)
        prepared.append((seg, ent, fade, decay, state))
        if c + 1 < chunks:
            tail = fade * step_ref[0, rows]
            b_low = act_ref[0, rows, wide : wide + LANES]
            gained = [
                dot(
                    b_low,
                    (
                        act_ref[0, rows, j * LANES : (j + 1) * LANES].astype(f32)
                        * pair_lanes(tail, j)
                    ).astype(bf16),
                    0,
                    0,
                )
                for j in range(pairs)
            ]
            state = expand(decay, pairs) * state + jnp.concatenate(gained, axis=1)

    dconv_ref[0] = jnp.zeros(dconv_ref.shape[1:], f32)
    dhead_ref[0] = jnp.zeros(dhead_ref.shape[1:], f32)
    dz_ref[:HALO] = jnp.zeros((HALO, groups * LANES), f32)
    dz_ref[HALO + length :] = jnp.zeros((8, groups * LANES), f32)
    draw_ref[0, :HALO, groups * LANES :] = jnp.zeros((HALO, LANES), bf16)
    grad = leave_ref[0].astype(f32)
    for c in reversed(range(chunks)):
        rows = slice(c * q, (c + 1) * q)
        seg, ent, fade, decay, state = prepared[c]
        step = step_ref[0, rows]
        tail = fade * step
        b_low = act_ref[0, rows, wide : wide + LANES]
        c_low = act_ref[0, rows, wide + LANES : wide + 2 * LANES]
        state_low = state.astype(bf16)
        grad_low = grad.astype(bf16)
        db = dbc_ref[0, rows, :LANES].astype(f32)
        dc = dbc_ref[0, rows, LANES:].astype(f32)
        dx = []
        by_step, by_tail, by_ent, next_grad = [], [], [], []
        for j in range(pairs):
            lanes = slice(j * LANES, (j + 1) * LANES)
            x = act_ref[0, rows, lanes].astype(f32)
            dy = dy_ref[0, rows, lanes].astype(f32)
            dscaled = dscaled_ref[0, rows, lanes].astype(f32)
            dweighted = dot(b_low, grad_low[:, lanes])
            wide_tail = pair_lanes(tail, j)
            entered = (dy * pair_lanes(ent, j)).astype(bf16)
            dx.append(
                dscaled * pair_lanes(step, j) + skip_ref[0:1, lanes] * dy + dweighted * wide_tail
            )
            by_step.append(dscaled * x)
            by_tail.append(dweighted * x)
            by_ent.append(dy * dot(c_low, state_low[:, lanes]))
            db = db + dot((x * wide_tail).astype(bf16), grad_low[:, lanes], 1, 1)
            dc = dc + dot(entered, state_low[:, lanes], 1, 1)
            next_grad.append(dot(c_low, entered, 0, 0))
        dtail = head_sum(jnp.concatenate(by_tail, axis=1))
        dent = head_sum(jnp.concatenate(by_ent, axis=1))
        moved = dtail * tail
        ddecay = head_sum(jnp.sum(grad * state, axis=0, keepdims=True))
        at_last = jnp.sum(moved, axis=0, keepdims=True) + ddecay * decay
        dcum = dcum_ref[0, rows] + dent * ent - moved
        dcum = dcum + jnp.where(iota((q, LANES), 0) == q - 1, at_last, 0.0)
        drates = dot(tri_f, dcum, 0, 0, precision=highest)
        rate = hp_ref[1:2]
        dstep = head_sum(jnp.concatenate(by_step, axis=1)) + dtail * fade + drates * rate
        dt_raw = raw_ref[0, HALO + c * q : HALO + (c + 1) * q, groups * LANES :].astype(f32)
        ddt = jnp.where(used, dstep * sigmoid(dt_raw + hp_ref[0:1]), 0.0)
        draw_ref[0, HALO + c * q : HALO + (c + 1) * q, groups * LANES :] = ddt.astype(bf16)
        dhead_ref[0, 0:1] += jnp.sum(ddt, axis=0, keepdims=True)
        dhead_ref[0, 1:2] += jnp.sum(
            jnp.where(used, drates * (rate * step), 0.0), axis=0, keepdims=True
        )
        grad = expand(decay, pairs) * grad + jnp.concatenate(next_grad, axis=1)
        for g in range(groups):
            lanes = slice(g * LANES, (g + 1) * LANES)
            z = conv_group(raw_ref, cw_ref, seg, c, q, g)
            sg = sigmoid(z)
            dact = dx[g] if g < pairs else (db, dc)[g - pairs]
            dz = dact * (sg * (1.0 + z * (1.0 - sg)))
            dz_ref[HALO + c * q : HALO + (c + 1) * q, lanes] = dz
            window = raw_ref[0, c * q : c * q + q + HALO, lanes].astype(f32)
            dconv_ref[0, 4:5, lanes] += jnp.sum(dz, axis=0, keepdims=True)
            dconv_ref[0, 3:4, lanes] += jnp.sum(dz * window[HALO:], axis=0, keepdims=True)
            for k in range(1, 4):
                near = seg[HALO:] == seg[HALO - k : HALO - k + q]
                source = jnp.where(near, window[HALO - k : HALO - k + q], 0.0)
                dconv_ref[0, 3 - k : 4 - k, lanes] += jnp.sum(dz * source, axis=0, keepdims=True)

    places = base_ref[0] - HALO + iota((HALO + length + 8, LANES), 0)
    seg = segment(starts_ref, n, places)
    total = HALO + length
    for g in range(groups):
        lanes = slice(g * LANES, (g + 1) * LANES)
        taps = cw_ref[:, lanes]
        out = taps[3:4] * dz_ref[:total, lanes]
        for k in range(1, 4):
            near = seg[k : k + total] == seg[:total]
            out = out + taps[3 - k : 4 - k] * jnp.where(near, dz_ref[k : k + total, lanes], 0.0)
        draw_ref[0, :, lanes] = out.astype(bf16)


def per_sequence(shape):
    return pl.BlockSpec((1,) + shape[1:], lambda n, *_: (n, 0, 0))


def shared(shape):
    return pl.BlockSpec(shape, lambda n, *_: (0, 0))


def call(kernel, scalars, inputs, outputs, flops, scratch=(), grid=None, ins=None, outs=None):
    specs = [shared(a.shape) if a.ndim == 2 else per_sequence(a.shape) for a in inputs]
    moved = sum(a.size * a.dtype.itemsize for a in list(inputs) + list(outputs))
    return pl.pallas_call(
        kernel,
        out_shape=outputs,
        grid_spec=pltpu.PrefetchScalarGridSpec(
            num_scalar_prefetch=len(scalars),
            grid=grid or (outputs[0].shape[0],),
            in_specs=ins or specs,
            out_specs=outs or [per_sequence(o.shape) for o in outputs],
            scratch_shapes=list(scratch),
        ),
        cost_estimate=pl.CostEstimate(flops=flops, transcendentals=0, bytes_accessed=moved),
        interpret=INTERPRET,
    )(*scalars, *inputs)


def spread(*shape, dtype=f32):
    return jax.ShapeDtypeStruct(shape, dtype)


def after(value, *others):
    return lax.optimization_barrier((value,) + others)[0]


def is_small():
    return lax.axis_size("lo") == 2 and lax.axis_size("bx") == 2


def gather_pieces(rows, hold):
    if not is_small():
        return [lax.all_gather(rows, PLANE, axis=0, tiled=False)]
    across = lax.ppermute(rows, "bx", SWAP)
    beside = lax.ppermute(rows, "lo", SWAP)
    corner = lax.ppermute(rows, ("lo", "bx"), CROSS)
    half = jnp.stack([after(rows, hold), beside, across, corner])
    return [half, lax.ppermute(half, "core", SWAP)]


def gather_single(rows):
    if not is_small():
        got = lax.all_gather(rows, PLANE, axis=0, tiled=False)
        return [got[i] for i in range(got.shape[0])]
    near = [
        rows,
        lax.ppermute(rows, "lo", SWAP),
        lax.ppermute(rows, "bx", SWAP),
        lax.ppermute(rows, ("lo", "bx"), CROSS),
    ]
    return near + [lax.ppermute(near[i], "core", SWAP) for i in range(4)]


def gather_edges(pieces, rows):
    low = lax.axis_size("lo")
    high = lax.axis_size("hi")
    place = lax.axis_index("lo")
    used = len(pieces) // 2 if is_small() else len(pieces)
    edges = []
    for i in range(0, used, low):
        at = [pieces[i + k][-rows:] for k in range(low)]
        edge = at[0]
        if low == 2:
            edge = jnp.where(place == 1, at[0], at[1])
        edges.append(edge)
    route = tuple((i, i + 1) for i in range(high - 1))
    came = lax.ppermute(jnp.stack(edges), "hi", route)
    if is_small():
        came = jnp.concatenate([came, lax.ppermute(came, "core", SWAP)])
    return came


def scatter_pieces(make):
    if not is_small():
        sent = make(0, lax.axis_size("bx") * lax.axis_size("core"))
        return lax.psum_scatter(sent, PLANE, scatter_dimension=0, tiled=False).astype(f32)
    other = make(2, 2)
    came = lax.ppermute(other, "core", SWAP)
    own = make(0, 2)

    def piece(i):
        return own[i].astype(f32) + came[i].astype(f32)

    beside = lax.ppermute(piece(1).astype(bf16), "lo", SWAP)
    across = lax.ppermute(piece(2).astype(bf16), "bx", SWAP)
    corner = lax.ppermute(piece(3).astype(bf16), ("lo", "bx"), CROSS)
    return piece(0) + across.astype(f32) + beside.astype(f32) + corner.astype(f32)


def sum_plane(stats):
    if not is_small():
        return lax.psum(stats, PLANE)
    rest = stats.shape[1:]
    grid = stats.reshape((2, 2) + rest)
    grid = grid + lax.ppermute(grid[::-1], "core", SWAP)
    grid = grid + lax.ppermute(grid[:, ::-1], "bx", SWAP)
    grid = grid + lax.ppermute(grid, "lo", SWAP)
    return grid.reshape(stats.shape)


def gather_starts(starts):
    if not is_small():
        return lax.all_gather(starts, ("bx", "core"), axis=0, tiled=True)
    half = jnp.concatenate([starts, lax.ppermute(starts, "bx", SWAP)])
    return jnp.concatenate([half, lax.ppermute(half, "core", SWAP)])


def piece_of(low, offset=0):
    def index(n, p, place):
        return (low * n + (p ^ place[0]) - offset, 0, 0)

    return index


def half_specs(halves, shape, low):
    count = halves[0].shape[0]
    specs = []
    for h in range(len(halves)):

        def index(n, p, place, h=h):
            return (jnp.clip(low * n + (p ^ place[0]) - h * count, 0, count - 1), 0, 0)

        specs.append(pl.BlockSpec((1,) + shape, index))
    return specs


def chain(state, decay, forward):
    size = lax.axis_size("hi")
    place = lax.axis_index("hi")
    enter = jnp.zeros(state.shape, bf16)
    for k in range(size - 1):
        source = k if forward else size - 1 - k
        target = source + 1 if forward else source - 1
        passed = (state + decay * enter.astype(f32)).astype(bf16)
        came = lax.ppermute(passed, "hi", ((source, target),))
        enter = jnp.where(place == target, came, enter)
    return enter


def to_shards(columns, width):
    low = lax.axis_size("lo")
    batch = lax.axis_size("bx") * lax.axis_size("core")
    rows = columns.shape[0]
    split = columns.reshape(rows, batch, low, width)
    return jnp.transpose(split, (2, 1, 0, 3)).reshape(low * batch, rows, width)


def from_shards(blocks):
    low = lax.axis_size("lo")
    batch = lax.axis_size("bx") * lax.axis_size("core")
    _, rows, width = blocks.shape
    split = blocks.reshape(low, batch, rows, width)
    return jnp.transpose(split, (2, 1, 0, 3)).reshape(rows, batch * low * width)


def exchange(blocks, axes=PLANE):
    return lax.all_to_all(blocks, axes, 0, 0, tiled=True)


def step_of(
    residual_in,
    seg_ids,
    doc_starts,
    norm_gain,
    in_weight,
    conv_weight,
    conv_bias,
    dt_bias,
    a_log,
    skip_weight,
    gate_gain,
    out_weight,
    cotangent,
):
    high, low = lax.axis_size("hi"), lax.axis_size("lo")
    batch = lax.axis_size("bx") * lax.axis_size("core")
    team = low * batch
    devices = high * team
    row_count, features = residual_in.shape[1:]
    heads = dt_bias.shape[0] // team
    inner = gate_gain.shape[0] * devices
    channels = conv_bias.shape[0] * devices
    width = inner // team
    shared_width = channels - inner
    taps = conv_weight.shape[1]
    length = low * row_count
    q = row_count
    total = HALO + length
    pad_width = width + shared_width + LANES
    at_dt = width + shared_width
    k_rows = in_weight.shape[0]
    o_rows = out_weight.shape[0]
    sequences = batch
    place_low = lax.axis_index("lo")
    place_batch = lax.axis_index("bx") * lax.axis_size("core") + lax.axis_index("core")
    shard = place_batch * low + place_low
    place = place_low.reshape(1).astype(jnp.int32)
    base = (lax.axis_index("hi") * length).reshape(1).astype(jnp.int32)

    lanes_of = conv_bias.shape[0]
    small = jnp.stack(
        [conv_weight[:, k] for k in range(taps)]
        + [conv_bias]
        + [jnp.pad(gain, (0, lanes_of - gain.shape[0])) for gain in (gate_gain, norm_gain)]
    )
    small = jnp.pad(small, ((0, 8 - taps - 3), (0, LANES - lanes_of))).reshape(-1)
    small_lanes = -(-small.shape[0] // k_rows)
    small = jnp.pad(small, (0, small_lanes * k_rows - 8 * LANES)).reshape(k_rows, small_lanes)
    at_small = at_dt + heads
    block = jnp.concatenate(
        [
            to_shards(in_weight[:, inner : 2 * inner], width),
            jnp.broadcast_to(
                in_weight[:, 2 * inner : inner + channels], (team, k_rows, shared_width)
            ),
            to_shards(in_weight[:, inner + channels :], heads),
            jnp.broadcast_to(small, (team, k_rows, small_lanes)),
            jnp.zeros((team, k_rows, pad_width - at_small - small_lanes), bf16),
        ],
        axis=2,
    )
    rows_of_plane = exchange(block)
    small = rows_of_plane[:, :, at_small : at_small + small_lanes].reshape(team, -1)
    small = small[:, : 8 * LANES].reshape(team, 8, LANES)
    rows_of_plane = rows_of_plane.reshape(team * k_rows, pad_width)
    conv_w = lax.all_gather(rows_of_plane, "hi", axis=0, tiled=True)

    resid = gather_single(after(residual_in[0], rows_of_plane))
    starts = gather_starts(after(doc_starts, rows_of_plane))
    halo = gather_edges(resid, HALO)

    small = lax.all_gather(small, "hi", axis=0, tiled=False).reshape(devices, 8, LANES)
    small = jnp.swapaxes(small.astype(f32), 0, 1)
    table = small[: taps + 1, :, :lanes_of].reshape(taps + 1, channels)
    full_gate = small[taps + 1, :, : gate_gain.shape[0]].reshape(1, inner)
    full_gain = small[taps + 2, :, : norm_gain.shape[0]].reshape(1, features)
    cw = jnp.concatenate(
        [lax.dynamic_slice_in_dim(table, shard * width, width, 1), table[:, inner:]], axis=1
    )
    cw = jnp.pad(cw, ((0, 8 - taps - 1), (0, 0)))
    gain_row = jnp.broadcast_to(
        lax.dynamic_slice_in_dim(full_gate, shard * width, width, 1), (8, width)
    )
    own_head = functools.partial(
        lax.dynamic_slice_in_dim, start_index=shard * heads, slice_size=heads
    )
    hp = jnp.stack([own_head(dt_bias), -jnp.exp(own_head(a_log))])
    hp = jnp.pad(hp, ((0, 6), (0, LANES - heads)))
    skip_row = jnp.broadcast_to(jnp.repeat(own_head(skip_weight), width // heads), (8, width))

    sub = features // width
    gate_block = exchange(after(to_shards(in_weight[:, :inner], width), rows_of_plane))
    gate_block = gate_block.reshape(sub, -1, width)
    gate_block = jnp.concatenate([gate_block[i] for i in range(sub)], axis=1)
    gate_rows_count = gate_block.shape[0]
    second = lax.all_gather(
        jnp.concatenate([gate_block, out_weight]), "hi", axis=0, tiled=False
    )

    norm_row = jnp.broadcast_to(full_gain, (8, features))
    (normed,) = call(
        functools.partial(norm_rows, low=low, slots=sequences),
        (place,),
        [halo, norm_row] + resid,
        (spread(sequences, total, features, dtype=bf16),),
        sequences * total * features * 10,
    )
    flat = normed.reshape(-1, features)
    raw = dot(flat, conv_w).astype(bf16).reshape(sequences, total, pad_width)

    act_shape = (sequences, length, width + shared_width)
    wide_shape = (sequences, length, width)
    col_shape = (sequences, length, LANES)
    row_shape = (sequences, 8, length)
    state_shape = (sequences, shared_width // 2, width)
    unit = sequences * length * width
    act, y_local, ent, step, cum, cum_r, state, decay = call(
        functools.partial(scan_forward, heads=heads, q=q),
        (starts, base),
        (raw, cw, hp, skip_row),
        (
            spread(*act_shape, dtype=bf16),
            spread(*wide_shape, dtype=bf16),
            spread(*col_shape),
            spread(*col_shape),
            spread(*col_shape),
            spread(*row_shape),
            spread(*state_shape),
            spread(sequences, 8, width),
        ),
        unit * 8 * q,
    )
    cot = gather_pieces(after(cotangent[0], normed), state)
    split = sequences // len(cot)
    decay = decay[:, :1]
    enter = chain(state, decay, True)

    gate_w = jnp.concatenate(
        [
            second[:, None, :gate_rows_count, i * width : (i + 1) * width]
            for i in range(sub)
        ],
        axis=1,
    ).reshape(features, width)
    gate = dot(flat, gate_w).astype(bf16).reshape(sequences, total, width)
    out_w = second[:, gate_rows_count:]
    out_w = exchange(out_w, ("bx", "core")).reshape(batch, high // batch, o_rows, features)
    out_w = jnp.swapaxes(out_w, 0, 1).reshape(width, features)
    u = [
        dot(half.reshape(-1, features), out_w, 1, 1).astype(bf16).reshape(-1, row_count, width)
        for half in cot
    ]

    def chunk(lanes):
        return pl.BlockSpec((1, q, lanes), lambda n, p, place: (n, p, 0))

    def whole(rows, lanes):
        return pl.BlockSpec((1, rows, lanes), lambda n, p, place: (n, 0, 0))

    def fixed(a):
        return pl.BlockSpec(a.shape, lambda n, p, place: (0, 0))

    across = pl.BlockSpec((1, 8, q), lambda n, p, place: (n, 0, p))
    states = whole(*state_shape[1:])
    u_specs = half_specs(cot, (row_count, width), low)
    grid = (sequences, low)
    y, stats, unscaled = call(
        functools.partial(gate_forward, heads=heads, q=q, split=split),
        (place,),
        [y_local, ent, act, enter, gate, gain_row] + u,
        (
            spread(*wide_shape, dtype=bf16),
            spread(*row_shape),
            spread(team, row_count, width, dtype=bf16),
        ),
        unit * 300,
        grid=grid,
        ins=[
            chunk(width),
            chunk(LANES),
            chunk(width + shared_width),
            states,
            whole(total, width),
            fixed(gain_row),
        ]
        + u_specs,
        outs=[chunk(width), across, pl.BlockSpec((1, q, width), piece_of(low))],
    )
    stats = sum_plane(stats)
    my_slot = 0 if is_small() else place_batch

    def mixed_pieces(first, slots):
        rows = unscaled[first * low : (first + slots) * low].reshape(-1, width)
        return dot(rows, out_w).astype(bf16).reshape(-1, row_count, features)

    mixed = scatter_pieces(mixed_pieces)
    own_squares = lax.dynamic_slice_in_dim(stats[my_slot, 0], place_low * row_count, row_count)
    mixed_scale = lax.rsqrt(own_squares / inner + epsilon)[:, None]
    mixed_out = (residual_in[0].astype(f32) + mixed_scale * mixed).astype(bf16)

    dy, dgate, mixer_low, enter_grad, gate_sums = call(
        functools.partial(gate_backward, heads=heads, q=q, columns=inner, split=split),
        (place,),
        [y, ent, act, gate, gain_row, stats] + u,
        (
            spread(*wide_shape, dtype=bf16),
            spread(sequences, total, width, dtype=bf16),
            spread(team, row_count, width, dtype=bf16),
            spread(*state_shape),
            spread(sequences, 8, width),
        ),
        unit * 300,
        grid=grid,
        ins=[
            chunk(width),
            chunk(LANES),
            chunk(width + shared_width),
            whole(total, width),
            fixed(gain_row),
            across,
        ]
        + u_specs,
        outs=[
            chunk(width),
            whole(total, width),
            pl.BlockSpec((1, q, width), piece_of(low)),
            states,
            whole(8, width),
        ],
    )
    leave = chain(enter_grad, decay, False)
    gate_sums = jnp.sum(gate_sums, axis=0)
    dskip = jnp.sum(gate_sums[1].reshape(heads, -1), axis=1)
    gain_all = lax.dynamic_update_slice(
        jnp.zeros((1, inner), f32), gate_sums[:1], (0, shard * width)
    )

    count = cot[0].shape[0]
    out_grad = 0.0
    for h, half in enumerate(cot):
        rows = mixer_low[h * count : (h + 1) * count].reshape(-1, width)
        out_grad = out_grad + dot(rows, half.reshape(-1, features), 0, 0)
    out_grad = out_grad.astype(bf16).reshape(high // batch, batch, o_rows, features)
    out_grad = exchange(
        jnp.swapaxes(out_grad, 0, 1).reshape(high, o_rows, features), ("bx", "core")
    )
    dgate_flat = dgate.reshape(-1, width)
    gate_grad = dot(flat, dgate_flat, 0, 0).astype(bf16)
    gate_grad = gate_grad.reshape(high, sub, gate_rows_count, width)
    gate_grad = jnp.concatenate([gate_grad[:, i] for i in range(sub)], axis=2)
    early = jnp.concatenate([gate_grad, out_grad], axis=1)
    early = lax.psum_scatter(early, "hi", scatter_dimension=0, tiled=False)

    dscaled, dbc, dcum = call(
        functools.partial(scan_backward_inner, heads=heads, q=q),
        (starts, base),
        (act, dy, step, cum, cum_r),
        (
            spread(*wide_shape, dtype=bf16),
            spread(sequences, length, shared_width, dtype=bf16),
            spread(*col_shape),
        ),
        unit * 16 * q,
    )
    draw, dconv, dhead = call(
        functools.partial(scan_backward_outer, heads=heads, q=q),
        (starts, base),
        (raw, act, dy, step, cum, dscaled, dbc, dcum, enter, leave, cw, hp, skip_row),
        (
            spread(sequences, total, pad_width, dtype=bf16),
            spread(sequences, 8, width + shared_width),
            spread(sequences, 8, LANES),
        ),
        unit * 2000,
        scratch=(pltpu.VMEM((total + 8, width + shared_width), f32),),
    )
    draw_flat = draw.reshape(-1, pad_width)

    edge_rows = draw[:, :HALO].reshape(-1, pad_width)
    returned = lax.ppermute(
        dot(edge_rows, conv_w, 1, 1).astype(bf16).reshape(sequences, HALO, features),
        "hi",
        tuple((i + 1, i) for i in range(high - 1)),
    )

    late = dot(flat, draw_flat, 0, 0).astype(bf16)
    dconv = jnp.sum(dconv, axis=0)
    dhead = jnp.sum(dhead, axis=0)

    def placed(mine, size):
        return lax.dynamic_update_slice(
            jnp.zeros((mine.shape[0], size), f32), mine, (0, shard * mine.shape[1])
        )

    by_owner = jnp.concatenate(
        [placed(dconv[: taps + 1, :width], inner), dconv[: taps + 1, width:]], axis=1
    ).reshape(taps + 1, devices, lanes_of)
    heads_all = placed(jnp.concatenate([dhead[:2, :heads], dskip[None]]), heads * team)
    spare = pad_width - at_dt - heads

    def rows_for_owners(array):
        array = jnp.broadcast_to(array, (array.shape[0], devices, array.shape[2]))
        return jnp.pad(array, ((0, 0), (0, 0), (0, spare - array.shape[2])))

    spare_rows = jnp.concatenate(
        [
            rows_for_owners(by_owner),
            rows_for_owners(gain_all.reshape(1, devices, -1)),
            rows_for_owners(heads_all[:, None]),
        ]
    )
    spare_rows = jnp.swapaxes(spare_rows, 0, 1)
    spare_rows = jnp.pad(spare_rows, ((0, 0), (0, k_rows - spare_rows.shape[1]), (0, 0)))
    spare_rows = spare_rows.reshape(devices * k_rows, spare).astype(bf16)
    late = jnp.concatenate([late[:, : at_dt + heads], spare_rows], axis=1)
    late_sum = lax.psum_scatter(late, "hi", scatter_dimension=0, tiled=True)

    def grad_pieces(first, slots):
        def slot(n, p, place):
            return (n + first, 0, 0)

        (out,) = call(
            functools.partial(normed_backward, q=q),
            (place,),
            (draw, dgate, returned, conv_w, gate_w),
            (spread(slots * low, row_count, features, dtype=bf16),),
            2 * slots * length * features * (pad_width + width),
            grid=(slots, low),
            ins=[
                pl.BlockSpec((1, total, pad_width), slot),
                pl.BlockSpec((1, total, width), slot),
                pl.BlockSpec((1, HALO, features), slot),
                fixed(conv_w),
                fixed(gate_w),
            ],
            outs=[pl.BlockSpec((1, q, features), piece_of(low))],
        )
        return out

    own_grad = scatter_pieces(grad_pieces)
    own_grad = own_grad * full_gain
    own = residual_in[0].astype(f32)
    own_scale = lax.rsqrt(jnp.mean(own * own, axis=-1, keepdims=True) + epsilon)
    unit_rows = own * own_scale
    along = jnp.mean(own_grad * unit_rows, axis=-1, keepdims=True)
    input_grad = cotangent[0].astype(f32) + own_scale * (own_grad - unit_rows * along)

    gate_share = jnp.concatenate(
        [early[None, :gate_rows_count, i * width : (i + 1) * width] for i in range(sub)]
    )
    gate_share = exchange(gate_share.reshape(team, k_rows, width))
    gate_share = from_shards(gate_share).astype(f32)
    out_share = early[gate_rows_count:].astype(f32)
    late_share = exchange(late_sum.reshape(team, k_rows, pad_width)).astype(f32)
    summed = jnp.sum(late_share[:, :, width:], axis=0)
    little = summed[:, shared_width + heads :]
    in_share = jnp.concatenate(
        [
            gate_share,
            from_shards(late_share[:, :, :width]),
            summed[:, :shared_width],
            from_shards(late_share[:, :, at_dt : at_dt + heads]),
        ],
        axis=1,
    )
    norm_share = jnp.sum(in_share * in_weight.astype(f32), axis=1) / norm_gain.astype(f32)
    return (
        mixed_out[None],
        input_grad[None],
        norm_share,
        in_share,
        little[:taps, :lanes_of].T,
        little[taps, :lanes_of],
        little[taps + 2, : heads * team],
        little[taps + 3, : heads * team],
        little[taps + 4, : heads * team],
        little[taps + 1, : gate_gain.shape[0]],
        out_share,
    )


def solution(mesh):
    seq, batch = mesh.shape["seq"], mesh.shape["batch"]
    low = max(1, 8 // batch)
    split = Mesh(
        mesh.devices.reshape(seq // low, low, batch // 2, 2), ("hi", "lo", "bx", "core")
    )
    everything = ("hi", "lo", "bx", "core")
    batches, blocks = ("bx", "core"), ("hi", "lo")
    rows = P(batches, blocks, None)
    return jax.shard_map(
        step_of,
        mesh=split,
        in_specs=(
            rows,
            P(batches, blocks),
            P(batches, None),
            P(everything),
            P(everything, None),
            P(everything, None),
            P(everything),
            P(),
            P(),
            P(),
            P(everything),
            P(everything, None),
            rows,
        ),
        out_specs=(
            rows,
            rows,
            P(everything),
            P(everything, None),
            P(everything, None),
            P(everything),
            P(),
            P(),
            P(),
            P(everything),
            P(everything, None),
        ),
        check_vma=False,
    )
```

time: 1390 us -> 482 us (0.35)
  waiting for transfers between devices: 911 us -> 113 us
  Pallas kernels: 0 us -> 120 us
  matrix products: 164 us -> 59 us
  blocking collectives: 122 us -> 29.9 us
  starting transfers between devices: 5.88 us -> 53.8 us
  other arithmetic: 82.3 us -> 39.9 us
  local copies, waits for them, and re-layouts: 71.3 us -> 45.3 us
    reduce_scatter x2, waiting for transfers between devices: 579 us -> 0.01 us  [the longest x1 0.01 us: step_of(): early = lax.psum_scatter(early, 'hi', scatter_dimension=0, tiled=False)]
    all_gather x4 -> x2, waiting for transfers between devices: 246 us -> 0.02 us  [the longest x1 0.02 us: step_of(): lax.all_gather(jnp.concatenate([gate_block, out_weight]), 'hi', axis=0, t...]
    pallas_call x0 -> x8, Pallas kernels: none -> 120 us  [call(): pl.pallas_call(kernel, out_shape=outputs, grid_spec=pltpu.PrefetchScalarG...]
    dot_general x18 -> x11, matrix products: 164 us -> 59 us  [dot(): lax.dot_general(a, b, (((ca,), (cb,)), ((), ())), precision=precision, pr...]
    unnamed x8 -> x4, waiting for transfers between devices: 84.8 us -> 0.07 us
    ppermute x2 -> x33, waiting for transfers between devices: 1.58 us -> 72.3 us  [the longest x6 25.5 us: chain(): came = lax.ppermute(passed, 'hi', ((source, target),))]
    all_gather x3 -> x1, blocking collectives: 78.5 us -> 14.2 us  [step_of(): lax.all_gather(small, 'hi', axis=0, tiled=False).reshape(devices, 8, LANES)]
    unnamed x1 -> x0, blocking collectives: 43.8 us -> none
  transfers between devices with their start and end apart: 9 -> 42, of which waited for: 8 -> 13; matrix products, arithmetic and copies ran while one was open for 13% -> 24% of each run, Pallas kernels for 0% -> 21%
where the time goes in v1:
time: 482 us; the launch traced here: 476 us
  Pallas kernels  120 us (25%)
  waiting for transfers between devices  113 us (23%)
  matrix products  59 us (12%)
  starting transfers between devices  53.8 us (11%)
  local copies, waits for them, and re-layouts  45.3 us (9%)
  other arithmetic  39.9 us (8%)
  blocking collectives  29.9 us (6%)
  between operations  15.1 us (3%)
    pallas_call x8, Pallas kernels, call(): pl.pallas_call(kernel, out_shape=outputs, grid_spec=pltpu.PrefetchScalarG...  120 us
    dot_general x11, matrix products, dot(): lax.dot_general(a, b, (((ca,), (cb,)), ((), ())), precision=precision, pr...  59 us
    all_to_all x5, waiting for transfers between devices, exchange(): return lax.all_to_all(blocks, axes, 0, 0, tiled=True)  40.8 us
    ppermute x6, waiting for transfers between devices, chain(): came = lax.ppermute(passed, 'hi', ((source, target),))  25.5 us
    all_to_all x5, starting transfers between devices, exchange(): return lax.all_to_all(blocks, axes, 0, 0, tiled=True)  18.4 us
    all_to_all x1, blocking collectives, exchange(): return lax.all_to_all(blocks, axes, 0, 0, tiled=True)  15.6 us
    ppermute x2, waiting for transfers between devices, scatter_pieces(): beside = lax.ppermute(piece(1).astype(bf16), 'lo', SWAP)  14.3 us
    all_gather x1, blocking collectives, step_of(): lax.all_gather(small, 'hi', axis=0, tiled=False).reshape(devices, 8, LANES)  14.2 us
  transfers between devices with their start and end apart: 42, of which 13 were waited for; matrix products, arithmetic and copies ran while one was open for 24% of the time, Pallas kernels for 21%

profile of v1, /device:TPU:0, one launch (start us, length us, event | category | flops | bytes accessed | tf_op | source)
XLA Modules:
  0.0 476.2 jit_solution(7300949161702893532)
XLA Ops:
  11.7 15.6 %all_to_all.30 = bf16[8,48,768]{2,1,0:T(8,128)(2,1)} all-to-all(bf16[8,48,768]{2,1,0:T(8,128)(2,1)S(1)} %concatenate.51), channel_id=1, replica_groups=mesh['hi'=4,'lo'=2,'bx'=2,'core'=2] {'lo','bx','core'}, dimensions={0} | all-to-all | bytes 1179648 | tf_op jit(solution)/shard_map/all_to_all | solution.py:666
  30.4 1.5 collective-permute-start.4
  31.9 1.5 collective-permute-start.2
  34.5 3.4 all-to-all-start.1
  38.0 14.2 %all_gather.12 = bf16[4,8,8,128]{3,2,1,0:T(8,128)(2,1)S(1)} all-gather(bf16[1,8,8,128]{3,2,1,0:T(8,128)(2,1)S(1)} %copy.86), channel_id=1, replica_groups=mesh['hi'=4,'lo'=2,'bx'=2,'core'=2] {'hi'}, dimensions={0}, use_global_device_ids=true | all-gather | bytes 81920 | tf_op jit(solution)/shard_map/all_gather | solution.py:741
  53.8 1.9 collective-permute-start
  55.7 1.3 constant_dynamic-slice_fusion.1
  57.0 12.1 %collective-permute-done = s32[1,12]{1,0:T(1,128)S(1)} collective-permute-done((s32[1,12]{1,0:T(1,128)S(1)}, s32[1,12]{1,0:T(1,128)S(1)}, u32[]{:S(2)}, u32[]{:S(2)}) %collective-permute-start) | collective-permute-done | bytes 80 | tf_op jit(solution)/shard_map/ppermute | solution.py:613
  70.7 1.8 pad_maximum_fusion.5
  73.4 3.7 collective-permute-start.5
  77.7 1.8 collective-permute-done.5
  83.0 7.8 %shard_map.203 = bf16[4,528,1536]{2,1,0:T(8,128)(2,1)} custom-call(s32[1]{0:T(128)} %bitcast.1.place_ref, bf16[4,16,1536]{2,1,0:T(8,128)(2,1)} %pad_maximum_fusion.7.halo_ref, f32[8,1536]{1,0:T(8,128)} %broadcast_in_dim.84.gain_ref, bf16[256,1536]{1,0:T(8,128)(2,1)} %bitcast.234, bf16[256,1536]{1,0:T(8,128)(2,1)} %copy-done.11, bf16[256,1536]{1,0:T(8,128)(2,1)} %copy-done.9, ...), custom_call_target="tpu_custom_call" | custom-call | flops 32440320 | bytes 13025280 | tf_op jit(solution)/shard_map/pallas_call | solution.py:513
  92.7 1.5 collective-permute-start.16
  94.2 9.3 %convolution_convert_fusion = bf16[2112,768]{1,0:T(8,128)(2,1)} fusion(bf16[2112,1536]{1,0:T(8,128)(2,1)} %bitcast.240, bf16[1536,768]{1,0:T(8,128)(2,1)} %all-gather.4.cloned.1.call-done.conv_ref), kind=kOutput, calls=%fused_computation | convolution fusion | flops 4984455168 | bytes 12091392 | tf_op jit(solution)/shard_map/dot_general | solution.py:25
  104.1 18.2 %shard_map.204 = (bf16[4,512,640]{2,1,0:T(8,128)(2,1)}, bf16[4,512,384]{2,1,0:T(8,128)(2,1)}, f32[4,512,128]{2,1,0:T(8,128)}, f32[4,512,128]{2,1,0:T(8,128)}, f3...) custom-call(s32[4,12]{1,0:T(4,128)} %pad_add_fusion.starts_ref, ...), custom_call_target="tpu_custom_call" | custom-call | flops 1610612736 | bytes 11522048 | tf_op jit(solution)/shard_map/pallas_call | solution.py:513
  122.3 6.4 %collective-permute-done.16 = bf16[256,1536]{1,0:T(8,128)(2,1)S(1)} collective-permute-done((bf16[256,1536]{1,0:T(8,128)(2,1)S(1)}, bf16[256,1536]{1,0:T(8,128)(2,1)S(1)}, u32[]{:S(2)}, u32[]{:S(2)}) %collective-permute-start.16) | collective-permute-done | bytes 786464 | tf_op jit(solution)/shard_map/ppermute | solution.py:545
  129.7 2.9 pad_maximum_fusion
  135.5 4.6 collective-permute-start.11
  140.2 2.4 slice.334
  142.5 4.3 all-to-all-start.2
  146.8 1.4 slice_bitcast_fusion.12
  150.1 7.6 %convolution_convert_fusion.1 = bf16[2112,384]{1,0:T(8,128)(2,1)} fusion(bf16[2112,1536]{1,0:T(8,128)(2,1)} %bitcast.241, bf16[1536,384]{1,0:T(8,128)(2,1)S(1)} %bitcast.260), kind=kOutput, calls=%fused_computation.1 | convolution fusion | flops 2492227584 | bytes 9289728 | tf_op jit(solution)/shard_map/dot_general | solution.py:25
  158.6 4.1 all-to-all-done.2
  162.7 4.9 %convolution_convert_fusion.6 = bf16[1024,384]{1,0:T(8,128)(2,1)} fusion(bf16[1024,1536]{1,0:T(8,128)(2,1)} %bitcast.46, bf16[384,1536]{1,0:T(8,128)(2,1)} %bitcast.47), kind=kOutput, calls=%fused_computation.47 | convolution fusion | flops 1208352768 | bytes 5111808 | tf_op jit(solution)/shard_map/dot_general | solution.py:25
  168.4 4.9 %convolution_convert_fusion.5 = bf16[1024,384]{1,0:T(8,128)(2,1)} fusion(bf16[1024,1536]{1,0:T(8,128)(2,1)} %bitcast.49, bf16[384,1536]{1,0:T(8,128)(2,1)} %bitcast.47), kind=kOutput, calls=%fused_computation.46 | convolution fusion | flops 1208352768 | bytes 5111808 | tf_op jit(solution)/shard_map/dot_general | solution.py:25
  173.9 9.4 %shard_map.205 = (bf16[4,512,384]{2,1,0:T(8,128)(2,1)}, f32[4,8,512]{2,1,0:T(8,128)}, bf16[8,256,384]{2,1,0:T(8,128)(2,1)}) custom-call(s32[1]{0:T(128)} %bitcast.1.place_ref, bf16[4,512,384]{2,1,0:T(8,128)(2,1)} %get-tuple-element.40.y_ref, f32[4,512,128]{2,1,0:T(8,128)} %get-tuple-element.41.ent_ref, bf16[4,512,640]{2,1,0:T(8,128)(2,1)} %get-tuple-element.42.act_ref, ...), custom_call_target="tpu_custom_call" | custom-call | flops 235929600 | bytes 12054528 | tf_op jit(solution)/shard_map/pallas_call | solution.py:513
  186.7 3.9 collective-permute-done.19
  190.6 1.6 collective-permute-start.20
  192.2 2.7 fusion.39
  195.6 10.9 %shard_map.206 = (bf16[4,512,384]{2,1,0:T(8,128)(2,1)}, bf16[4,528,384]{2,1,0:T(8,128)(2,1)}, bf16[8,256,384]{2,1,0:T(8,128)(2,1)}, f32[4,128,384]{2,1,0:T(8,128)}, f32[4,8,384]{2,1,0:T(8,128)}) custom-call(s32[1]{0:T(128)} %bitcast.1.place_ref, bf16[4,512,384]{2,1,0:T(8,128)(2,1)} %get-tuple-element.50.y_ref, f32[4,512,128]{2,1,0:T(8,128)} %get-tuple-element.41.ent_ref, ...), custom_call_target="tpu_custom_call" | custom-call | flops 235929600 | bytes 14118912 | tf_op jit(solution)/shard_map/pallas_call | solution.py:513
  206.5 3.7 convolution_bitcast_fusion.1
  210.2 2.5 fusion.1
  212.7 3.5 all-to-all-start.3
  216.3 8.2 %fusion.2 = bf16[1536,384]{1,0:T(8,128)(2,1)} fusion(bf16[4,528,1536]{2,1,0:T(8,128)(2,1)} %shard_map.203, bf16[4,528,384]{2,1,0:T(8,128)(2,1)} %get-tuple-element.60.dgate_ref), kind=kOutput, calls=%fused_computation.12 | convolution fusion | flops 2492006400 | bytes 9289728 | tf_op jit(solution)/shard_map/dot_general | solution.py:25
  225.3 1.4 reduce_sum.75
  228.5 2.3 slice_bitcast_fusion.8
  233.7 1.3 reshape_squeeze.8
  235.0 1.3 reduce_sum.77
  236.3 2.7 pad_maximum_fusion.1
  239.3 1.8 collective-permute-start.27
  241.9 20.9 %shard_map.207 = (bf16[4,512,384]{2,1,0:T(8,128)(2,1)}, bf16[4,512,256]{2,1,0:T(8,128)(2,1)}, f32[4,512,128]{2,1,0:T(8,128)}) custom-call(s32[4,12]{1,0:T(4,128)} %pad_add_fusion.starts_ref, s32[1]{0:T(128)} %bitcast.15.base_ref, bf16[4,512,640]{2,1,0:T(8,128)(2,1)} %get-tuple-element.42.act_ref, bf16[4,512,384]{2,1,0:T(8,128)(2,1)} %get-tuple-element.51.dy_ref, ...), custom_call_target="tpu_custom_call" | custom-call | flops 3221225472 | bytes 10027008 | tf_op jit(solution)/shard_map/pallas_call | solution.py:513
  262.8 24.8 %collective-permute-done.27 = bf16[4,128,384]{2,1,0:T(8,128)(2,1)S(1)} collective-permute-done((bf16[4,128,384]{2,1,0:T(8,128)(2,1)S(1)}, bf16[4,128,384]{2,1,0:T(8,128)(2,1)S(1)}, u32[]{:S(2)}, u32[]{:S(2)}) %collective-permute-start.27) | collective-permute-done | bytes 393248 | tf_op jit(solution)/shard_map/ppermute | solution.py:644
  288.4 35.6 %shard_map.208 = (bf16[4,528,768]{2,1,0:T(8,128)(2,1)}, f32[4,8,640]{2,1,0:T(8,128)}, f32[4,8,128]{2,1,0:T(8,128)}) custom-call(s32[4,12]{1,0:T(4,128)} %pad_add_fusion.starts_ref, s32[1]{0:T(128)} %bitcast.15.base_ref, bf16[4,528,768]{2,1,0:T(8,128)(2,1)} %bitcast.245, bf16[4,512,640]{2,1,0:T(8,128)(2,1)} %get-tuple-element.42.act_ref, ...), custom_call_target="tpu_custom_call" | custom-call | flops 1572864000 | bytes 17371136 | tf_op jit(solution)/shard_map/pallas_call | solution.py:513
  326.7 1.3 collective-permute-start.28
  328.0 9.3 %convolution_bitcast_fusion = bf16[1536,768]{0,1:T(8,128)(2,1)S(1)} fusion(bf16[4,528,1536]{2,1,0:T(8,128)(2,1)} %shard_map.203, bf16[4,528,768]{2,1,0:T(8,128)(2,1)} %get-tuple-element.59.draw_ref), kind=kOutput, calls=%fused_computation.3 | convolution fusion | flops 4982833152 | bytes 12091392 | tf_op jit(solution)/shard_map/dot_general | solution.py:25
  338.0 8.6 %shard_map.210 = bf16[4,256,1536]{2,1,0:T(8,128)(2,1)} custom-call(s32[1]{0:T(128)} %bitcast.1.place_ref, bf16[4,528,768]{2,1,0:T(8,128)(2,1)} %get-tuple-element.59.draw_ref, bf16[4,528,384]{2,1,0:T(8,128)(2,1)} %get-tuple-element.60.dgate_ref, bf16[4,16,1536]{2,1,0:T(8,128)(2,1)} %copy-done.38, bf16[1536,768]{1,0:T(8,128)(2,1)} %all-gather.4.cloned.1.call-done.conv_ref, ...), custom_call_target="tpu_custom_call" | custom-call | flops 3623878656 | bytes 11747328 | tf_op jit(solution)/shard_map/pallas_call | solution.py:513
  349.4 2.5 copy.107
  353.1 4.8 %convolution_convert_fusion.2 = bf16[1024,1536]{1,0:T(8,128)(2,1)} fusion(bf16[1024,384]{1,0:T(8,128)(2,1)S(1)} %bitcast.275, bf16[384,1536]{1,0:T(8,128)(2,1)} %bitcast.47), kind=kOutput, calls=%fused_computation.4 | convolution fusion | flops 1209532416 | bytes 5111808 | tf_op jit(solution)/shard_map/dot_general | solution.py:25
  358.7 8.7 %shard_map.209 = bf16[4,256,1536]{2,1,0:T(8,128)(2,1)} custom-call(s32[1]{0:T(128)} %bitcast.1.place_ref, bf16[4,528,768]{2,1,0:T(8,128)(2,1)} %get-tuple-element.59.draw_ref, bf16[4,528,384]{2,1,0:T(8,128)(2,1)} %get-tuple-element.60.dgate_ref, bf16[4,16,1536]{2,1,0:T(8,128)(2,1)} %copy-done.38, bf16[1536,768]{1,0:T(8,128)(2,1)} %all-gather.4.cloned.1.call-done.conv_ref, ...), custom_call_target="tpu_custom_call" | custom-call | flops 3623878656 | bytes 11747328 | tf_op jit(solution)/shard_map/pallas_call | solution.py:513
  367.4 4.2 fusion.22
  371.6 3.1 convolution_convert_fusion.3
  375.4 2.8 collective-permute-start.31
  378.9 3.3 fusion.14
  383.2 1.9 collective-permute-start.23
  385.1 6.8 %collective-permute-done.30 = bf16[256,1536]{1,0:T(8,128)(2,1)S(1)} collective-permute-done((bf16[256,1536]{1,0:T(8,128)(2,1)S(1)}, bf16[256,1536]{1,0:T(8,128)(2,1)S(1)}, u32[]{:S(2)}, u32[]{:S(2)}) %collective-permute-start.30) | collective-permute-done | bytes 786464 | tf_op jit(solution)/shard_map/ppermute | solution.py:594
  392.0 2.3 collective-permute-start.24
  396.1 3.4 all-to-all-start.4
  399.5 14.3 %collective-permute-done.31 = bf16[256,1536]{1,0:T(8,128)(2,1)} collective-permute-done((bf16[256,1536]{1,0:T(8,128)(2,1)}, bf16[256,1536]{1,0:T(8,128)(2,1)}, u32[]{:S(2)}, u32[]{:S(2)}) %collective-permute-start.31) | collective-permute-done | bytes 786464 | tf_op jit(solution)/shard_map/ppermute | solution.py:593
  413.8 2.7 fusion.5
  416.5 33.2 %all-to-all-done.4 = bf16[8,48,384]{2,1,0:T(8,128)(2,1)S(1)} async-done(((bf16[8,48,384]{2,1,0:T(8,128)(2,1)}), bf16[8,48,384]{2,1,0:T(8,128)(2,1)S(1)}, u32[]{:S(2)}, u32[]{:S(2)}) %all-to-all-start.4) | async-done | bytes 294944 | tf_op jit(solution)/shard_map/all_to_all | solution.py:666
  449.7 3.8 all-to-all-start.5
  453.5 6.0 %fusion.9 = (f32[1,256,1536]{2,1,0:T(8,128)}, bf16[1,256,1536]{2,1,0:T(8,128)(2,1)}) fusion(f32[256]{0:T(256)S(1)} %broadcast_multiply_fusion.1, f32[256]{0:T(256)S(1)} %add_rsqrt_fusion, bf16[1,256,1536]{2,1,0:T(8,128)(2,1)S(1)} %copy-done.5, bf16[1,256,1536]{2,1,0:T(8,128)(2,1)S(1)} %copy-done.1, f32[1536]{0:T(1024)S(1)} %broadcast_in_dim.83, ...), kind=kLoop, calls=%fused_computation.25 | loop fusion | flops 11403264 | bytes 11805696 | tf_op jit(solution)/shard_map/broadcast_in_dim | solution.py:1038
  461.2 2.6 all-to-all-done.5
  467.6 1.3 multiply_reduce_fusion
  (262 shorter events, 56.8 us)
Async XLA Ops:
  7.2 87.0 %all-gather.4.cloned.1.call-start = ((), (), s32[]{:S(2)}) async-start(), calls=%async_computation.8 | async-start | bytes 2949120 | tf_op jit(solution)/shard_map/all_gather | solution.py:735
  11.3 16.1 %copy-start.39 = (f32[48]{0:T(128)S(1)}, f32[48]{0:T(128)}, u32[]{:S(2)}) copy-start(f32[48]{0:T(128)} %param.21) | copy-start | bytes 580
  11.7 17.5 %copy-start.35 = (f32[48]{0:T(128)S(1)}, f32[48]{0:T(128)}, u32[]{:S(2)}) copy-start(f32[48]{0:T(128)} %param.20) | copy-start | bytes 580
  11.7 17.5 %copy-start.36 = (f32[48]{0:T(128)S(1)}, f32[48]{0:T(128)}, u32[]{:S(2)}) copy-start(f32[48]{0:T(128)} %param.19) | copy-start | bytes 580
  11.7 18.2 %copy-start = (bf16[1,256,1536]{2,1,0:T(8,128)(2,1)S(1)}, bf16[1,256,1536]{2,1,0:T(8,128)(2,1)}, u32[]{:S(2)}) copy-start(bf16[1,256,1536]{2,1,0:T(8,128)(2,1)} %param.13) | copy-start | bytes 2359300
  28.2 25.6 %copy-start.33 = (s32[1,12]{1,0:T(1,128)S(1)}, s32[1,12]{1,0:T(1,128)}, u32[]{:S(2)}) copy-start(s32[1,12]{1,0:T(1,128)} %param.14) | copy-start | bytes 148
  29.9 42.8 %collective-permute-start.3 = (bf16[256,1536]{1,0:T(8,128)(2,1)S(1)}, bf16[256,1536]{1,0:T(8,128)(2,1)S(1)}, u32[]{:S(2)}, u32[]{:S(2)}) collective-permute-start(bf16[256,1536]{1,0:T(8,128)(2,1)S(1)} %bitcast.235), channel_id=1, source_target_pairs={{0,2},{2,0},{1,3},{3,1},{4,6},{6,4},{5,7},{7,5},{8,10},{10,8},{9,1... | collective-permute-start | bytes 2359304 | tf_op jit(solution)/shard_map/ppermute | solution.py:557
  30.4 42.1 %collective-permute-start.4 = (bf16[256,1536]{1,0:T(8,128)(2,1)S(1)}, bf16[256,1536]{1,0:T(8,128)(2,1)S(1)}, u32[]{:S(2)}, u32[]{:S(2)}) collective-permute-start(bf16[256,1536]{1,0:T(8,128)(2,1)S(1)} %bitcast.236), channel_id=1, source_target_pairs={{0,6},{6,0},{2,4},{4,2},{1,7},{7,1},{3,5},{5,3},{8,14},{14,8},{10,... | collective-permute-start | bytes 2359304 | tf_op jit(solution)/shard_map/ppermute | solution.py:558
  31.9 41.3 %collective-permute-start.2 = (bf16[256,1536]{1,0:T(8,128)(2,1)S(1)}, bf16[256,1536]{1,0:T(8,128)(2,1)S(1)}, u32[]{:S(2)}, u32[]{:S(2)}) collective-permute-start(bf16[256,1536]{1,0:T(8,128)(2,1)S(1)} %bitcast.237), channel_id=1, source_target_pairs={{0,4},{4,0},{1,5},{5,1},{2,6},{6,2},{3,7},{7,3},{8,12},{12,8},{9,1... | collective-permute-start | bytes 2359304 | tf_op jit(solution)/shard_map/ppermute | solution.py:556
  33.4 48.1 %collective-permute-start.7 = (bf16[256,1536]{1,0:T(8,128)(2,1)S(1)}, bf16[256,1536]{1,0:T(8,128)(2,1)}, u32[]{:S(2)}, u32[]{:S(2)}) collective-permute-start(bf16[256,1536]{1,0:T(8,128)(2,1)S(1)} %bitcast.238), channel_id=1, source_target_pairs={{0,1},{1,0},{2,3},{3,2},{4,5},{5,4},{6,7},{7,6},{8,9},{9,8},{10,11... | collective-permute-start | bytes 2359304 | tf_op jit(solution)/shard_map/ppermute | solution.py:560
  34.5 36.1 %all-to-all-start.1 = ((bf16[8,48,384]{2,1,0:T(8,128)(2,1)}), bf16[8,48,384]{2,1,0:T(8,128)(2,1)S(1)}, u32[]{:S(2)}, u32[]{:S(2)}) async-start(bf16[8,48,384]{2,1,0:T(8,128)(2,1)} %bitcast.26), calls=%async_computation.1 | async-start | bytes 589824 | tf_op jit(solution)/shard_map/all_to_all | solution.py:666
  38.0 102.2 %all-gather.6.cloned.1.call-start = ((), (), s32[]{:S(2)}) async-start(), calls=%async_computation.10 | async-start | bytes 2949120 | tf_op jit(solution)/shard_map/all_gather | solution.py:765
  53.8 23.3 %slice-start.2 = ((f32[5,3328]{1,0:T(8,128)}), f32[5,256]{1,0:T(8,128)S(1)}, s32[]{:S(2)}) async-start(f32[5,3328]{1,0:T(8,128)} %reshape.242), calls=%async_computation.14 | async-start | bytes 16384 | tf_op jit(solution)/shard_map/slice | solution.py:747
  53.8 15.3 %collective-permute-start = (s32[1,12]{1,0:T(1,128)S(1)}, s32[1,12]{1,0:T(1,128)S(1)}, u32[]{:S(2)}, u32[]{:S(2)}) collective-permute-start(s32[1,12]{1,0:T(1,128)S(1)} %copy-done.33), channel_id=1, source_target_pairs={{0,2},{2,0},{1,3},{3,1},{4,6},{6,4},{5,7},{7,5},{8,10},{10,8},{9,1... | collective-permute-start | bytes 152 | tf_op jit(solution)/shard_map/ppermute | solution.py:613
  69.7 3.7 collective-permute-start.1
  70.7 6.4 %copy-start.28 = (f32[5,384]{1,0:T(8,128)S(1)}, f32[5,384]{1,0:T(8,128)}, u32[]{:S(2)}) copy-start(f32[5,384]{1,0:T(8,128)} %constant_dynamic-slice_fusion.1) | copy-start | bytes 23044
  72.6 9.7 %copy-start.10 = (bf16[256,1536]{1,0:T(8,128)(2,1)}, bf16[256,1536]{1,0:T(8,128)(2,1)S(1)}, u32[]{:S(2)}) copy-start(bf16[256,1536]{1,0:T(8,128)(2,1)S(1)} %collective-permute-done.4.refs_3_) | copy-start | bytes 2359300
  72.6 8.9 %collective-permute-start.10 = (bf16[256,1536]{1,0:T(8,128)(2,1)S(1)}, bf16[256,1536]{1,0:T(8,128)(2,1)S(1)}, u32[]{:S(2)}, u32[]{:S(2)}) collective-permute-start(bf16[256,1536]{1,0:T(8,128)(2,1)S(1)} %collective-permute-done.4.refs_3_), channel_id=1, source_target_pairs={{0,1},{1,0},{2,3},{3,2},{4,5},{5,4},{6,7},{7,6},{8,9},{9,8},{10,11... | collective-permute-start | bytes 2359304 | tf_op jit(solution)/shard_map/ppermute | solution.py:560
  72.7 10.3 %copy-start.9 = (bf16[256,1536]{1,0:T(8,128)(2,1)}, bf16[256,1536]{1,0:T(8,128)(2,1)S(1)}, u32[]{:S(2)}) copy-start(bf16[256,1536]{1,0:T(8,128)(2,1)S(1)} %collective-permute-done.3.refs_2_) | copy-start | bytes 2359300
  72.7 8.9 %collective-permute-start.9 = (bf16[256,1536]{1,0:T(8,128)(2,1)S(1)}, bf16[256,1536]{1,0:T(8,128)(2,1)S(1)}, u32[]{:S(2)}, u32[]{:S(2)}) collective-permute-start(bf16[256,1536]{1,0:T(8,128)(2,1)S(1)} %collective-permute-done.3.refs_2_), channel_id=1, source_target_pairs={{0,1},{1,0},{2,3},{3,2},{4,5},{5,4},{6,7},{7,6},{8,9},{9,8},{10,11... | collective-permute-start | bytes 2359304 | tf_op jit(solution)/shard_map/ppermute | solution.py:560
  73.2 9.1 %copy-start.11 = (bf16[256,1536]{1,0:T(8,128)(2,1)}, bf16[256,1536]{1,0:T(8,128)(2,1)S(1)}, u32[]{:S(2)}) copy-start(bf16[256,1536]{1,0:T(8,128)(2,1)S(1)} %collective-permute-done.2.refs_1_) | copy-start | bytes 2359300
  73.2 8.3 %collective-permute-start.8 = (bf16[256,1536]{1,0:T(8,128)(2,1)S(1)}, bf16[256,1536]{1,0:T(8,128)(2,1)S(1)}, u32[]{:S(2)}, u32[]{:S(2)}) collective-permute-start(bf16[256,1536]{1,0:T(8,128)(2,1)S(1)} %collective-permute-done.2.refs_1_), channel_id=1, source_target_pairs={{0,1},{1,0},{2,3},{3,2},{4,5},{5,4},{6,7},{7,6},{8,9},{9,8},{10,11... | collective-permute-start | bytes 2359304 | tf_op jit(solution)/shard_map/ppermute | solution.py:560
  73.4 6.1 %collective-permute-start.5 = (bf16[2,16,1536]{2,1,0:T(8,128)(2,1)S(1)}, bf16[2,16,1536]{2,1,0:T(8,128)(2,1)S(1)}, u32[]{:S(2)}, u32[]{:S(2)}) collective-permute-start(bf16[2,16,1536]{2,1,0:T(8,128)(2,1)S(1)} %pad_maximum_fusion.8), channel_id=1, source_target_pairs={{0,8},{8,16},{16,24},{1,9},{9,17},{17,25},{2,10},{10,18},{18,26},{... | collective-permute-start | bytes 294920 | tf_op jit(solution)/shard_map/ppermute | solution.py:576
  79.5 1.3 collective-permute-start.6
  83.0 7.8 %copy-start.5 = (bf16[1,256,1536]{2,1,0:T(8,128)(2,1)S(1)}, bf16[1,256,1536]{2,1,0:T(8,128)(2,1)}, u32[]{:S(2)}) copy-start(bf16[1,256,1536]{2,1,0:T(8,128)(2,1)} %param.24) | copy-start | bytes 2359300
  90.7 31.5 %collective-permute-start.14 = (bf16[256,1536]{1,0:T(8,128)(2,1)S(1)}, bf16[256,1536]{1,0:T(8,128)(2,1)S(1)}, u32[]{:S(2)}, u32[]{:S(2)}) collective-permute-start(bf16[256,1536]{1,0:T(8,128)(2,1)S(1)} %bitcast.246), channel_id=1, source_target_pairs={{0,4},{4,0},{1,5},{5,1},{2,6},{6,2},{3,7},{7,3},{8,12},{12,8},{9,1... | collective-permute-start | bytes 2359304 | tf_op jit(solution)/shard_map/ppermute | solution.py:544
  92.0 30.2 %collective-permute-start.15 = (bf16[256,1536]{1,0:T(8,128)(2,1)S(1)}, bf16[256,1536]{1,0:T(8,128)(2,1)S(1)}, u32[]{:S(2)}, u32[]{:S(2)}) collective-permute-start(bf16[256,1536]{1,0:T(8,128)(2,1)S(1)} %bitcast.247), channel_id=1, source_target_pairs={{0,2},{2,0},{1,3},{3,1},{4,6},{6,4},{5,7},{7,5},{8,10},{10,8},{9,1... | collective-permute-start | bytes 2359304 | tf_op jit(solution)/shard_map/ppermute | solution.py:543
  92.7 36.0 %collective-permute-start.16 = (bf16[256,1536]{1,0:T(8,128)(2,1)S(1)}, bf16[256,1536]{1,0:T(8,128)(2,1)S(1)}, u32[]{:S(2)}, u32[]{:S(2)}) collective-permute-start(bf16[256,1536]{1,0:T(8,128)(2,1)S(1)} %bitcast.248), channel_id=1, source_target_pairs={{0,6},{6,0},{2,4},{4,2},{1,7},{7,1},{3,5},{5,3},{8,14},{14,8},{10,... | collective-permute-start | bytes 2359304 | tf_op jit(solution)/shard_map/ppermute | solution.py:545
  94.2 9.3 %copy-start.30 = (f32[384]{0:T(512)S(1)}, f32[384]{0:T(512)}, u32[]{:S(2)}) copy-start(f32[384]{0:T(512)} %reshape.243) | copy-start | bytes 4612
  122.2 10.3 %copy-start.12 = (bf16[256,1536]{1,0:T(8,128)(2,1)}, bf16[256,1536]{1,0:T(8,128)(2,1)S(1)}, u32[]{:S(2)}) copy-start(bf16[256,1536]{1,0:T(8,128)(2,1)S(1)} %collective-permute-done.14) | copy-start | bytes 2359300
  122.3 10.3 %copy-start.14 = (bf16[256,1536]{1,0:T(8,128)(2,1)}, bf16[256,1536]{1,0:T(8,128)(2,1)S(1)}, u32[]{:S(2)}) copy-start(bf16[256,1536]{1,0:T(8,128)(2,1)S(1)} %collective-permute-done.15) | copy-start | bytes 2359300
  132.6 35.8 %collective-permute-start.17 = (bf16[4,256,1536]{2,1,0:T(8,128)(2,1)}, bf16[4,256,1536]{2,1,0:T(8,128)(2,1)}, u32[]{:S(2)}, u32[]{:S(2)}) collective-permute-start(bf16[4,256,1536]{2,1,0:T(8,128)(2,1)} %pad_maximum_fusion), channel_id=1, source_target_pairs={{0,1},{1,0},{2,3},{3,2},{4,5},{5,4},{6,7},{7,6},{8,9},{9,8},{10,11... | collective-permute-start | bytes 9437192 | tf_op jit(solution)/shard_map/ppermute | solution.py:547
  135.5 13.6 %collective-permute-start.11 = (bf16[4,128,384]{2,1,0:T(8,128)(2,1)S(1)}, bf16[4,128,384]{2,1,0:T(8,128)(2,1)S(1)}, u32[]{:S(2)}, u32[]{:S(2)}) collective-permute-start(bf16[4,128,384]{2,1,0:T(8,128)(2,1)S(1)} %add_convert_fusion.8), channel_id=1, source_target_pairs={{0,8},{1,9},{2,10},{3,11},{4,12},{5,13},{6,14},{7,15}} | collective-permute-start | bytes 1179656 | tf_op jit(solution)/shard_map/ppermute | solution.py:644
  142.5 20.2 %all-to-all-start.2 = ((bf16[4,96,1536]{2,1,0:T(8,128)(2,1)}), bf16[4,96,1536]{2,1,0:T(8,128)(2,1)}, u32[]{:S(2)}, u32[]{:S(2)}) async-start(bf16[4,96,1536]{2,1,0:T(8,128)(2,1)} %slice.334), calls=%async_computation.2 | async-start | bytes 2359296 | tf_op jit(solution)/shard_map/all_to_all | solution.py:666
  148.4 9.3 %copy-start.8 = (bf16[4,4,96,384]{3,2,1,0:T(8,128)(2,1)}, bf16[4,4,96,384]{3,2,1,0:T(8,128)(2,1)S(1)}, u32[]{:S(2)}) copy-start(bf16[4,4,96,384]{3,2,1,0:T(8,128)(2,1)S(1)} %pad_maximum_fusion.4) | copy-start | bytes 3538948
  149.2 8.5 %collective-permute-start.12 = (bf16[4,128,384]{2,1,0:T(8,128)(2,1)S(1)}, bf16[4,128,384]{2,1,0:T(8,128)(2,1)S(1)}, u32[]{:S(2)}, u32[]{:S(2)}) collective-permute-start(bf16[4,128,384]{2,1,0:T(8,128)(2,1)S(1)} %add_convert_fusion.7), channel_id=1, source_target_pairs={{8,16},{9,17},{10,18},{11,19},{12,20},{13,21},{14,22},{15,23}} | collective-permute-start | bytes 1179656 | tf_op jit(solution)/shard_map/ppermute | solution.py:644
  157.9 9.7 %collective-permute-start.13 = (bf16[4,128,384]{2,1,0:T(8,128)(2,1)S(1)}, bf16[4,128,384]{2,1,0:T(8,128)(2,1)S(1)}, u32[]{:S(2)}, u32[]{:S(2)}) collective-permute-start(bf16[4,128,384]{2,1,0:T(8,128)(2,1)S(1)} %add_convert_fusion.6), channel_id=1, source_target_pairs={{16,24},{17,25},{18,26},{19,27},{20,28},{21,29},{22,30},{23,31}} | collective-permute-start | bytes 1179656 | tf_op jit(solution)/shard_map/ppermute | solution.py:644
  184.1 1.3 collective-permute-start.18
  186.3 4.3 collective-permute-start.19
  190.6 4.3 collective-permute-start.20
  212.7 23.6 %all-to-all-start.3 = ((bf16[4,96,1536]{2,1,0:T(8,128)(2,1)}), bf16[4,96,1536]{2,1,0:T(8,128)(2,1)S(1)}, u32[]{:S(2)}, u32[]{:S(2)}) async-start(bf16[4,96,1536]{2,1,0:T(8,128)(2,1)} %bitcast.77), calls=%async_computation.3 | async-start | bytes 2359296 | tf_op jit(solution)/shard_map/all_to_all | solution.py:666
  216.3 178.0 %reduce-scatter.5.cloned.1.call-start = ((), (), s32[]{:S(2)}) async-start(), calls=%async_computation.9 | async-start | bytes 2949120 | tf_op jit(solution)/shard_map/reduce_scatter | solution.py:921
  216.3 8.2 %copy-start.3 = (f32[4,128,384]{2,1,0:T(8,128)S(1)}, f32[4,128,384]{2,1,0:T(8,128)}, u32[]{:S(2)}) copy-start(f32[4,128,384]{2,1,0:T(8,128)} %get-tuple-element.58) | copy-start | bytes 2359300
  216.3 8.2 %copy-start.27 = (f32[4,384]{1,0:T(4,128)S(1)}, f32[4,384]{1,0:T(4,128)}, u32[]{:S(2)}) copy-start(f32[4,384]{1,0:T(4,128)} %copy-done.26) | copy-start | bytes 18436
  224.6 6.2 %collective-permute-start.25 = (bf16[4,128,384]{2,1,0:T(8,128)(2,1)S(1)}, bf16[4,128,384]{2,1,0:T(8,128)(2,1)S(1)}, u32[]{:S(2)}, u32[]{:S(2)}) collective-permute-start(bf16[4,128,384]{2,1,0:T(8,128)(2,1)S(1)} %add_convert_fusion.5), channel_id=1, source_target_pairs={{24,16},{25,17},{26,18},{27,19},{28,20},{29,21},{30,22},{31,23}} | collective-permute-start | bytes 1179656 | tf_op jit(solution)/shard_map/ppermute | solution.py:644
  231.7 7.4 %collective-permute-start.26 = (bf16[4,128,384]{2,1,0:T(8,128)(2,1)}, bf16[4,128,384]{2,1,0:T(8,128)(2,1)S(1)}, u32[]{:S(2)}, u32[]{:S(2)}) collective-permute-start(bf16[4,128,384]{2,1,0:T(8,128)(2,1)} %add_convert_fusion.4), channel_id=1, source_target_pairs={{16,8},{17,9},{18,10},{19,11},{20,12},{21,13},{22,14},{23,15}} | collective-permute-start | bytes 1179656 | tf_op jit(solution)/shard_map/ppermute | solution.py:644
  239.0 210.7 %reduce-scatter.7.cloned.1.call-start = ((), (), s32[]{:S(2)}) async-start(), calls=%async_computation.11 | async-start | bytes 2949120 | tf_op jit(solution)/shard_map/reduce_scatter | solution.py:985
  239.3 48.3 %collective-permute-start.27 = (bf16[4,128,384]{2,1,0:T(8,128)(2,1)S(1)}, bf16[4,128,384]{2,1,0:T(8,128)(2,1)S(1)}, u32[]{:S(2)}, u32[]{:S(2)}) collective-permute-start(bf16[4,128,384]{2,1,0:T(8,128)(2,1)S(1)} %add_convert_fusion.3), channel_id=1, source_target_pairs={{8,0},{9,1},{10,2},{11,3},{12,4},{13,5},{14,6},{15,7}} | collective-permute-start | bytes 1179656 | tf_op jit(solution)/shard_map/ppermute | solution.py:644
  288.4 37.5 %copy-start.7 = (bf16[1536,768]{1,0:T(8,128)(2,1)S(1)}, bf16[1536,768]{1,0:T(8,128)(2,1)}, u32[]{:S(2)}) copy-start(bf16[1536,768]{1,0:T(8,128)(2,1)} %all-gather.4.cloned.1.call-done.conv_ref) | copy-start | bytes 7077892
  326.7 10.6 %collective-permute-start.28 = (bf16[4,16,1536]{2,1,0:T(8,128)(2,1)S(1)}, bf16[4,16,1536]{2,1,0:T(8,128)(2,1)S(1)}, u32[]{:S(2)}, u32[]{:S(2)}) collective-permute-start(bf16[4,16,1536]{2,1,0:T(8,128)(2,1)S(1)} %bitcast.290), channel_id=1, source_target_pairs={{8,0},{16,8},{24,16},{9,1},{17,9},{25,17},{10,2},{18,10},{26,18},{... | collective-permute-start | bytes 589832 | tf_op jit(solution)/shard_map/ppermute | solution.py:949
  337.3 9.5 %copy-start.29 = (f32[4,8,128]{2,1,0:T(8,128)S(1)}, f32[4,8,128]{2,1,0:T(8,128)}, u32[]{:S(2)}) copy-start(f32[4,8,128]{2,1,0:T(8,128)} %get-tuple-element.64) | copy-start | bytes 49156
  337.3 9.5 %copy-start.32 = (bf16[6]{0:T(256)(128)(2,1)S(1)}, bf16[6]{0:T(256)(128)(2,1)}, u32[]{:S(2)}) copy-start(bf16[6]{0:T(256)(128)(2,1)} %reduce_sum.77) | copy-start | bytes 40
  346.6 20.7 %collective-permute-start.29 = (bf16[4,256,1536]{2,1,0:T(8,128)(2,1)}, bf16[4,256,1536]{2,1,0:T(8,128)(2,1)}, u32[]{:S(2)}, u32[]{:S(2)}) collective-permute-start(bf16[4,256,1536]{2,1,0:T(8,128)(2,1)} %shard_map.210), channel_id=1, source_target_pairs={{0,1},{1,0},{2,3},{3,2},{4,5},{5,4},{6,7},{7,6},{8,9},{9,8},{10,11... | collective-permute-start | bytes 9437192 | tf_op jit(solution)/shard_map/ppermute | solution.py:587
  357.8 21.0 %collective-permute-start.21 = (bf16[4,256,1536]{2,1,0:T(8,128)(2,1)}, bf16[4,256,1536]{2,1,0:T(8,128)(2,1)}, u32[]{:S(2)}, u32[]{:S(2)}) collective-permute-start(bf16[4,256,1536]{2,1,0:T(8,128)(2,1)} %bitcast.56), channel_id=1, source_target_pairs={{0,1},{1,0},{2,3},{3,2},{4,5},{5,4},{6,7},{7,6},{8,9},{9,8},{10,11... | collective-permute-start | bytes 9437192 | tf_op jit(solution)/shard_map/ppermute | solution.py:587
  371.5 20.4 %collective-permute-start.30 = (bf16[256,1536]{1,0:T(8,128)(2,1)S(1)}, bf16[256,1536]{1,0:T(8,128)(2,1)S(1)}, u32[]{:S(2)}, u32[]{:S(2)}) collective-permute-start(bf16[256,1536]{1,0:T(8,128)(2,1)S(1)} %get-tuple-element.67), channel_id=1, source_target_pairs={{0,2},{2,0},{1,3},{3,1},{4,6},{6,4},{5,7},{7,5},{8,10},{10,8},{9,1... | collective-permute-start | bytes 2359304 | tf_op jit(solution)/shard_map/ppermute | solution.py:594
  374.7 7.5 %copy-start.4 = (bf16[1024,1536]{1,0:T(8,128)(2,1)}, bf16[1024,1536]{1,0:T(8,128)(2,1)S(1)}, u32[]{:S(2)}) copy-start(bf16[1024,1536]{1,0:T(8,128)(2,1)S(1)} %convolution_convert_fusion.3) | copy-start | bytes 9437188
  375.4 38.4 %collective-permute-start.31 = (bf16[256,1536]{1,0:T(8,128)(2,1)}, bf16[256,1536]{1,0:T(8,128)(2,1)}, u32[]{:S(2)}, u32[]{:S(2)}) collective-permute-start(bf16[256,1536]{1,0:T(8,128)(2,1)} %get-tuple-element.69), channel_id=1, source_target_pairs={{0,4},{4,0},{1,5},{5,1},{2,6},{6,2},{3,7},{7,3},{8,12},{12,8},{9,1... | collective-permute-start | bytes 2359304 | tf_op jit(solution)/shard_map/ppermute | solution.py:593
  378.3 35.6 %collective-permute-start.32 = (bf16[256,1536]{1,0:T(8,128)(2,1)}, bf16[256,1536]{1,0:T(8,128)(2,1)}, u32[]{:S(2)}, u32[]{:S(2)}) collective-permute-start(bf16[256,1536]{1,0:T(8,128)(2,1)} %get-tuple-element.68), channel_id=1, source_target_pairs={{0,6},{6,0},{2,4},{4,2},{1,7},{7,1},{3,5},{5,3},{8,14},{14,8},{10,... | collective-permute-start | bytes 2359304 | tf_op jit(solution)/shard_map/ppermute | solution.py:595
  382.2 71.2 %collective-permute-start.22 = (bf16[256,1536]{1,0:T(8,128)(2,1)}, bf16[256,1536]{1,0:T(8,128)(2,1)}, u32[]{:S(2)}, u32[]{:S(2)}) collective-permute-start(bf16[256,1536]{1,0:T(8,128)(2,1)} %get-tuple-element.70), channel_id=1, source_target_pairs={{0,2},{2,0},{1,3},{3,1},{4,6},{6,4},{5,7},{7,5},{8,10},{10,8},{9,1... | collective-permute-start | bytes 2359304 | tf_op jit(solution)/shard_map/ppermute | solution.py:594
  383.2 70.3 %collective-permute-start.23 = (bf16[256,1536]{1,0:T(8,128)(2,1)}, bf16[256,1536]{1,0:T(8,128)(2,1)}, u32[]{:S(2)}, u32[]{:S(2)}) collective-permute-start(bf16[256,1536]{1,0:T(8,128)(2,1)} %get-tuple-element.72), channel_id=1, source_target_pairs={{0,4},{4,0},{1,5},{5,1},{2,6},{6,2},{3,7},{7,3},{8,12},{12,8},{9,1... | collective-permute-start | bytes 2359304 | tf_op jit(solution)/shard_map/ppermute | solution.py:593
  392.0 61.5 %collective-permute-start.24 = (bf16[256,1536]{1,0:T(8,128)(2,1)}, bf16[256,1536]{1,0:T(8,128)(2,1)}, u32[]{:S(2)}, u32[]{:S(2)}) collective-permute-start(bf16[256,1536]{1,0:T(8,128)(2,1)} %get-tuple-element.71), channel_id=1, source_target_pairs={{0,6},{6,0},{2,4},{4,2},{1,7},{7,1},{3,5},{5,3},{8,14},{14,8},{10,... | collective-permute-start | bytes 2359304 | tf_op jit(solution)/shard_map/ppermute | solution.py:595
  396.1 53.6 %all-to-all-start.4 = ((bf16[8,48,384]{2,1,0:T(8,128)(2,1)}), bf16[8,48,384]{2,1,0:T(8,128)(2,1)S(1)}, u32[]{:S(2)}, u32[]{:S(2)}) async-start(bf16[8,48,384]{2,1,0:T(8,128)(2,1)} %bitcast.83), calls=%async_computation.5 | async-start | bytes 589824 | tf_op jit(solution)/shard_map/all_to_all | solution.py:666
  449.7 14.1 %all-to-all-start.5 = ((bf16[8,48,768]{2,1,0:T(8,128)(2,1)}), bf16[8,48,768]{2,1,0:T(8,128)(2,1)S(1)}, u32[]{:S(2)}, u32[]{:S(2)}) async-start(bf16[8,48,768]{2,1,0:T(8,128)(2,1)} %bitcast.277), calls=%async_computation.6 | async-start | bytes 1179648 | tf_op jit(solution)/shard_map/all_to_all | solution.py:666
  453.5 6.0 %copy-start.23 = (bf16[1,192,1536]{2,1,0:T(8,128)(2,1)S(1)}, bf16[1,192,1536]{2,1,0:T(8,128)(2,1)}, u32[]{:S(2)}) copy-start(bf16[1,192,1536]{2,1,0:T(8,128)(2,1)} %reduce-scatter.5.cloned.1.call-done) | copy-start | bytes 1769476
  (21 other events, 57.3 us)
Sparse Core Ops, SparseCore 0:
  27.5 50.3 all-gather.3
  80.1 48.7 all-gather.5
  239.1 64.9 reduce-scatter.4
  352.1 48.0 reduce-scatter.6

commit v2 on v1

--- a/solution.py
+++ b/solution.py
@@ -10,7 +10,6 @@
 
 f32 = jnp.float32
 bf16 = jnp.bfloat16
-highest = lax.Precision.HIGHEST
 epsilon = 1e-05
 HALO = 16
 LANES = 128
@@ -61,22 +60,27 @@
 def head_sum(wide):
     rows = wide.shape[1]
     half = LANES // 2
-    pick = (iota((rows, LANES), 0) // half == iota((rows, LANES), 1)).astype(f32)
-    return dot(wide, pick, precision=highest)
-
-
-def lower_triangle(q):
-    return iota((q, q), 0) >= iota((q, q), 1)
-
-
-def conv_group(raw_ref, cw_ref, seg, c, q, g):
+    pick = (iota((rows, LANES), 0) // half == iota((rows, LANES), 1)).astype(bf16)
+    return dot(wide.astype(bf16), pick)
+
+
+def exact_dot(ones, values):
+    total = 0.0
+    for _ in range(3):
+        term = values.astype(bf16)
+        total = total + dot(ones, term)
+        values = values - term.astype(f32)
+    return total
+
+
+def conv_group(raw_ref, cw_ref, win_ref, near, c, q, g):
     lanes = slice(g * LANES, (g + 1) * LANES)
-    window = raw_ref[0, c * q : c * q + q + HALO, lanes].astype(f32)
+    win_ref[g] = raw_ref[0, c * q : c * q + q + HALO, lanes].astype(f32)
     taps = cw_ref[:, lanes]
-    out = taps[4:5] + taps[3:4] * window[HALO:]
+    out = taps[4:5] + taps[3:4] * win_ref[g, HALO : HALO + q]
     for k in range(1, 4):
-        near = seg[HALO:] == seg[HALO - k : HALO - k + q]
-        out = out + taps[3 - k : 4 - k] * jnp.where(near, window[HALO - k : HALO - k + q], 0.0)
+        shifted = win_ref[g, HALO - k : HALO - k + q]
+        out = out + taps[3 - k : 4 - k] * jnp.where(near[k - 1], shifted, 0.0)
     return out
 
 
@@ -95,6 +99,7 @@
     hp_ref,
     skip_ref,
     act_ref,
+    slope_ref,
     y_ref,
     ent_ref,
     step_ref,
@@ -102,6 +107,7 @@
     cumr_ref,
     state_ref,
     decay_ref,
+    win_ref,
     *,
     heads,
     q,
@@ -110,8 +116,7 @@
     length = y_ref.shape[1]
     pairs = heads // 2
     wide = pairs * LANES
-    tri = lower_triangle(q)
-    tri_f = tri.astype(f32)
+    lower = (iota((q, q), 0) >= iota((q, q), 1)).astype(bf16)
     state = None
     block = None
     for c in range(length // q):
@@ -119,23 +124,32 @@
         seg, seg_r = chunk_segments(starts_ref, base_ref, n, c, q)
         own = seg[HALO:]
         prev = seg[HALO - 1 : HALO]
+        near = [own == seg[HALO - k : HALO - k + q] for k in range(1, 4)]
         act = []
         for g in range(pairs + 2):
-            z = conv_group(raw_ref, cw_ref, seg, c, q, g)
-            a = z * sigmoid(z)
-            act_ref[0, rows, g * LANES : (g + 1) * LANES] = a.astype(bf16)
+            lanes = slice(g * LANES, (g + 1) * LANES)
+            z = conv_group(raw_ref, cw_ref, win_ref, near, c, q, g)
+            sg = sigmoid(z)
+            a = z * sg
+            act_ref[0, rows, lanes] = a.astype(bf16)
+            slope_ref[0, rows, lanes] = (sg + a * (1.0 - sg)).astype(bf16)
             act.append(a)
         b_low, c_low = act[pairs].astype(bf16), act[pairs + 1].astype(bf16)
         dt_raw = raw_ref[0, HALO + c * q : HALO + (c + 1) * q, wide + 2 * LANES :].astype(f32)
         used = iota((1, LANES), 1) < heads
         step = jnp.where(used, softplus(dt_raw + hp_ref[0:1]), 0.0)
-        cum = dot(tri_f, hp_ref[1:2] * step, precision=highest)
+        cum = exact_dot(lower, hp_ref[1:2] * step)
         cum_r = cum.T
         step_ref[0, rows] = step
         cum_ref[0, rows] = cum
         cumr_ref[0, :, rows] = cum_r[:8]
-        same = tri & (own[:, :1] == seg_r[:1])
         scores = dot(c_low, b_low, 1, 1)
+        parts = []
+        for top, end in ((0, q),):
+            at = slice(top, end)
+            causal = iota((q, end), 0) >= iota((q, end), 1)
+            same = causal & (own[at, :1] == seg_r[:1, :end])
+            parts.append((at, end, jnp.where(same, 0.0, MASKED)))
         last = cum[q - 1 : q]
         ent = jnp.where(own == prev, jnp.exp(cum), 0.0)
         tail = jnp.where(own == own[q - 1 : q], jnp.exp(last - cum), 0.0) * step
@@ -146,12 +160,19 @@
         for j in range(pairs):
             lanes = slice(j * LANES, (j + 1) * LANES)
             scaled = act[j] * pair_lanes(step, j)
-            out = skip_ref[0:1, lanes] * act[j]
-            for half in range(2):
-                h = 2 * j + half
-                mixing = jnp.exp(jnp.where(same, cum[:, h : h + 1] - cum_r[h : h + 1], MASKED)) * scores
-                part = jnp.where(low_half() == (half == 0), scaled, 0.0)
-                out = out + dot(mixing.astype(bf16), part.astype(bf16))
+            halves = [
+                jnp.where(low_half() == (half == 0), scaled, 0.0).astype(bf16) for half in range(2)
+            ]
+            within = []
+            for at, end, bias in parts:
+                mixing = []
+                for half in range(2):
+                    h = 2 * j + half
+                    decays = jnp.exp(cum[at, h : h + 1] - cum_r[h : h + 1, :end] + bias)
+                    mixing.append((decays * scores[at, :end]).astype(bf16))
+                out = dot(jnp.concatenate(mixing, axis=1), jnp.concatenate(halves, axis=0))
+                within.append(out)
+            out = skip_ref[0:1, lanes] * act[j] + jnp.concatenate(within, axis=0)
             if c:
                 out = out + pair_lanes(ent, j) * dot(c_low, state_low[:, lanes])
             y_ref[0, rows, lanes] = out.astype(bf16)
@@ -314,45 +335,57 @@
     n = pl.program_id(0)
     pairs = heads // 2
     wide = pairs * LANES
-    tri = lower_triangle(q)
-    for c in range(dy_ref.shape[1] // q):
-        rows = slice(c * q, (c + 1) * q)
-        first = base_ref[0] + c * q
-        seg = segment(starts_ref, n, first + iota((q, LANES), 0))
-        seg_r = segment(starts_ref, n, first + iota((8, q), 1))
-        same = tri & (seg[:, :1] == seg_r[:1])
-        b_low = act_ref[0, rows, wide : wide + LANES]
-        c_low = act_ref[0, rows, wide + LANES : wide + 2 * LANES]
-        scores = dot(c_low, b_low, 1, 1)
-        step = step_ref[0, rows]
-        cum = cum_ref[0, rows]
-        cum_r = cumr_ref[0, :, rows]
-        dscores = jnp.zeros((q, q), f32)
-        lane = iota((q, LANES), 1)
-        gain_t = jnp.zeros((q, LANES), f32)
-        lost = []
-        for j in range(pairs):
-            lanes = slice(j * LANES, (j + 1) * LANES)
-            scaled = (act_ref[0, rows, lanes].astype(f32) * pair_lanes(step, j)).astype(bf16)
-            dy = dy_ref[0, rows, lanes].astype(f32)
-            out = jnp.zeros((q, LANES), f32)
-            for half in range(2):
-                h = 2 * j + half
-                decays = jnp.exp(jnp.where(same, cum[:, h : h + 1] - cum_r[h : h + 1], MASKED))
-                mixing = decays * scores
-                part = jnp.where(low_half() == (half == 0), dy, 0.0).astype(bf16)
-                dmix = dot(part, scaled, 1, 1) * decays
-                dscores = dscores + dmix
-                flow = dmix * scores
-                gain_t = jnp.where(lane == h, jnp.sum(flow, axis=1, keepdims=True), gain_t)
-                lost.append(jnp.sum(flow, axis=0, keepdims=True))
-                out = out + dot(mixing.astype(bf16), part, 0, 0)
-            dscaled_ref[0, rows, lanes] = out.astype(bf16)
-        lost = jnp.concatenate(lost + [jnp.zeros((LANES - heads, q), f32)], axis=0)
-        dcum_ref[0, rows] = gain_t - lost.T
-        dlow = dscores.astype(bf16)
-        dbc_ref[0, rows, :LANES] = dot(dlow, c_low, 0, 0).astype(bf16)
-        dbc_ref[0, rows, LANES:] = dot(dlow, b_low).astype(bf16)
+    rows = slice(0, q)
+    first = base_ref[0] + pl.program_id(1) * q
+    seg = segment(starts_ref, n, first + iota((q, LANES), 0))
+    seg_r = segment(starts_ref, n, first + iota((8, q), 1))
+    b_low = act_ref[0, rows, wide : wide + LANES]
+    c_low = act_ref[0, rows, wide + LANES : wide + 2 * LANES]
+    scores = dot(b_low, c_low, 1, 1)
+    step = step_ref[0, rows]
+    cum = cum_ref[0, rows]
+    cum_r = cumr_ref[0, :, rows]
+    parts = []
+    for top in (0,):
+        at = slice(top, top + q)
+        shape = (q, q - top)
+        causal = iota(shape, 0) <= iota(shape, 1)
+        same = causal & (seg[at, :1] == seg_r[:1, top:])
+        parts.append((at, top, jnp.where(same, 0.0, MASKED)))
+    dscores = [jnp.zeros((q, q), f32)]
+    lane = iota((q, LANES), 1)
+    lost = [jnp.zeros((q, LANES), f32)]
+    gains = []
+    for j in range(pairs):
+        lanes = slice(j * LANES, (j + 1) * LANES)
+        scaled = (act_ref[0, rows, lanes].astype(f32) * pair_lanes(step, j)).astype(bf16)
+        dy = dy_ref[0, rows, lanes]
+        mixing = []
+        both = jnp.concatenate(
+            [jnp.where(low_half() == (half == 0), dy, jnp.zeros_like(dy)) for half in range(2)],
+            axis=0,
+        )
+        dboth = dot(scaled, both, 1, 1)
+        for half in range(2):
+            h = 2 * j + half
+            gain = []
+            for i, (at, top, bias) in enumerate(parts):
+                decays = jnp.exp(cum_r[h : h + 1, top:] - cum[at, h : h + 1] + bias)
+                dmix = dboth[:, half * q : (half + 1) * q] * decays
+                dscores[i] = dscores[i] + dmix
+                flow = dmix * scores[at, top:]
+                lost[i] = jnp.where(lane == h, jnp.sum(flow, axis=1, keepdims=True), lost[i])
+                gain.append(jnp.sum(flow, axis=0, keepdims=True))
+                mixing.append((decays * scores[at, top:]).astype(bf16))
+            gains.append(gain[0])
+        dscaled_ref[0, rows, lanes] = dot(
+            jnp.concatenate(mixing, axis=1), both
+        ).astype(bf16)
+    gains = jnp.concatenate(gains + [jnp.zeros((LANES - heads, q), f32)], axis=0)
+    dcum_ref[0, rows] = gains.T - jnp.concatenate(lost, axis=0)
+    low = dscores[0].astype(bf16)
+    dbc_ref[0, rows, :LANES] = dot(low, c_low).astype(bf16)
+    dbc_ref[0, rows, LANES:] = dot(low, b_low, 0, 0).astype(bf16)
 
 
 def scan_backward_outer(
@@ -360,6 +393,7 @@
     base_ref,
     raw_ref,
     act_ref,
+    slope_ref,
     dy_ref,
     step_ref,
     cum_ref,
@@ -384,7 +418,7 @@
     chunks = length // q
     pairs = heads // 2
     wide = pairs * LANES
-    tri_f = lower_triangle(q).astype(f32)
+    upper = (iota((q, q), 0) <= iota((q, q), 1)).astype(bf16)
     used = iota((1, LANES), 1) < heads
     groups = pairs + 2
 
@@ -399,7 +433,7 @@
         ent = jnp.where(own == prev, jnp.exp(cum), 0.0)
         fade = jnp.where(own == own[q - 1 : q], jnp.exp(last - cum), 0.0)
         decay = jnp.where(own[q - 1 : q] == prev, jnp.exp(last), 0.0)
-        prepared.append((seg, ent, fade, decay, state))
+        prepared.append((ent, fade, decay, state))
         if c + 1 < chunks:
             tail = fade * step_ref[0, rows]
             b_low = act_ref[0, rows, wide : wide + LANES]
@@ -417,15 +451,15 @@
             ]
             state = expand(decay, pairs) * state + jnp.concatenate(gained, axis=1)
 
-    dconv_ref[0] = jnp.zeros(dconv_ref.shape[1:], f32)
     dhead_ref[0] = jnp.zeros(dhead_ref.shape[1:], f32)
-    dz_ref[:HALO] = jnp.zeros((HALO, groups * LANES), f32)
-    dz_ref[HALO + length :] = jnp.zeros((8, groups * LANES), f32)
+    dz_ref[:, :HALO] = jnp.zeros((groups, HALO, LANES), f32)
+    dz_ref[:, HALO + length :] = jnp.zeros((groups, 8, LANES), f32)
     draw_ref[0, :HALO, groups * LANES :] = jnp.zeros((HALO, LANES), bf16)
     grad = leave_ref[0].astype(f32)
     for c in reversed(range(chunks)):
         rows = slice(c * q, (c + 1) * q)
-        seg, ent, fade, decay, state = prepared[c]
+        at = slice(HALO + c * q, HALO + (c + 1) * q)
+        ent, fade, decay, state = prepared[c]
         step = step_ref[0, rows]
         tail = fade * step
         b_low = act_ref[0, rows, wide : wide + LANES]
@@ -434,7 +468,6 @@
         grad_low = grad.astype(bf16)
         db = dbc_ref[0, rows, :LANES].astype(f32)
         dc = dbc_ref[0, rows, LANES:].astype(f32)
-        dx = []
         by_step, by_tail, by_ent, next_grad = [], [], [], []
         for j in range(pairs):
             lanes = slice(j * LANES, (j + 1) * LANES)
@@ -444,58 +477,54 @@
             dweighted = dot(b_low, grad_low[:, lanes])
             wide_tail = pair_lanes(tail, j)
             entered = (dy * pair_lanes(ent, j)).astype(bf16)
-            dx.append(
-                dscaled * pair_lanes(step, j) + skip_ref[0:1, lanes] * dy + dweighted * wide_tail
-            )
-            by_step.append(dscaled * x)
-            by_tail.append(dweighted * x)
-            by_ent.append(dy * dot(c_low, state_low[:, lanes]))
+            dx = dscaled * pair_lanes(step, j) + skip_ref[0:1, lanes] * dy + dweighted * wide_tail
+            dz_ref[j, at] = dx * slope_ref[0, rows, lanes].astype(f32)
+            by_step.append((dscaled * x).astype(bf16))
+            by_tail.append((dweighted * x).astype(bf16))
+            by_ent.append((dy * dot(c_low, state_low[:, lanes])).astype(bf16))
             db = db + dot((x * wide_tail).astype(bf16), grad_low[:, lanes], 1, 1)
             dc = dc + dot(entered, state_low[:, lanes], 1, 1)
             next_grad.append(dot(c_low, entered, 0, 0))
+        dz_ref[pairs, at] = db * slope_ref[0, rows, wide : wide + LANES].astype(f32)
+        dz_ref[pairs + 1, at] = dc * slope_ref[0, rows, wide + LANES : wide + 2 * LANES].astype(f32)
         dtail = head_sum(jnp.concatenate(by_tail, axis=1))
         dent = head_sum(jnp.concatenate(by_ent, axis=1))
         moved = dtail * tail
-        ddecay = head_sum(jnp.sum(grad * state, axis=0, keepdims=True))
+        ddecay = head_sum(
+            jnp.broadcast_to(jnp.sum(grad * state, axis=0, keepdims=True), (8, wide))
+        )[:1]
         at_last = jnp.sum(moved, axis=0, keepdims=True) + ddecay * decay
         dcum = dcum_ref[0, rows] + dent * ent - moved
         dcum = dcum + jnp.where(iota((q, LANES), 0) == q - 1, at_last, 0.0)
-        drates = dot(tri_f, dcum, 0, 0, precision=highest)
+        drates = exact_dot(upper, dcum)
         rate = hp_ref[1:2]
         dstep = head_sum(jnp.concatenate(by_step, axis=1)) + dtail * fade + drates * rate
-        dt_raw = raw_ref[0, HALO + c * q : HALO + (c + 1) * q, groups * LANES :].astype(f32)
+        dt_raw = raw_ref[0, at, groups * LANES :].astype(f32)
         ddt = jnp.where(used, dstep * sigmoid(dt_raw + hp_ref[0:1]), 0.0)
-        draw_ref[0, HALO + c * q : HALO + (c + 1) * q, groups * LANES :] = ddt.astype(bf16)
+        draw_ref[0, at, groups * LANES :] = ddt.astype(bf16)
         dhead_ref[0, 0:1] += jnp.sum(ddt, axis=0, keepdims=True)
         dhead_ref[0, 1:2] += jnp.sum(
             jnp.where(used, drates * (rate * step), 0.0), axis=0, keepdims=True
         )
         grad = expand(decay, pairs) * grad + jnp.concatenate(next_grad, axis=1)
-        for g in range(groups):
-            lanes = slice(g * LANES, (g + 1) * LANES)
-            z = conv_group(raw_ref, cw_ref, seg, c, q, g)
-            sg = sigmoid(z)
-            dact = dx[g] if g < pairs else (db, dc)[g - pairs]
-            dz = dact * (sg * (1.0 + z * (1.0 - sg)))
-            dz_ref[HALO + c * q : HALO + (c + 1) * q, lanes] = dz
-            window = raw_ref[0, c * q : c * q + q + HALO, lanes].astype(f32)
-            dconv_ref[0, 4:5, lanes] += jnp.sum(dz, axis=0, keepdims=True)
-            dconv_ref[0, 3:4, lanes] += jnp.sum(dz * window[HALO:], axis=0, keepdims=True)
-            for k in range(1, 4):
-                near = seg[HALO:] == seg[HALO - k : HALO - k + q]
-                source = jnp.where(near, window[HALO - k : HALO - k + q], 0.0)
-                dconv_ref[0, 3 - k : 4 - k, lanes] += jnp.sum(dz * source, axis=0, keepdims=True)
-
-    places = base_ref[0] - HALO + iota((HALO + length + 8, LANES), 0)
+
+    total = HALO + length
+    places = base_ref[0] - HALO + iota((total + 8, LANES), 0)
     seg = segment(starts_ref, n, places)
-    total = HALO + length
+    near = [seg[k : k + total] == seg[:total] for k in range(1, 4)]
+    dconv_ref[0, 5:] = jnp.zeros((3, groups * LANES), f32)
     for g in range(groups):
         lanes = slice(g * LANES, (g + 1) * LANES)
         taps = cw_ref[:, lanes]
-        out = taps[3:4] * dz_ref[:total, lanes]
+        raw = raw_ref[0, :, lanes].astype(f32)
+        dz = dz_ref[g, :total]
+        out = taps[3:4] * dz
+        dconv_ref[0, 4:5, lanes] = jnp.sum(dz, axis=0, keepdims=True)
+        dconv_ref[0, 3:4, lanes] = jnp.sum(dz * raw, axis=0, keepdims=True)
         for k in range(1, 4):
-            near = seg[k : k + total] == seg[:total]
-            out = out + taps[3 - k : 4 - k] * jnp.where(near, dz_ref[k : k + total, lanes], 0.0)
+            shifted = jnp.where(near[k - 1], dz_ref[g, k : k + total], 0.0)
+            out = out + taps[3 - k : 4 - k] * shifted
+            dconv_ref[0, 3 - k : 4 - k, lanes] = jnp.sum(shifted * raw, axis=0, keepdims=True)
         draw_ref[0, :, lanes] = out.astype(bf16)
 
 
@@ -594,6 +623,34 @@
     across = lax.ppermute(piece(2).astype(bf16), "bx", SWAP)
     corner = lax.ppermute(piece(3).astype(bf16), ("lo", "bx"), CROSS)
     return piece(0) + across.astype(f32) + beside.astype(f32) + corner.astype(f32)
+
+
+def scatter_halves(make):
+    if not is_small():
+        return scatter_pieces(make)
+    other = make(2, 2)
+    came = lax.ppermute(other, "core", SWAP)
+    own = make(0, 2)
+    middle = own.shape[2] // 2
+    left, right = slice(0, middle), slice(middle, 2 * middle)
+
+    def piece(i, half):
+        return own[i, :, half].astype(f32) + came[i, :, half].astype(f32)
+
+    def pair(i, j, half):
+        return jnp.stack([piece(i, half), piece(j, half)]).astype(bf16)
+
+    by_x = lax.ppermute(pair(2, 3, left), "bx", SWAP)
+    by_y = lax.ppermute(pair(1, 3, right), "lo", SWAP)
+    last_y = lax.ppermute((piece(1, left) + by_x[1].astype(f32)).astype(bf16), "lo", SWAP)
+    last_x = lax.ppermute((piece(2, right) + by_y[1].astype(f32)).astype(bf16), "bx", SWAP)
+    return jnp.concatenate(
+        [
+            piece(0, left) + by_x[0].astype(f32) + last_y.astype(f32),
+            piece(0, right) + by_y[0].astype(f32) + last_x.astype(f32),
+        ],
+        axis=1,
+    )
 
 
 def sum_plane(stats):
@@ -783,11 +840,12 @@
     row_shape = (sequences, 8, length)
     state_shape = (sequences, shared_width // 2, width)
     unit = sequences * length * width
-    act, y_local, ent, step, cum, cum_r, state, decay = call(
+    act, slope, y_local, ent, step, cum, cum_r, state, decay = call(
         functools.partial(scan_forward, heads=heads, q=q),
         (starts, base),
         (raw, cw, hp, skip_row),
         (
+            spread(*act_shape, dtype=bf16),
             spread(*act_shape, dtype=bf16),
             spread(*wide_shape, dtype=bf16),
             spread(*col_shape),
@@ -798,6 +856,7 @@
             spread(sequences, 8, width),
         ),
         unit * 8 * q,
+        scratch=(pltpu.VMEM((at_dt // LANES, HALO + q, LANES), f32),),
     )
     cot = gather_pieces(after(cotangent[0], normed), state)
     split = sequences // len(cot)
@@ -920,6 +979,9 @@
     early = jnp.concatenate([gate_grad, out_grad], axis=1)
     early = lax.psum_scatter(early, "hi", scatter_dimension=0, tiled=False)
 
+    def piecewise(lanes):
+        return pl.BlockSpec((1, q, lanes), lambda n, p, *_: (n, p, 0))
+
     dscaled, dbc, dcum = call(
         functools.partial(scan_backward_inner, heads=heads, q=q),
         (starts, base),
@@ -930,18 +992,22 @@
             spread(*col_shape),
         ),
         unit * 16 * q,
+        grid=grid,
+        ins=[piecewise(a.shape[2]) for a in (act, dy, step, cum)]
+        + [pl.BlockSpec((1, 8, q), lambda n, p, *_: (n, 0, p))],
+        outs=[piecewise(width), piecewise(shared_width), piecewise(LANES)],
     )
     draw, dconv, dhead = call(
         functools.partial(scan_backward_outer, heads=heads, q=q),
         (starts, base),
-        (raw, act, dy, step, cum, dscaled, dbc, dcum, enter, leave, cw, hp, skip_row),
+        (raw, act, slope, dy, step, cum, dscaled, dbc, dcum, enter, leave, cw, hp, skip_row),
         (
             spread(sequences, total, pad_width, dtype=bf16),
             spread(sequences, 8, width + shared_width),
             spread(sequences, 8, LANES),
         ),
         unit * 2000,
-        scratch=(pltpu.VMEM((total + 8, width + shared_width), f32),),
+        scratch=(pltpu.VMEM((at_dt // LANES, total + 8, LANES), f32),),
     )
     draw_flat = draw.reshape(-1, pad_width)
 
@@ -1006,7 +1072,7 @@
         )
         return out
 
-    own_grad = scatter_pieces(grad_pieces)
+    own_grad = scatter_halves(grad_pieces)
     own_grad = own_grad * full_gain
     own = residual_in[0].astype(f32)
     own_scale = lax.rsqrt(jnp.mean(own * own, axis=-1, keepdims=True) + epsilon)

time: 482 us -> 431 us (0.89)
  waiting for transfers between devices: 113 us -> 90.3 us
  Pallas kernels: 120 us -> 107 us
  local copies, waits for them, and re-layouts: 45.3 us -> 38.3 us
    ppermute x0 -> x5, waiting for transfers between devices: none -> 40.6 us  [the longest x1 31.2 us: scatter_halves(): lax.ppermute((piece(1, left) + by_x[1].astype(f32)).astype(bf16), 'lo', S...]
    all_to_all x5, waiting for transfers between devices: 40.8 us -> 14.1 us  [exchange(): return lax.all_to_all(blocks, axes, 0, 0, tiled=True)]
    ppermute x6, waiting for transfers between devices: 25.5 us -> 1.49 us  [chain(): came = lax.ppermute(passed, 'hi', ((source, target),))]
    ppermute x2 -> x1, waiting for transfers between devices: 14.3 us -> 0.01 us  [scatter_pieces(): beside = lax.ppermute(piece(1).astype(bf16), 'lo', SWAP)]
    pallas_call x8, Pallas kernels: 120 us -> 107 us  [call(): pl.pallas_call(kernel, out_shape=outputs, grid_spec=pltpu.PrefetchScalarG...]
    ppermute x1, waiting for transfers between devices: 0.01 us -> 11 us  [step_of(): lax.ppermute(dot(edge_rows, conv_w, 1, 1).astype(bf16).reshape(sequences,...]
    ppermute x2 -> x1, waiting for transfers between devices: 6.84 us -> 0.01 us  [scatter_pieces(): across = lax.ppermute(piece(2).astype(bf16), 'bx', SWAP)]
    broadcast_in_dim x1 -> x0, other arithmetic: 6.02 us -> none  [step_of(): input_grad[None]]
  transfers between devices with their start and end apart: 42 -> 43, of which waited for: 13 -> 14; matrix products, arithmetic and copies ran while one was open for 24% -> 26% of each run, Pallas kernels for 21% -> 23%
where the time goes in v2:
time: 431 us; the launch traced here: 426 us
  Pallas kernels  107 us (25%)
  waiting for transfers between devices  90.3 us (21%)
  matrix products  55.2 us (13%)
  starting transfers between devices  51.4 us (12%)
  other arithmetic  39.5 us (9%)
  local copies, waits for them, and re-layouts  38.3 us (9%)
  blocking collectives  29.9 us (7%)
  between operations  15.1 us (4%)
    pallas_call x8, Pallas kernels, call(): pl.pallas_call(kernel, out_shape=outputs, grid_spec=pltpu.PrefetchScalarG...  107 us
    dot_general x11, matrix products, dot(): lax.dot_general(a, b, (((ca,), (cb,)), ((), ())), precision=precision, pr...  55.2 us
    ppermute x1, waiting for transfers between devices, scatter_halves(): lax.ppermute((piece(1, left) + by_x[1].astype(f32)).astype(bf16), 'lo', S...  31.2 us
    all_to_all x5, starting transfers between devices, exchange(): return lax.all_to_all(blocks, axes, 0, 0, tiled=True)  17.8 us
    all_to_all x1, blocking collectives, exchange(): return lax.all_to_all(blocks, axes, 0, 0, tiled=True)  15.6 us
    all_gather x1, blocking collectives, step_of(): lax.all_gather(small, 'hi', axis=0, tiled=False).reshape(devices, 8, LANES)  14.2 us
    all_to_all x5, waiting for transfers between devices, exchange(): return lax.all_to_all(blocks, axes, 0, 0, tiled=True)  14.1 us
    ppermute x1, waiting for transfers between devices, gather_starts(): half = jnp.concatenate([starts, lax.ppermute(starts, 'bx', SWAP)])  12.1 us
  transfers between devices with their start and end apart: 43, of which 14 were waited for; matrix products, arithmetic and copies ran while one was open for 26% of the time, Pallas kernels for 23%

profile of v2, /device:TPU:0, one launch (start us, length us, event | category | flops | bytes accessed | tf_op | source)
XLA Modules:
  0.0 426.1 jit_solution(12056296554918209899)
XLA Ops:
  11.7 15.6 %all_to_all.30 = bf16[8,48,768]{2,1,0:T(8,128)(2,1)} all-to-all(bf16[8,48,768]{2,1,0:T(8,128)(2,1)S(1)} %concatenate.67), channel_id=1, replica_groups=mesh['hi'=4,'lo'=2,'bx'=2,'core'=2] {'lo','bx','core'}, dimensions={0} | all-to-all | bytes 1179648 | tf_op jit(solution)/shard_map/all_to_all | solution.py:723
  30.4 1.5 collective-permute-start.4
  31.9 1.5 collective-permute-start.2
  34.5 3.4 all-to-all-start.1
  38.0 14.2 %all_gather.12 = bf16[4,8,8,128]{3,2,1,0:T(8,128)(2,1)S(1)} all-gather(bf16[1,8,8,128]{3,2,1,0:T(8,128)(2,1)S(1)} %copy.86), channel_id=1, replica_groups=mesh['hi'=4,'lo'=2,'bx'=2,'core'=2] {'hi'}, dimensions={0}, use_global_device_ids=true | all-gather | bytes 81920 | tf_op jit(solution)/shard_map/all_gather | solution.py:798
  53.8 1.9 collective-permute-start
  55.7 1.3 constant_dynamic-slice_fusion.1
  57.0 12.1 %collective-permute-done = s32[1,12]{1,0:T(1,128)S(1)} collective-permute-done((s32[1,12]{1,0:T(1,128)}, s32[1,12]{1,0:T(1,128)S(1)}, u32[]{:S(2)}, u32[]{:S(2)}) %collective-permute-start) | collective-permute-done | bytes 80 | tf_op jit(solution)/shard_map/ppermute | solution.py:670
  70.7 1.8 pad_maximum_fusion.7
  73.5 4.0 collective-permute-start.5
  78.2 1.3 collective-permute-done.5
  82.9 7.7 %shard_map.203 = bf16[4,528,1536]{2,1,0:T(8,128)(2,1)} custom-call(s32[1]{0:T(128)} %bitcast.1.place_ref, bf16[4,16,1536]{2,1,0:T(8,128)(2,1)} %pad_maximum_fusion.9.halo_ref, f32[8,1536]{1,0:T(8,128)} %broadcast_in_dim.82.gain_ref, bf16[256,1536]{1,0:T(8,128)(2,1)} %bitcast.222, bf16[256,1536]{1,0:T(8,128)(2,1)} %copy-done.13, ...), custom_call_target="tpu_custom_call" | custom-call | flops 32440320 | bytes 13025280 | tf_op jit(solution)/shard_map/pallas_call | solution.py:542
  90.6 1.3 collective-permute-start.14
  92.6 1.5 collective-permute-start.16
  94.1 9.3 %convolution_convert_fusion = bf16[2112,768]{1,0:T(8,128)(2,1)} fusion(bf16[2112,1536]{1,0:T(8,128)(2,1)} %bitcast.230, bf16[1536,768]{1,0:T(8,128)(2,1)} %all-gather.4.cloned.1.call-done.conv_ref), kind=kOutput, calls=%fused_computation | convolution fusion | flops 4984455168 | bytes 12091392 | tf_op jit(solution)/shard_map/dot_general | solution.py:24
  104.0 17.8 %shard_map.204 = (bf16[4,512,640]{2,1,0:T(8,128)(2,1)}, bf16[4,512,640]{2,1,0:T(8,128)(2,1)}, bf16[4,512,384]{2,1,0:T(8,128)(2,1)}, f32[4,512,128]{2,1,0:T(8,128...) custom-call(s32[4,12]{1,0:T(4,128)} %pad_add_fusion.starts_ref, ...), custom_call_target="tpu_custom_call" | custom-call | flops 1610612736 | bytes 14143488 | tf_op jit(solution)/shard_map/pallas_call | solution.py:542
  121.9 6.8 %collective-permute-done.16 = bf16[256,1536]{1,0:T(8,128)(2,1)S(1)} collective-permute-done((bf16[256,1536]{1,0:T(8,128)(2,1)S(1)}, bf16[256,1536]{1,0:T(8,128)(2,1)S(1)}, u32[]{:S(2)}, u32[]{:S(2)}) %collective-permute-start.16) | collective-permute-done | bytes 786464 | tf_op jit(solution)/shard_map/ppermute | solution.py:574
  129.5 3.0 pad_maximum_fusion
  135.4 4.6 %collective-permute-start.11 = (bf16[4,128,384]{2,1,0:T(8,128)(2,1)S(1)}, bf16[4,128,384]{2,1,0:T(8,128)(2,1)S(1)}, u32[]{:S(2)}, u32[]{:S(2)}) collective-permute-start(bf16[4,128,384]{2,1,0:T(8,128)(2,1)S(1)} %add_convert_fusion.11), channel_id=1, source_target_pairs={{0,8},{1,9},{2,10},{3,11},{4,12},{5,13},{6,14},{7,15}} | collective-permute-start | bytes 1179656 | tf_op jit(solution)/shard_map/ppermute | solution.py:701
  140.1 2.4 slice.382
  142.4 3.5 all-to-all-start.2
  146.0 1.4 slice_bitcast_fusion.12
  147.6 1.5 collective-permute-done.11
  150.0 7.6 %convolution_convert_fusion.1 = bf16[2112,384]{1,0:T(8,128)(2,1)} fusion(bf16[2112,1536]{1,0:T(8,128)(2,1)} %bitcast.231, bf16[1536,384]{1,0:T(8,128)(2,1)S(1)} %bitcast.254), kind=kOutput, calls=%fused_computation.1 | convolution fusion | flops 2492227584 | bytes 9289728 | tf_op jit(solution)/shard_map/dot_general | solution.py:24
  159.2 2.6 all-to-all-done.2
  161.8 5.0 %convolution_convert_fusion.6 = bf16[1024,384]{1,0:T(8,128)(2,1)} fusion(bf16[1024,1536]{1,0:T(8,128)(2,1)} %bitcast.46, bf16[384,1536]{1,0:T(8,128)(2,1)S(1)} %bitcast.250), kind=kOutput, calls=%fused_computation.40 | convolution fusion | flops 1208352768 | bytes 5111808 | tf_op jit(solution)/shard_map/dot_general | solution.py:24
  167.6 4.6 %convolution_convert_fusion.5 = bf16[1024,384]{1,0:T(8,128)(2,1)} fusion(bf16[1024,1536]{1,0:T(8,128)(2,1)} %bitcast.49, bf16[384,1536]{1,0:T(8,128)(2,1)S(1)} %bitcast.251), kind=kOutput, calls=%fused_computation.39 | convolution fusion | flops 1208352768 | bytes 5111808 | tf_op jit(solution)/shard_map/dot_general | solution.py:24
  172.8 9.3 %shard_map.205 = (bf16[4,512,384]{2,1,0:T(8,128)(2,1)}, f32[4,8,512]{2,1,0:T(8,128)}, bf16[8,256,384]{2,1,0:T(8,128)(2,1)}) custom-call(s32[1]{0:T(128)} %bitcast.1.place_ref, bf16[4,512,384]{2,1,0:T(8,128)(2,1)} %get-tuple-element.41.y_ref, f32[4,512,128]{2,1,0:T(8,128)} %get-tuple-element.42.ent_ref, bf16[4,512,640]{2,1,0:T(8,128)(2,1)} %get-tuple-element.43.act_ref, ...), custom_call_target="tpu_custom_call" | custom-call | flops 235929600 | bytes 12054528 | tf_op jit(solution)/shard_map/pallas_call | solution.py:542
  185.5 2.4 fusion.33
  187.9 1.5 collective-permute-done.19
  189.4 1.6 collective-permute-start.20
  191.1 3.5 convolution_convert_fusion.2
  195.2 10.8 %shard_map.206 = (bf16[4,512,384]{2,1,0:T(8,128)(2,1)}, bf16[4,528,384]{2,1,0:T(8,128)(2,1)}, bf16[8,256,384]{2,1,0:T(8,128)(2,1)}, f32[4,128,384]{2,1,0:T(8,128)}, f32[4,8,384]{2,1,0:T(8,128)}) custom-call(s32[1]{0:T(128)} %bitcast.1.place_ref, bf16[4,512,384]{2,1,0:T(8,128)(2,1)} %get-tuple-element.52.y_ref, f32[4,512,128]{2,1,0:T(8,128)} %get-tuple-element.42.ent_ref, ...), custom_call_target="tpu_custom_call" | custom-call | flops 235929600 | bytes 14118912 | tf_op jit(solution)/shard_map/pallas_call | solution.py:542
  208.0 3.7 convolution_bitcast_fusion.1
  211.7 2.6 fusion.1
  214.3 3.7 all-to-all-start.3
  219.1 7.1 %fusion.2 = bf16[1536,384]{1,0:T(8,128)(2,1)S(1)} fusion(bf16[4,528,1536]{2,1,0:T(8,128)(2,1)} %shard_map.203, bf16[4,528,384]{2,1,0:T(8,128)(2,1)} %get-tuple-element.62.dgate_ref), kind=kOutput, calls=%fused_computation.12 | convolution fusion | flops 2492006400 | bytes 9289728 | tf_op jit(solution)/shard_map/dot_general | solution.py:24
  228.1 1.3 collective-permute-start.27
  229.4 4.4 %all-to-all-done.3 = bf16[4,96,1536]{2,1,0:T(8,128)(2,1)S(1)} async-done(((bf16[4,96,1536]{2,1,0:T(8,128)(2,1)}), bf16[4,96,1536]{2,1,0:T(8,128)(2,1)S(1)}, u32[]{:S(2)}, u32[]{:S(2)}) %all-to-all-start.3) | async-done | bytes 1179680 | tf_op jit(solution)/shard_map/all_to_all | solution.py:723
  233.8 2.5 pad_maximum_fusion.1
  236.3 16.2 %shard_map.207 = (bf16[4,512,384]{2,1,0:T(8,128)(2,1)}, bf16[4,512,256]{2,1,0:T(8,128)(2,1)}, f32[4,512,128]{2,1,0:T(8,128)}) custom-call(s32[4,12]{1,0:T(4,128)} %pad_add_fusion.starts_ref, s32[1]{0:T(128)} %bitcast.15.base_ref, bf16[4,512,640]{2,1,0:T(8,128)(2,1)} %get-tuple-element.43.act_ref, bf16[4,512,384]{2,1,0:T(8,128)(2,1)} %get-tuple-element.53.dy_ref, ...), custom_call_target="tpu_custom_call" | custom-call | flops 3221225472 | bytes 10027008 | tf_op jit(solution)/shard_map/pallas_call | solution.py:542
  253.4 27.3 %shard_map.208 = (bf16[4,528,768]{2,1,0:T(8,128)(2,1)}, f32[4,8,640]{2,1,0:T(8,128)}, f32[4,8,128]{2,1,0:T(8,128)}) custom-call(s32[4,12]{1,0:T(4,128)} %pad_add_fusion.starts_ref, s32[1]{0:T(128)} %bitcast.15.base_ref, bf16[4,528,768]{2,1,0:T(8,128)(2,1)} %bitcast.235, bf16[4,512,640]{2,1,0:T(8,128)(2,1)} %get-tuple-element.43.act_ref, ...), custom_call_target="tpu_custom_call" | custom-call | flops 1572864000 | bytes 19992576 | tf_op jit(solution)/shard_map/pallas_call | solution.py:542
  282.4 1.7 collective-permute-start.28
  284.5 11.0 %collective-permute-done.28.back_ref = bf16[4,16,1536]{2,1,0:T(8,128)(2,1)S(1)} collective-permute-done((bf16[4,16,1536]{2,1,0:T(8,128)(2,1)S(1)}, bf16[4,16,1536]{2,1,0:T(8,128)(2,1)S(1)}, u32[]{:S(2)}, u32[]{:S(2)}) %collective-permute-start.28) | collective-permute-done | bytes 196640 | tf_op jit(solution)/shard_map/ppermute | solution.py:1015
  296.2 8.6 %shard_map.210 = bf16[4,256,1536]{2,1,0:T(8,128)(2,1)} custom-call(s32[1]{0:T(128)} %bitcast.1.place_ref, bf16[4,528,768]{2,1,0:T(8,128)(2,1)} %get-tuple-element.61.draw_ref, bf16[4,528,384]{2,1,0:T(8,128)(2,1)} %get-tuple-element.62.dgate_ref, bf16[4,16,1536]{2,1,0:T(8,128)(2,1)} %copy-done.43, bf16[1536,768]{1,0:T(8,128)(2,1)} %all-gather.4.cloned.1.call-done.conv_ref, ...), custom_call_target="tpu_custom_call" | custom-call | flops 3623878656 | bytes 11747328 | tf_op jit(solution)/shard_map/pallas_call | solution.py:542
  304.8 9.3 %convolution_bitcast_fusion = bf16[1536,768]{0,1:T(8,128)(2,1)S(1)} fusion(bf16[4,528,1536]{2,1,0:T(8,128)(2,1)} %shard_map.203, bf16[4,528,768]{2,1,0:T(8,128)(2,1)} %get-tuple-element.61.draw_ref), kind=kOutput, calls=%fused_computation.3 | convolution fusion | flops 4982833152 | bytes 12091392 | tf_op jit(solution)/shard_map/dot_general | solution.py:24
  315.3 2.5 copy.107
  319.1 8.7 %shard_map.209 = bf16[4,256,1536]{2,1,0:T(8,128)(2,1)} custom-call(s32[1]{0:T(128)} %bitcast.1.place_ref, bf16[4,528,768]{2,1,0:T(8,128)(2,1)} %get-tuple-element.61.draw_ref, bf16[4,528,384]{2,1,0:T(8,128)(2,1)} %get-tuple-element.62.dgate_ref, bf16[4,16,1536]{2,1,0:T(8,128)(2,1)} %copy-done.43, bf16[1536,768]{1,0:T(8,128)(2,1)} %all-gather.4.cloned.1.call-done.conv_ref, ...), custom_call_target="tpu_custom_call" | custom-call | flops 3623878656 | bytes 11747328 | tf_op jit(solution)/shard_map/pallas_call | solution.py:542
  327.8 2.2 add_convert_fusion.5
  330.3 1.4 collective-permute-start.30
  331.7 1.8 convolution_convert_fusion.3
  334.2 3.7 fusion.12
  338.7 2.0 collective-permute-start.23
  341.4 9.2 %collective-permute-done.32 = bf16[2,256,768]{2,1,0:T(8,128)(2,1)S(1)} collective-permute-done((bf16[2,256,768]{2,1,0:T(8,128)(2,1)S(1)}, bf16[2,256,768]{2,1,0:T(8,128)(2,1)S(1)}, u32[]{:S(2)}, u32[]{:S(2)}) %collective-permute-start.32) | collective-permute-done | bytes 786464 | tf_op jit(solution)/shard_map/ppermute | solution.py:644
  351.5 1.9 fusion.18
  353.5 1.4 collective-permute-start.31
  357.2 3.4 all-to-all-start.4
  361.5 31.2 %collective-permute-done.31 = bf16[256,768]{1,0:T(8,128)(2,1)S(1)} collective-permute-done((bf16[256,768]{1,0:T(8,128)(2,1)S(1)}, bf16[256,768]{1,0:T(8,128)(2,1)S(1)}, u32[]{:S(2)}, u32[]{:S(2)}) %collective-permute-start.31) | collective-permute-done | bytes 393248 | tf_op jit(solution)/shard_map/ppermute | solution.py:645
  393.5 2.2 bitcast_add_fusion.1
  395.7 3.9 fusion.6
  399.7 3.7 all-to-all-start.5
  403.4 2.7 fusion.9
  407.0 6.8 %all-to-all-done.5 = bf16[8,48,768]{2,1,0:T(8,128)(2,1)S(1)} async-done(((bf16[8,48,768]{2,1,0:T(8,128)(2,1)}), bf16[8,48,768]{2,1,0:T(8,128)(2,1)S(1)}, u32[]{:S(2)}, u32[]{:S(2)}) %all-to-all-start.5) | async-done | bytes 589856 | tf_op jit(solution)/shard_map/all_to_all | solution.py:723
  417.6 1.3 multiply_reduce_fusion
  (278 shorter events, 53.4 us)
Async XLA Ops:
  7.2 86.9 %all-gather.4.cloned.1.call-start = ((), (), s32[]{:S(2)}) async-start(), calls=%async_computation.8 | async-start | bytes 2949120 | tf_op jit(solution)/shard_map/all_gather | solution.py:792
  11.3 16.1 %copy-start.44 = (f32[48]{0:T(128)S(1)}, f32[48]{0:T(128)}, u32[]{:S(2)}) copy-start(f32[48]{0:T(128)} %param.21) | copy-start | bytes 580
  11.7 17.5 %copy-start.40 = (f32[48]{0:T(128)S(1)}, f32[48]{0:T(128)}, u32[]{:S(2)}) copy-start(f32[48]{0:T(128)} %param.20) | copy-start | bytes 580
  11.7 17.5 %copy-start.41 = (f32[48]{0:T(128)S(1)}, f32[48]{0:T(128)}, u32[]{:S(2)}) copy-start(f32[48]{0:T(128)} %param.19) | copy-start | bytes 580
  11.7 18.2 %copy-start = (bf16[1,256,1536]{2,1,0:T(8,128)(2,1)S(1)}, bf16[1,256,1536]{2,1,0:T(8,128)(2,1)}, u32[]{:S(2)}) copy-start(bf16[1,256,1536]{2,1,0:T(8,128)(2,1)} %param.13) | copy-start | bytes 2359300
  29.9 43.0 %collective-permute-start.3 = (bf16[256,1536]{1,0:T(8,128)(2,1)S(1)}, bf16[256,1536]{1,0:T(8,128)(2,1)S(1)}, u32[]{:S(2)}, u32[]{:S(2)}) collective-permute-start(bf16[256,1536]{1,0:T(8,128)(2,1)S(1)} %bitcast.223), channel_id=1, source_target_pairs={{0,2},{2,0},{1,3},{3,1},{4,6},{6,4},{5,7},{7,5},{8,10},{10,8},{9,1... | collective-permute-start | bytes 2359304 | tf_op jit(solution)/shard_map/ppermute | solution.py:586
  30.4 42.1 %collective-permute-start.4 = (bf16[256,1536]{1,0:T(8,128)(2,1)S(1)}, bf16[256,1536]{1,0:T(8,128)(2,1)S(1)}, u32[]{:S(2)}, u32[]{:S(2)}) collective-permute-start(bf16[256,1536]{1,0:T(8,128)(2,1)S(1)} %bitcast.224), channel_id=1, source_target_pairs={{0,6},{6,0},{2,4},{4,2},{1,7},{7,1},{3,5},{5,3},{8,14},{14,8},{10,... | collective-permute-start | bytes 2359304 | tf_op jit(solution)/shard_map/ppermute | solution.py:587
  31.9 41.3 %collective-permute-start.2 = (bf16[256,1536]{1,0:T(8,128)(2,1)S(1)}, bf16[256,1536]{1,0:T(8,128)(2,1)S(1)}, u32[]{:S(2)}, u32[]{:S(2)}) collective-permute-start(bf16[256,1536]{1,0:T(8,128)(2,1)S(1)} %bitcast.225), channel_id=1, source_target_pairs={{0,4},{4,0},{1,5},{5,1},{2,6},{6,2},{3,7},{7,3},{8,12},{12,8},{9,1... | collective-permute-start | bytes 2359304 | tf_op jit(solution)/shard_map/ppermute | solution.py:585
  33.3 48.1 %collective-permute-start.7 = (bf16[256,1536]{1,0:T(8,128)(2,1)S(1)}, bf16[256,1536]{1,0:T(8,128)(2,1)}, u32[]{:S(2)}, u32[]{:S(2)}) collective-permute-start(bf16[256,1536]{1,0:T(8,128)(2,1)S(1)} %bitcast.226), channel_id=1, source_target_pairs={{0,1},{1,0},{2,3},{3,2},{4,5},{5,4},{6,7},{7,6},{8,9},{9,8},{10,11... | collective-permute-start | bytes 2359304 | tf_op jit(solution)/shard_map/ppermute | solution.py:589
  34.5 36.1 %all-to-all-start.1 = ((bf16[8,48,384]{2,1,0:T(8,128)(2,1)}), bf16[8,48,384]{2,1,0:T(8,128)(2,1)S(1)}, u32[]{:S(2)}, u32[]{:S(2)}) async-start(bf16[8,48,384]{2,1,0:T(8,128)(2,1)} %bitcast.26), calls=%async_computation.1 | async-start | bytes 589824 | tf_op jit(solution)/shard_map/all_to_all | solution.py:723
  38.0 102.1 %all-gather.6.cloned.1.call-start = ((), (), s32[]{:S(2)}) async-start(), calls=%async_computation.10 | async-start | bytes 2949120 | tf_op jit(solution)/shard_map/all_gather | solution.py:822
  53.8 23.8 %slice-start.2 = ((f32[5,3328]{1,0:T(8,128)}), f32[5,256]{1,0:T(8,128)S(1)}, s32[]{:S(2)}) async-start(f32[5,3328]{1,0:T(8,128)} %reshape.323), calls=%async_computation.14 | async-start | bytes 16384 | tf_op jit(solution)/shard_map/slice | solution.py:804
  53.8 15.3 %collective-permute-start = (s32[1,12]{1,0:T(1,128)}, s32[1,12]{1,0:T(1,128)S(1)}, u32[]{:S(2)}, u32[]{:S(2)}) collective-permute-start(s32[1,12]{1,0:T(1,128)} %param.14), channel_id=1, source_target_pairs={{0,2},{2,0},{1,3},{3,1},{4,6},{6,4},{5,7},{7,5},{8,10},{10,8},{9,1... | collective-permute-start | bytes 152 | tf_op jit(solution)/shard_map/ppermute | solution.py:670
  70.4 3.2 collective-permute-start.1
  70.7 6.9 %copy-start.33 = (f32[5,384]{1,0:T(8,128)S(1)}, f32[5,384]{1,0:T(8,128)}, u32[]{:S(2)}) copy-start(f32[5,384]{1,0:T(8,128)} %constant_dynamic-slice_fusion.1) | copy-start | bytes 23044
  70.7 8.8 %copy-start.39 = (s32[1,12]{1,0:T(1,128)S(1)}, s32[1,12]{1,0:T(1,128)}, u32[]{:S(2)}) copy-start(s32[1,12]{1,0:T(1,128)} %copy-done.38) | copy-start | bytes 148
  72.6 10.3 %copy-start.12 = (bf16[256,1536]{1,0:T(8,128)(2,1)}, bf16[256,1536]{1,0:T(8,128)(2,1)S(1)}, u32[]{:S(2)}) copy-start(bf16[256,1536]{1,0:T(8,128)(2,1)S(1)} %collective-permute-done.4.refs_3_) | copy-start | bytes 2359300
  72.6 8.9 %collective-permute-start.10 = (bf16[256,1536]{1,0:T(8,128)(2,1)S(1)}, bf16[256,1536]{1,0:T(8,128)(2,1)S(1)}, u32[]{:S(2)}, u32[]{:S(2)}) collective-permute-start(bf16[256,1536]{1,0:T(8,128)(2,1)S(1)} %collective-permute-done.4.refs_3_), channel_id=1, source_target_pairs={{0,1},{1,0},{2,3},{3,2},{4,5},{5,4},{6,7},{7,6},{8,9},{9,8},{10,11... | collective-permute-start | bytes 2359304 | tf_op jit(solution)/shard_map/ppermute | solution.py:589
  72.9 10.0 %copy-start.11 = (bf16[256,1536]{1,0:T(8,128)(2,1)}, bf16[256,1536]{1,0:T(8,128)(2,1)S(1)}, u32[]{:S(2)}) copy-start(bf16[256,1536]{1,0:T(8,128)(2,1)S(1)} %collective-permute-done.3.refs_2_) | copy-start | bytes 2359300
  72.9 8.6 %collective-permute-start.9 = (bf16[256,1536]{1,0:T(8,128)(2,1)S(1)}, bf16[256,1536]{1,0:T(8,128)(2,1)S(1)}, u32[]{:S(2)}, u32[]{:S(2)}) collective-permute-start(bf16[256,1536]{1,0:T(8,128)(2,1)S(1)} %collective-permute-done.3.refs_2_), channel_id=1, source_target_pairs={{0,1},{1,0},{2,3},{3,2},{4,5},{5,4},{6,7},{7,6},{8,9},{9,8},{10,11... | collective-permute-start | bytes 2359304 | tf_op jit(solution)/shard_map/ppermute | solution.py:589
  73.2 9.1 %copy-start.13 = (bf16[256,1536]{1,0:T(8,128)(2,1)}, bf16[256,1536]{1,0:T(8,128)(2,1)S(1)}, u32[]{:S(2)}) copy-start(bf16[256,1536]{1,0:T(8,128)(2,1)S(1)} %collective-permute-done.2.refs_1_) | copy-start | bytes 2359300
  73.2 8.3 %collective-permute-start.8 = (bf16[256,1536]{1,0:T(8,128)(2,1)S(1)}, bf16[256,1536]{1,0:T(8,128)(2,1)S(1)}, u32[]{:S(2)}, u32[]{:S(2)}) collective-permute-start(bf16[256,1536]{1,0:T(8,128)(2,1)S(1)} %collective-permute-done.2.refs_1_), channel_id=1, source_target_pairs={{0,1},{1,0},{2,3},{3,2},{4,5},{5,4},{6,7},{7,6},{8,9},{9,8},{10,11... | collective-permute-start | bytes 2359304 | tf_op jit(solution)/shard_map/ppermute | solution.py:589
  73.5 6.0 %collective-permute-start.5 = (bf16[2,16,1536]{2,1,0:T(8,128)(2,1)S(1)}, bf16[2,16,1536]{2,1,0:T(8,128)(2,1)S(1)}, u32[]{:S(2)}, u32[]{:S(2)}) collective-permute-start(bf16[2,16,1536]{2,1,0:T(8,128)(2,1)S(1)} %pad_maximum_fusion.10), channel_id=1, source_target_pairs={{0,8},{8,16},{16,24},{1,9},{9,17},{17,25},{2,10},{10,18},{18,26},{... | collective-permute-start | bytes 294920 | tf_op jit(solution)/shard_map/ppermute | solution.py:605
  79.5 1.3 collective-permute-start.6
  82.9 7.8 %copy-start.5 = (bf16[1,256,1536]{2,1,0:T(8,128)(2,1)S(1)}, bf16[1,256,1536]{2,1,0:T(8,128)(2,1)}, u32[]{:S(2)}) copy-start(bf16[1,256,1536]{2,1,0:T(8,128)(2,1)} %param.24) | copy-start | bytes 2359300
  90.6 31.2 %collective-permute-start.14 = (bf16[256,1536]{1,0:T(8,128)(2,1)S(1)}, bf16[256,1536]{1,0:T(8,128)(2,1)S(1)}, u32[]{:S(2)}, u32[]{:S(2)}) collective-permute-start(bf16[256,1536]{1,0:T(8,128)(2,1)S(1)} %bitcast.240), channel_id=1, source_target_pairs={{0,4},{4,0},{1,5},{5,1},{2,6},{6,2},{3,7},{7,3},{8,12},{12,8},{9,1... | collective-permute-start | bytes 2359304 | tf_op jit(solution)/shard_map/ppermute | solution.py:573
  91.9 29.9 %collective-permute-start.15 = (bf16[256,1536]{1,0:T(8,128)(2,1)S(1)}, bf16[256,1536]{1,0:T(8,128)(2,1)S(1)}, u32[]{:S(2)}, u32[]{:S(2)}) collective-permute-start(bf16[256,1536]{1,0:T(8,128)(2,1)S(1)} %bitcast.241), channel_id=1, source_target_pairs={{0,2},{2,0},{1,3},{3,1},{4,6},{6,4},{5,7},{7,5},{8,10},{10,8},{9,1... | collective-permute-start | bytes 2359304 | tf_op jit(solution)/shard_map/ppermute | solution.py:572
  92.6 36.0 %collective-permute-start.16 = (bf16[256,1536]{1,0:T(8,128)(2,1)S(1)}, bf16[256,1536]{1,0:T(8,128)(2,1)S(1)}, u32[]{:S(2)}, u32[]{:S(2)}) collective-permute-start(bf16[256,1536]{1,0:T(8,128)(2,1)S(1)} %bitcast.242), channel_id=1, source_target_pairs={{0,6},{6,0},{2,4},{4,2},{1,7},{7,1},{3,5},{5,3},{8,14},{14,8},{10,... | collective-permute-start | bytes 2359304 | tf_op jit(solution)/shard_map/ppermute | solution.py:574
  94.1 9.3 %copy-start.36 = (f32[384]{0:T(512)S(1)}, f32[384]{0:T(512)}, u32[]{:S(2)}) copy-start(f32[384]{0:T(512)} %reshape.324) | copy-start | bytes 4612
  121.8 10.7 %copy-start.14 = (bf16[256,1536]{1,0:T(8,128)(2,1)}, bf16[256,1536]{1,0:T(8,128)(2,1)S(1)}, u32[]{:S(2)}) copy-start(bf16[256,1536]{1,0:T(8,128)(2,1)S(1)} %collective-permute-done.14) | copy-start | bytes 2359300
  121.9 10.7 %copy-start.16 = (bf16[256,1536]{1,0:T(8,128)(2,1)}, bf16[256,1536]{1,0:T(8,128)(2,1)S(1)}, u32[]{:S(2)}) copy-start(bf16[256,1536]{1,0:T(8,128)(2,1)S(1)} %collective-permute-done.15) | copy-start | bytes 2359300
  132.5 35.1 %collective-permute-start.17 = (bf16[4,256,1536]{2,1,0:T(8,128)(2,1)}, bf16[4,256,1536]{2,1,0:T(8,128)(2,1)}, u32[]{:S(2)}, u32[]{:S(2)}) collective-permute-start(bf16[4,256,1536]{2,1,0:T(8,128)(2,1)} %pad_maximum_fusion), channel_id=1, source_target_pairs={{0,1},{1,0},{2,3},{3,2},{4,5},{5,4},{6,7},{7,6},{8,9},{9,8},{10,11... | collective-permute-start | bytes 9437192 | tf_op jit(solution)/shard_map/ppermute | solution.py:576
  135.4 13.6 %collective-permute-start.11 = (bf16[4,128,384]{2,1,0:T(8,128)(2,1)S(1)}, bf16[4,128,384]{2,1,0:T(8,128)(2,1)S(1)}, u32[]{:S(2)}, u32[]{:S(2)}) collective-permute-start(bf16[4,128,384]{2,1,0:T(8,128)(2,1)S(1)} %add_convert_fusion.11), channel_id=1, source_target_pairs={{0,8},{1,9},{2,10},{3,11},{4,12},{5,13},{6,14},{7,15}} | collective-permute-start | bytes 1179656 | tf_op jit(solution)/shard_map/ppermute | solution.py:701
  142.4 19.3 %all-to-all-start.2 = ((bf16[4,96,1536]{2,1,0:T(8,128)(2,1)}), bf16[4,96,1536]{2,1,0:T(8,128)(2,1)S(1)}, u32[]{:S(2)}, u32[]{:S(2)}) async-start(bf16[4,96,1536]{2,1,0:T(8,128)(2,1)} %slice.382), calls=%async_computation.2 | async-start | bytes 2359296 | tf_op jit(solution)/shard_map/all_to_all | solution.py:723
  147.5 10.0 %copy-start.10 = (bf16[4,4,96,384]{3,2,1,0:T(8,128)(2,1)}, bf16[4,4,96,384]{3,2,1,0:T(8,128)(2,1)S(1)}, u32[]{:S(2)}) copy-start(bf16[4,4,96,384]{3,2,1,0:T(8,128)(2,1)S(1)} %pad_maximum_fusion.4) | copy-start | bytes 3538948
  149.2 8.4 %collective-permute-start.12 = (bf16[4,128,384]{2,1,0:T(8,128)(2,1)S(1)}, bf16[4,128,384]{2,1,0:T(8,128)(2,1)S(1)}, u32[]{:S(2)}, u32[]{:S(2)}) collective-permute-start(bf16[4,128,384]{2,1,0:T(8,128)(2,1)S(1)} %add_convert_fusion.10), channel_id=1, source_target_pairs={{8,16},{9,17},{10,18},{11,19},{12,20},{13,21},{14,22},{15,23}} | collective-permute-start | bytes 1179656 | tf_op jit(solution)/shard_map/ppermute | solution.py:701
  158.5 8.3 %collective-permute-start.13 = (bf16[4,128,384]{2,1,0:T(8,128)(2,1)}, bf16[4,128,384]{2,1,0:T(8,128)(2,1)S(1)}, u32[]{:S(2)}, u32[]{:S(2)}) collective-permute-start(bf16[4,128,384]{2,1,0:T(8,128)(2,1)} %add_convert_fusion.9), channel_id=1, source_target_pairs={{16,24},{17,25},{18,26},{19,27},{20,28},{21,29},{22,30},{23,31}} | collective-permute-start | bytes 1179656 | tf_op jit(solution)/shard_map/ppermute | solution.py:701
  161.8 29.3 %copy-start.8 = (bf16[4,96,1536]{2,1,0:T(8,128)(2,1)}, bf16[4,96,1536]{2,1,0:T(8,128)(2,1)S(1)}, u32[]{:S(2)}) copy-start(bf16[4,96,1536]{2,1,0:T(8,128)(2,1)S(1)} %all-to-all-done.2) | copy-start | bytes 3538948
  183.0 1.3 collective-permute-start.18
  185.1 4.3 %collective-permute-start.19 = (f32[2,2,8,512]{3,2,1,0:T(8,128)S(1)}, f32[2,2,8,512]{3,2,1,0:T(8,128)S(1)}, u32[]{:S(2)}, u32[]{:S(2)}) collective-permute-start(f32[2,2,8,512]{3,2,1,0:T(8,128)S(1)} %rev.7), channel_id=1, source_target_pairs={{0,2},{2,0},{1,3},{3,1},{4,6},{6,4},{5,7},{7,5},{8,10},{10,8},{9,1... | collective-permute-start | bytes 196616 | tf_op jit(solution)/shard_map/ppermute | solution.py:662
  189.4 5.2 %collective-permute-start.20 = (f32[2,2,8,512]{3,2,1,0:T(8,128)S(1)}, f32[2,2,8,512]{3,2,1,0:T(8,128)S(1)}, u32[]{:S(2)}, u32[]{:S(2)}) collective-permute-start(f32[2,2,8,512]{3,2,1,0:T(8,128)S(1)} %add.194), channel_id=1, source_target_pairs={{0,4},{4,0},{1,5},{5,1},{2,6},{6,2},{3,7},{7,3},{8,12},{12,8},{9,1... | collective-permute-start | bytes 196616 | tf_op jit(solution)/shard_map/ppermute | solution.py:663
  194.6 139.6 %collective-permute-start.21 = (bf16[4,256,1536]{2,1,0:T(8,128)(2,1)}, bf16[4,256,1536]{2,1,0:T(8,128)(2,1)}, u32[]{:S(2)}, u32[]{:S(2)}) collective-permute-start(bf16[4,256,1536]{2,1,0:T(8,128)(2,1)} %bitcast.56), channel_id=1, source_target_pairs={{0,1},{1,0},{2,3},{3,2},{4,5},{5,4},{6,7},{7,6},{8,9},{9,8},{10,11... | collective-permute-start | bytes 9437192 | tf_op jit(solution)/shard_map/ppermute | solution.py:616
  195.2 10.8 %copy-start.32 = (f32[4,384]{1,0:T(4,128)S(1)}, f32[4,384]{1,0:T(4,128)}, u32[]{:S(2)}) copy-start(f32[4,384]{1,0:T(4,128)} %copy-done.31) | copy-start | bytes 18436
  207.3 10.7 %collective-permute-start.25 = (bf16[4,128,384]{2,1,0:T(8,128)(2,1)S(1)}, bf16[4,128,384]{2,1,0:T(8,128)(2,1)S(1)}, u32[]{:S(2)}, u32[]{:S(2)}) collective-permute-start(bf16[4,128,384]{2,1,0:T(8,128)(2,1)S(1)} %add_convert_fusion.8), channel_id=1, source_target_pairs={{24,16},{25,17},{26,18},{27,19},{28,20},{29,21},{30,22},{31,23}} | collective-permute-start | bytes 1179656 | tf_op jit(solution)/shard_map/ppermute | solution.py:701
  214.3 19.5 %all-to-all-start.3 = ((bf16[4,96,1536]{2,1,0:T(8,128)(2,1)}), bf16[4,96,1536]{2,1,0:T(8,128)(2,1)S(1)}, u32[]{:S(2)}, u32[]{:S(2)}) async-start(bf16[4,96,1536]{2,1,0:T(8,128)(2,1)} %bitcast.78), calls=%async_computation.3 | async-start | bytes 2359296 | tf_op jit(solution)/shard_map/all_to_all | solution.py:723
  218.0 137.4 %reduce-scatter.5.cloned.1.call-start = ((), (), s32[]{:S(2)}) async-start(), calls=%async_computation.9 | async-start | bytes 2949120 | tf_op jit(solution)/shard_map/reduce_scatter | solution.py:980
  218.2 9.0 %collective-permute-start.26 = (bf16[4,128,384]{2,1,0:T(8,128)(2,1)S(1)}, bf16[4,128,384]{2,1,0:T(8,128)(2,1)S(1)}, u32[]{:S(2)}, u32[]{:S(2)}) collective-permute-start(bf16[4,128,384]{2,1,0:T(8,128)(2,1)S(1)} %add_convert_fusion.7), channel_id=1, source_target_pairs={{16,8},{17,9},{18,10},{19,11},{20,12},{21,13},{22,14},{23,15}} | collective-permute-start | bytes 1179656 | tf_op jit(solution)/shard_map/ppermute | solution.py:701
  228.1 24.5 %collective-permute-start.27 = (bf16[4,128,384]{2,1,0:T(8,128)(2,1)}, bf16[4,128,384]{2,1,0:T(8,128)(2,1)S(1)}, u32[]{:S(2)}, u32[]{:S(2)}) collective-permute-start(bf16[4,128,384]{2,1,0:T(8,128)(2,1)} %add_convert_fusion.6), channel_id=1, source_target_pairs={{8,0},{9,1},{10,2},{11,3},{12,4},{13,5},{14,6},{15,7}} | collective-permute-start | bytes 1179656 | tf_op jit(solution)/shard_map/ppermute | solution.py:701
  236.3 163.4 %reduce-scatter.7.cloned.1.call-start = ((), (), s32[]{:S(2)}) async-start(), calls=%async_computation.11 | async-start | bytes 2949120 | tf_op jit(solution)/shard_map/reduce_scatter | solution.py:1051
  236.3 16.3 %copy-start.34 = (f32[4,8,384]{2,1,0:T(8,128)S(1)}, f32[4,8,384]{2,1,0:T(8,128)}, u32[]{:S(2)}) copy-start(f32[4,8,384]{2,1,0:T(8,128)} %get-tuple-element.65) | copy-start | bytes 147460
  253.4 28.2 %copy-start.7 = (bf16[1536,768]{1,0:T(8,128)(2,1)S(1)}, bf16[1536,768]{1,0:T(8,128)(2,1)}, u32[]{:S(2)}) copy-start(bf16[1536,768]{1,0:T(8,128)(2,1)} %all-gather.4.cloned.1.call-done.conv_ref) | copy-start | bytes 7077892
  282.4 13.0 %collective-permute-start.28 = (bf16[4,16,1536]{2,1,0:T(8,128)(2,1)S(1)}, bf16[4,16,1536]{2,1,0:T(8,128)(2,1)S(1)}, u32[]{:S(2)}, u32[]{:S(2)}) collective-permute-start(bf16[4,16,1536]{2,1,0:T(8,128)(2,1)S(1)} %bitcast.284), channel_id=1, source_target_pairs={{8,0},{16,8},{24,16},{9,1},{17,9},{25,17},{10,2},{18,10},{26,18},{... | collective-permute-start | bytes 589832 | tf_op jit(solution)/shard_map/ppermute | solution.py:1015
  304.7 9.4 %copy-start.30 = (f32[4,8,640]{2,1,0:T(8,128)S(1)}, f32[4,8,640]{2,1,0:T(8,128)}, u32[]{:S(2)}) copy-start(f32[4,8,640]{2,1,0:T(8,128)} %get-tuple-element.64) | copy-start | bytes 245764
  304.7 9.6 %copy-start.35 = (f32[4,8,128]{2,1,0:T(8,128)S(1)}, f32[4,8,128]{2,1,0:T(8,128)}, u32[]{:S(2)}) copy-start(f32[4,8,128]{2,1,0:T(8,128)} %get-tuple-element.66) | copy-start | bytes 49156
  304.8 23.1 %collective-permute-start.29 = (bf16[4,256,1536]{2,1,0:T(8,128)(2,1)}, bf16[4,256,1536]{2,1,0:T(8,128)(2,1)}, u32[]{:S(2)}, u32[]{:S(2)}) collective-permute-start(bf16[4,256,1536]{2,1,0:T(8,128)(2,1)} %shard_map.210), channel_id=1, source_target_pairs={{0,1},{1,0},{2,3},{3,2},{4,5},{5,4},{6,7},{7,6},{8,9},{9,8},{10,11... | collective-permute-start | bytes 9437192 | tf_op jit(solution)/shard_map/ppermute | solution.py:632
  330.1 20.5 %collective-permute-start.32 = (bf16[2,256,768]{2,1,0:T(8,128)(2,1)S(1)}, bf16[2,256,768]{2,1,0:T(8,128)(2,1)S(1)}, u32[]{:S(2)}, u32[]{:S(2)}) collective-permute-start(bf16[2,256,768]{2,1,0:T(8,128)(2,1)S(1)} %pad_maximum_fusion.6), channel_id=1, source_target_pairs={{0,4},{4,0},{1,5},{5,1},{2,6},{6,2},{3,7},{7,3},{8,12},{12,8},{9,1... | collective-permute-start | bytes 2359304 | tf_op jit(solution)/shard_map/ppermute | solution.py:644
  330.3 20.5 %collective-permute-start.30 = (bf16[2,256,768]{2,1,0:T(8,128)(2,1)S(1)}, bf16[2,256,768]{2,1,0:T(8,128)(2,1)S(1)}, u32[]{:S(2)}, u32[]{:S(2)}) collective-permute-start(bf16[2,256,768]{2,1,0:T(8,128)(2,1)S(1)} %pad_maximum_fusion.5), channel_id=1, source_target_pairs={{0,2},{2,0},{1,3},{3,1},{4,6},{6,4},{5,7},{7,5},{8,10},{10,8},{9,1... | collective-permute-start | bytes 2359304 | tf_op jit(solution)/shard_map/ppermute | solution.py:643
  337.9 57.8 %collective-permute-start.22 = (bf16[256,1536]{1,0:T(8,128)(2,1)}, bf16[256,1536]{1,0:T(8,128)(2,1)}, u32[]{:S(2)}, u32[]{:S(2)}) collective-permute-start(bf16[256,1536]{1,0:T(8,128)(2,1)} %get-tuple-element.77), channel_id=1, source_target_pairs={{0,2},{2,0},{1,3},{3,1},{4,6},{6,4},{5,7},{7,5},{8,10},{10,8},{9,1... | collective-permute-start | bytes 2359304 | tf_op jit(solution)/shard_map/ppermute | solution.py:623
  338.7 57.0 %collective-permute-start.23 = (bf16[256,1536]{1,0:T(8,128)(2,1)}, bf16[256,1536]{1,0:T(8,128)(2,1)}, u32[]{:S(2)}, u32[]{:S(2)}) collective-permute-start(bf16[256,1536]{1,0:T(8,128)(2,1)} %get-tuple-element.79), channel_id=1, source_target_pairs={{0,4},{4,0},{1,5},{5,1},{2,6},{6,2},{3,7},{7,3},{8,12},{12,8},{9,1... | collective-permute-start | bytes 2359304 | tf_op jit(solution)/shard_map/ppermute | solution.py:622
  340.7 55.0 %collective-permute-start.24 = (bf16[256,1536]{1,0:T(8,128)(2,1)}, bf16[256,1536]{1,0:T(8,128)(2,1)}, u32[]{:S(2)}, u32[]{:S(2)}) collective-permute-start(bf16[256,1536]{1,0:T(8,128)(2,1)} %get-tuple-element.78), channel_id=1, source_target_pairs={{0,6},{6,0},{2,4},{4,2},{1,7},{7,1},{3,5},{5,3},{8,14},{14,8},{10,... | collective-permute-start | bytes 2359304 | tf_op jit(solution)/shard_map/ppermute | solution.py:624
  353.5 39.3 %collective-permute-start.31 = (bf16[256,768]{1,0:T(8,128)(2,1)S(1)}, bf16[256,768]{1,0:T(8,128)(2,1)S(1)}, u32[]{:S(2)}, u32[]{:S(2)}) collective-permute-start(bf16[256,768]{1,0:T(8,128)(2,1)S(1)} %get-tuple-element.71), channel_id=1, source_target_pairs={{0,4},{4,0},{1,5},{5,1},{2,6},{6,2},{3,7},{7,3},{8,12},{12,8},{9,1... | collective-permute-start | bytes 1179656 | tf_op jit(solution)/shard_map/ppermute | solution.py:645
  354.8 38.7 %collective-permute-start.33 = (bf16[256,768]{1,0:T(8,128)(2,1)S(1)}, bf16[256,768]{1,0:T(8,128)(2,1)}, u32[]{:S(2)}, u32[]{:S(2)}) collective-permute-start(bf16[256,768]{1,0:T(8,128)(2,1)S(1)} %get-tuple-element.72), channel_id=1, source_target_pairs={{0,2},{2,0},{1,3},{3,1},{4,6},{6,4},{5,7},{7,5},{8,10},{10,8},{9,1... | collective-permute-start | bytes 1179656 | tf_op jit(solution)/shard_map/ppermute | solution.py:646
  357.2 42.5 %all-to-all-start.4 = ((bf16[8,48,384]{2,1,0:T(8,128)(2,1)}), bf16[8,48,384]{2,1,0:T(8,128)(2,1)S(1)}, u32[]{:S(2)}, u32[]{:S(2)}) async-start(bf16[8,48,384]{2,1,0:T(8,128)(2,1)} %bitcast.84), calls=%async_computation.5 | async-start | bytes 589824 | tf_op jit(solution)/shard_map/all_to_all | solution.py:723
  399.7 14.1 %all-to-all-start.5 = ((bf16[8,48,768]{2,1,0:T(8,128)(2,1)}), bf16[8,48,768]{2,1,0:T(8,128)(2,1)S(1)}, u32[]{:S(2)}, u32[]{:S(2)}) async-start(bf16[8,48,768]{2,1,0:T(8,128)(2,1)} %bitcast.271), calls=%async_computation.6 | async-start | bytes 1179648 | tf_op jit(solution)/shard_map/all_to_all | solution.py:723
  (27 other events, 64.8 us)
Sparse Core Ops, SparseCore 0:
  27.5 50.3 all-gather.3
  80.1 48.7 all-gather.5
  236.4 53.3 reduce-scatter.4
  317.9 47.2 reduce-scatter.6
